TPU v7x, 256 devices: a whole 4x4x8 slice. The times are simulated.
256 devices in a mesh: seq: 64 (over y, z, x_lo), head: 4 (over x_hi, core).
Axes of the slice: x: 4 (x_hi: 2, x_lo: 2; x = x_hi * 2 + x_lo), y: 4, z: 8, core: 2. Of those that a mesh axis runs over, the one named last changes fastest.
Arguments:
- inputs: bfloat16 [32768, 5376], P('seq'), may hold values from -6 to 6
- queries: bfloat16 [32768, 16, 128], P('seq', 'head'), may hold values from -24 to 24
- out_grad: bfloat16 [32768, 16, 128], P('seq', 'head'), may hold values from -6 to 6
- segment_ids: int32 [32768], P('seq'), may hold values from 0 to 63, never falling along the last dimension, each value on 1 to 2048 neighbouring positions
- k_weight: bfloat16 [5376, 1024], P('seq', 'head'), may hold values from -0.078125 to 0.078125
- v_weight: bfloat16 [5376, 1024], P('seq', 'head'), may hold values from -0.078125 to 0.078125
- k_gain: float32 [128], replicated, may hold values from 0.1 to 1.9
Outputs:
- inputs_grad: bfloat16 [32768, 5376], P('seq', 'head')
- query_grad: bfloat16 [32768, 16, 128], P('seq', 'head')
- k_weight_grad: float32 [5376, 1024], P('seq', 'head')
- v_weight_grad: float32 [5376, 1024], P('seq', 'head')
Inputs may be any that keep to these rules, and one draw needn't show every extreme that they name: `segment_ids`: tokens of one packed document share an id; ids never fall along the row; a document holds at most 2048 tokens.
All inputs are finite; a program needn't handle non-finite values.
Results may differ from a plain program's by a relative error of at most 0.01065.
The roundings to bfloat16 on the way count: a program that leaves them out, or rounds other values in their place, can miss the bound.
Values may be sent and summed in bfloat16 or wider, within the bound.
No kernel may reach another device: no remote copies, remote signals or barrier semaphores. Data moves between devices by JAX's collectives and lax.ppermute only.
A program may use at most 128 MiB of HBM per device.

v0:
```python
import jax
import jax.numpy as jnp
from jax import lax
from jax.experimental import pallas as pl
from jax.experimental.pallas import tpu as pltpu
from jax.sharding import Mesh, PartitionSpec as P

WIN = 1024
NY, NZ, NX = 4, 8, 2
F32, BF16 = jnp.float32, jnp.bfloat16

score_scale = 168.0 ** (-0.5)


def hop(block, axis, n, step):
    return lax.ppermute(block, axis, [(i, (i + step) % n) for i in range(n)])


def seq_shift(block, distance):
    count = NY * NZ * NX
    route = [(i, i + distance) for i in range(count) if 0 <= i + distance < count]
    return lax.ppermute(block, ("y", "z", "xl"), route)


def ring_gather(block, axis, n, put, buffer, split, between=None):
    me = lax.axis_index(axis)
    half = n // 2
    up = down = block
    steps = []
    for t in range(1, half):
        up, down = hop(up, axis, n, 1), hop(down, axis, n, -1)
        if between is not None:
            up, down = between(t, up, down)
        steps.append((up, down, t))
    top, bottom = hop(split(up, 0), axis, n, 1), hop(split(down, 1), axis, n, -1)
    buffer = put(buffer, block, me, None)
    for up, down, t in steps:
        buffer = put(buffer, up, lax.rem(me + n - t, n), None)
        buffer = put(buffer, down, lax.rem(me + t, n), None)
    far = lax.rem(me + half, n)
    return put(put(buffer, top, far, 0), bottom, far, 1)


def ring_reduce(own, axis, n, split, join, between=None):
    me = lax.axis_index(axis)
    half = n // 2
    far = own(lax.rem(me + half, n))
    up = hop(split(far, 0).astype(BF16), axis, n, 1)
    down = hop(split(far, 1).astype(BF16), axis, n, -1)
    up, down = up.astype(F32), down.astype(F32)
    for t in range(2, half + 1):
        ahead = own(lax.rem(me + half - t + 1, n))
        behind = own(lax.rem(me + n - half + t - 1, n))
        if t == 2:
            ahead = join(split(ahead, 0) + up, split(ahead, 1))
            behind = join(split(behind, 0), split(behind, 1) + down)
        else:
            ahead, behind = ahead + up, behind + down
        if between is not None:
            ahead, behind = between(t, ahead, behind)
        ahead, behind = ahead.astype(BF16), behind.astype(BF16)
        up, down = hop(ahead, axis, n, 1), hop(behind, axis, n, -1)
        up, down = up.astype(F32), down.astype(F32)
    return own(me) + up + down


def majors(block, part):
    h = block.shape[0] // 2
    return block[part * h : (part + 1) * h]


def take(array, index, axis):
    return lax.dynamic_index_in_dim(array, index, axis, keepdims=False)


def join_majors(a, b):
    return jnp.concatenate([a, b], 0)


SWAP = [(2 * h + i, 2 * h + 1 - i, h) for h in (0, 1) for i in (0, 1)]
NEAR = [(2 * h + i, 3 - 2 * h - i, h) for h in (0, 1) for i in (0, 1)]
FAR = [(2 * h + i, 2 - 2 * h + i, h) for h in (0, 1) for i in (0, 1)]


def y_route(block, route, back):
    pairs = [(a * NX + xl, b * NX + xl) for a, b, xl in route]
    return lax.ppermute(block, ("y", "xl"), [(b, a) for a, b in pairs] if back else pairs)


def y_place(xl):
    y = lax.axis_index("y")
    return y // 2 == xl, lax.rem(y, 2) == 0


def put_strip(buffer, block, index, part):
    start = (0 if part is None else part * (buffer.shape[0] // 2), index, 0, 0)
    return lax.dynamic_update_slice(buffer, block[:, None], start)


def gather_half(shard, xl):
    other = hop(shard, "xl", NX, 1)
    pair = jnp.where(xl == 0, join_majors(shard, other), join_majors(other, shard))
    rows, width = pair.shape
    holder, even = y_place(xl)
    swap, near, far = [y_route(pair, route, False) for route in (SWAP, NEAR, FAR)]
    one, two = jnp.where(holder, pair, far), jnp.where(holder, swap, near)
    near = jnp.stack([jnp.where(even, one, two), jnp.where(even, two, one)])
    full = jnp.zeros((NY // 2, NZ, rows, width), BF16)


    def rest(near, between):
        return ring_gather(near, "z", NZ, put_strip, full, majors, between).reshape(-1, width)

    return near, rest


def reduce_half(grad, xl, between):
    width = grad.shape[1]
    grad = grad.reshape(NY // 2, NZ, -1, width)
    over_z = ring_reduce(
        lambda i: take(grad, i, 1).astype(F32), "z", NZ, majors, join_majors, between
    )
    holder, even = y_place(xl)
    mine = jnp.where(even, over_z[0], over_z[1])
    other = jnp.where(even, over_z[1], over_z[0]).astype(BF16)
    over_y = jnp.where(holder, mine, 0.0)
    for block, route in ((other, SWAP), (other, NEAR), (mine.astype(BF16), FAR)):
        over_y = over_y + y_route(block, route, True).astype(F32)
    parts = over_y.reshape(NX, -1, width)
    away = hop(take(parts, 1 - xl, 0).astype(BF16), "xl", NX, 1)
    return take(parts, xl, 0) + away.astype(F32)


QB, KB = 256, 256
SEG_ROWS = 16
DOT_ROWS = (((1,), (1,)), ((), ()))
LOG2E = 1.4426950408889634


def attention_kernel(
    q_ref, do_ref, two_ref, one_ref, own_ref, qseg_ref,
    dq_ref, back_ref, mine_ref, kv, kseg_ref, s_buf, dp_buf, ds_buf, acc
):
    tok = q_ref.shape[0]
    hd = q_ref.shape[1] // 2
    span = WIN + QB
    step = pl.program_id(0)

    @pl.when(step == 0)
    def _():
        for i, ref in enumerate((two_ref, one_ref, own_ref)):
            kv[i * tok : (i + 1) * tok] = ref[:tok]
            ids = ref[tok:].astype(F32).T
            for j in range(tok // ids.shape[0]):
                low = i * tok + j * ids.shape[0]
                column = ids[:, j : j + 1]
                kseg_ref[low : low + ids.shape[0]] = jnp.broadcast_to(column, (ids.shape[0], 128))
        acc[...] = jnp.zeros_like(acc)

    base = pl.multiple_of(step * QB, QB)
    q_rows = pl.ds(base, QB)
    q = jnp.concatenate([q_ref[q_rows, :hd], q_ref[q_rows, hd:]], 0)
    do = jnp.concatenate([do_ref[q_rows, :hd], do_ref[q_rows, hd:]], 0)
    qseg = qseg_ref[step]
    r_minus_c = lax.broadcasted_iota(jnp.int32, (KB, QB), 1) - lax.broadcasted_iota(
        jnp.int32, (KB, QB), 0
    )
    chunks = span // KB

    def each(body, carry):
        for i in range(chunks):
            carry = body(i, carry)
        return carry

    def fold(x, op):
        return op(x.reshape(KB // 8, 8, 2 * QB), axis=0)

    def at(i):
        c = i * KB
        return c, pl.ds(c, KB), pl.ds(pl.multiple_of(base + c, 128), KB)

    def score(i, peak):
        c, here, rows = at(i)
        s = lax.dot_general(kv[rows, :hd], q, DOT_ROWS, preferred_element_type=F32)
        kseg = kseg_ref[rows, :]
        kseg = jnp.concatenate([kseg] * (QB // kseg.shape[1]), 1)
        ok = kseg == qseg
        if c < QB:
            ok = ok & (r_minus_c < c)
        if c + KB > WIN:
            ok = ok & (r_minus_c >= c - WIN)
        s = jnp.where(jnp.concatenate([ok, ok], 1), s * (score_scale * LOG2E), -1e30)
        s_buf[here] = s
        dp_buf[here] = lax.dot_general(kv[rows, hd:], do, DOT_ROWS, preferred_element_type=F32)
        return jnp.maximum(peak, fold(s, jnp.max))

    peak = each(score, jnp.full((8, 2 * QB), -1e30, F32))
    peak = jnp.max(peak, axis=0, keepdims=True)

    def power(i, denom):
        _, here, _ = at(i)
        p = jnp.exp2(s_buf[here] - peak)
        s_buf[here] = p
        return denom + fold(p, jnp.sum)

    denom = each(power, jnp.zeros((8, 2 * QB), F32))
    inverse = 1.0 / jnp.sum(denom, axis=0, keepdims=True)

    def value(i, delta):
        _, here, rows = at(i)
        p = s_buf[here] * inverse
        s_buf[here] = p
        low = p.astype(BF16)
        acc[rows, hd:] += jnp.dot(low, do, preferred_element_type=F32)
        return delta + fold(low.astype(F32) * dp_buf[here], jnp.sum)

    delta = each(value, jnp.zeros((8, 2 * QB), F32))
    delta = jnp.sum(delta, axis=0, keepdims=True)

    def key(i, none):
        _, here, rows = at(i)
        ds = (s_buf[here] * (dp_buf[here] - delta)).astype(BF16)
        ds_buf[here] = ds
        acc[rows, :hd] += jnp.dot(ds, q, preferred_element_type=F32)
        return none

    each(key, 0)
    k_turned = kv[pl.ds(base, span), :hd].T
    dq = jnp.dot(k_turned, ds_buf[...], preferred_element_type=F32) * score_scale
    dq = dq.T.astype(BF16)
    dq_ref[q_rows, :hd] = dq[:QB]
    dq_ref[q_rows, hd:] = dq[QB:]

    @pl.when(step == pl.num_programs(0) - 1)
    def _():
        back_ref[:, :hd] = (acc[: 2 * tok, :hd] * score_scale).astype(BF16)
        back_ref[:, hd:] = acc[: 2 * tok, hd:].astype(BF16)
        mine_ref[:, :hd] = acc[2 * tok :, :hd] * score_scale
        mine_ref[:, hd:] = acc[2 * tok :, hd:]


def attention(q, do, kv_two, kv_one, kv_own, qseg):
    tok, width = q.shape
    span = WIN + QB
    whole = pl.BlockSpec(memory_space=pltpu.VMEM)
    flops = 10 * (2 * tok) * span * (width // 2)
    return pl.pallas_call(
        attention_kernel,
        grid=(tok // QB,),
        in_specs=[whole] * 6,
        out_specs=[whole] * 3,
        out_shape=[
            jax.ShapeDtypeStruct((tok, width), BF16),
            jax.ShapeDtypeStruct((2 * tok, width), BF16),
            jax.ShapeDtypeStruct((tok, width), F32),
        ],
        scratch_shapes=[
            pltpu.VMEM((3 * tok, width), BF16),
            pltpu.VMEM((3 * tok, 128), F32),
            pltpu.VMEM((span, 2 * QB), F32),
            pltpu.VMEM((span, 2 * QB), F32),
            pltpu.VMEM((span, 2 * QB), BF16),
            pltpu.VMEM((3 * tok, width), F32),
        ],
        compiler_params=pltpu.CompilerParams(vmem_limit_bytes=24 << 20),
        cost_estimate=pl.CostEstimate(
            flops=flops, bytes_accessed=8 << 20, transcendentals=2 * tok * span
        ),
    )(q, do, kv_two, kv_one, kv_own, qseg)


def weight_grad_kernel(own_ref, par_ref, g_ref, h_ref, o_ref):
    total = jnp.dot(own_ref[...], g_ref[...], preferred_element_type=F32)
    total = total + jnp.dot(par_ref[...], h_ref[...], preferred_element_type=F32)
    o_ref[...] = total.astype(BF16)


def weight_grad(own_turned, par_turned, own_grads, par_grads):
    depth, tok = own_turned.shape
    width = own_grads.shape[1]
    block = depth // 8
    left = pl.BlockSpec((block, tok), lambda i: (i, 0))
    right = pl.BlockSpec((tok, width), lambda i: (0, 0))
    return pl.pallas_call(
        weight_grad_kernel,
        grid=(8,),
        in_specs=[left, left, right, right],
        out_specs=pl.BlockSpec((block, width), lambda i: (i, 0)),
        out_shape=jax.ShapeDtypeStruct((depth, width), BF16),
        compiler_params=pltpu.CompilerParams(vmem_limit_bytes=60 << 20),
        cost_estimate=pl.CostEstimate(
            flops=4 * depth * tok * width, bytes_accessed=12 << 20, transcendentals=0
        ),
    )(own_turned, par_turned, own_grads, par_grads)


def copy_kernel(where, x_ref, o_ref):
    o_ref[...] = x_ref[...]


def piece(inputs, where):
    tok, depth = inputs.shape
    rows, cols = tok // 4, depth // 2
    return pl.pallas_call(
        copy_kernel,
        grid_spec=pltpu.PrefetchScalarGridSpec(
            num_scalar_prefetch=1,
            grid=(2,),
            in_specs=[pl.BlockSpec((rows, cols), lambda i, w: (2 * w[0] + i, w[1]))],
            out_specs=pl.BlockSpec((rows, cols), lambda i, w: (i, 0)),
        ),
        out_shape=jax.ShapeDtypeStruct((2 * rows, cols), inputs.dtype),
        compiler_params=pltpu.CompilerParams(vmem_limit_bytes=60 << 20),
        cost_estimate=pl.CostEstimate(flops=0, bytes_accessed=3 << 20, transcendentals=0),
    )(where, inputs)


def turn_kernel(where, x_ref, o_ref):
    o_ref[...] = x_ref[...].T


def turned(inputs, where, depth):
    tok = inputs.shape[0]
    steps = 7
    cols = depth // steps
    return pl.pallas_call(
        turn_kernel,
        grid_spec=pltpu.PrefetchScalarGridSpec(
            num_scalar_prefetch=1,
            grid=(steps,),
            in_specs=[pl.BlockSpec((tok, cols), lambda i, w: (0, steps * w[0] + i))],
            out_specs=pl.BlockSpec((cols, tok), lambda i, w: (i, 0)),
        ),
        out_shape=jax.ShapeDtypeStruct((depth, tok), inputs.dtype),
        compiler_params=pltpu.CompilerParams(vmem_limit_bytes=60 << 20),
        cost_estimate=pl.CostEstimate(flops=0, bytes_accessed=6 << 20, transcendentals=0),
    )(where, inputs)


def project_kernel(where, x_ref, w_ref, *o_refs):
    step = pl.program_id(1)
    width = o_refs[0].shape[1]
    for g, o_ref in enumerate(o_refs):
        part = jnp.dot(
            x_ref[...], w_ref[:, g * width : (g + 1) * width], preferred_element_type=F32
        )

        @pl.when(step == 0)
        def _():
            o_ref[...] = part

        @pl.when(step > 0)
        def _():
            o_ref[...] += part


def project(inputs, where, weight, groups):
    tok = inputs.shape[0]
    depth, width = weight.shape
    steps = 3
    cols, rows = depth // steps, tok // 2
    out = jax.ShapeDtypeStruct((tok, width // groups), F32)
    return pl.pallas_call(
        project_kernel,
        grid_spec=pltpu.PrefetchScalarGridSpec(
            num_scalar_prefetch=1,
            grid=(2, steps),
            in_specs=[
                pl.BlockSpec((rows, cols), lambda j, i, w: (j, steps * w[0] + i)),
                pl.BlockSpec((cols, width), lambda j, i, w: (i, 0)),
            ],
            out_specs=[pl.BlockSpec((rows, width // groups), lambda j, i, w: (j, 0))] * groups,
        ),
        out_shape=[out] * groups,
        compiler_params=pltpu.CompilerParams(vmem_limit_bytes=16 << 20),
        cost_estimate=pl.CostEstimate(
            flops=2 * tok * depth * width, bytes_accessed=8 << 20, transcendentals=0
        ),
    )(where, inputs, weight)


def far_kernel(where, w_ref, g_ref, h_ref, o_ref):
    tok = g_ref.shape[0]
    for i, ref in enumerate((g_ref, h_ref)):
        part = lax.dot_general(w_ref[...], ref[...], DOT_ROWS, preferred_element_type=F32)
        o_ref[:, i * tok : (i + 1) * tok] = part.astype(BF16)


def near_kernel(where, w_ref, g_ref, h_ref, r_ref, own_ref, low_ref):
    tok = g_ref.shape[0]
    for i, ref in enumerate((g_ref, h_ref)):
        part = lax.dot_general(w_ref[...], ref[...], DOT_ROWS, preferred_element_type=F32)
        part = part + r_ref[:, i * tok : (i + 1) * tok].astype(F32)
        low_ref[:, i * tok : (i + 1) * tok] = part.astype(BF16)
        if i == 0:
            own_ref[...] = part


def input_term(where, weight, own_grads, par_grads, received=None):
    depth, width = weight.shape
    tok = own_grads.shape[0]
    steps = 4
    rows = depth // 2 // steps
    grads = pl.BlockSpec((tok, width), lambda i, w: (0, 0))
    both = pl.BlockSpec((rows, 2 * tok), lambda i, w: (i, 0))
    in_specs = [pl.BlockSpec((rows, width), lambda i, w: (steps * w[0] + i, 0)), grads, grads]
    low = jax.ShapeDtypeStruct((depth // 2, 2 * tok), BF16)
    if received is None:
        kernel, out_specs, out_shape, more = far_kernel, both, low, ()
    else:
        kernel, more = near_kernel, (received,)
        in_specs.append(both)
        out_specs = [pl.BlockSpec((rows, tok), lambda i, w: (i, 0)), both]
        out_shape = [jax.ShapeDtypeStruct((depth // 2, tok), F32), low]
    return pl.pallas_call(
        kernel,
        grid_spec=pltpu.PrefetchScalarGridSpec(
            num_scalar_prefetch=1, grid=(steps,), in_specs=in_specs, out_specs=out_specs
        ),
        out_shape=out_shape,
        compiler_params=pltpu.CompilerParams(vmem_limit_bytes=16 << 20),
        cost_estimate=pl.CostEstimate(
            flops=2 * tok * depth * width, bytes_accessed=6 << 20, transcendentals=0
        ),
    )(where, weight, own_grads, par_grads, *more)


def after(value, *others):
    return lax.optimization_barrier((value, *others))[0]


def per_device(inputs, queries, out_grad, segment_ids, k_weight, v_weight, k_gain):
    tok, depth = inputs.shape
    hd = queries.shape[2]
    heads = queries.shape[1]
    groups = k_weight.shape[1] // hd
    xl, xh, core = lax.axis_index("xl"), lax.axis_index("xh"), lax.axis_index("c")
    xl_array = jnp.full((1,), xl, jnp.int32)
    zero_array = jnp.zeros((1,), jnp.int32)

    def group(g):
        return slice(2 * g * hd, 2 * (g + 1) * hd)

    shard = jnp.concatenate(
        [w[:, g * hd : (g + 1) * hd] for g in range(groups) for w in (k_weight, v_weight)], 1
    )
    half = depth // 2
    some = hop(piece(inputs, jnp.stack([core, 1 - xl]).astype(jnp.int32)), "xl", NX, 1)
    near, gather_rest = gather_half(shard, xl)
    near, seg = lax.optimization_barrier((near, segment_ids))
    own_turned = turned(inputs, after(xl_array, near), half)
    held = {}

    def meanwhile(t, up, down):
        if t == 2:
            up, down, held["turned"] = lax.optimization_barrier((up, down, own_turned))
        return up, down

    weight = gather_rest(near, meanwhile)
    own_turned = held["turned"]
    rest = hop(some, "c", 2, 1)
    par_in = jnp.where(core == 0, join_majors(some, rest), join_majors(rest, some))

    ids = (seg + 1).astype(F32)
    query_seg = ids.reshape(tok // QB, 1, QB)
    key_seg = jnp.zeros((SEG_ROWS, 2 * hd), BF16)
    key_seg = key_seg.at[: tok // (2 * hd)].set(ids.astype(BF16).reshape(-1, 2 * hd))
    q_flat = after(queries, near).reshape(tok, heads * hd)
    do_flat = after(out_grad, near).reshape(tok, heads * hd)

    par_raw = project(par_in, zero_array, weight, groups)
    from_par = [hop(par_raw[0], "xl", NX, 1)]
    from_par.append(hop(after(par_raw[1], from_par[0]), "xl", NX, 1))
    own_raw = project(inputs, after(xl_array, *par_raw), weight, groups)
    par_turned = turned(par_in, after(zero_array, *own_raw), half)
    from_par[0], par_turned = lax.optimization_barrier((from_par[0], par_turned))

    def forward(own_raw, from_par, gain):
        raw = own_raw + from_par
        k_raw = raw[:, :hd]
        k_inv = lax.rsqrt(jnp.mean(k_raw * k_raw, axis=-1, keepdims=True) + 1e-06)
        k_normed = k_raw * k_inv
        own = jnp.concatenate([k_normed * gain, raw[:, hd:]], 1).astype(BF16)
        return join_majors(own, key_seg), k_normed, k_inv

    def attend(own, g):
        one, two = seq_shift(own, 1), seq_shift(own, 2)
        dq, back, mine = attention(
            q_flat[:, group(g)], do_flat[:, group(g)], two, one, own, query_seg
        )
        one, two = seq_shift(back[tok:], -1), seq_shift(back[:tok], -2)
        return dq, mine, one, two

    def backward(k_normed, k_inv, mine, one, two, gain):
        grads = mine + one.astype(F32) + two.astype(F32)
        normed_grad = grads[:, :hd] * gain
        raw_grad = (
            normed_grad - k_normed * jnp.mean(normed_grad * k_normed, axis=-1, keepdims=True)
        ) * k_inv
        return jnp.concatenate([raw_grad, grads[:, hd:]], 1).astype(BF16)

    state = [forward(own_raw[0], from_par[0], k_gain)]
    for g in range(1, groups):
        arrived, gain = after(from_par[g], state[-1][0]), after(k_gain, state[-1][0])
        state.append(forward(own_raw[g], arrived, gain))
    sent = [attend(state[g][0], g) for g in range(groups)]
    dqs = [t[0] for t in sent]
    lows = []
    for g in range(groups):
        mine, one, two = sent[g][1:]
        if lows:
            mine = after(mine, lows[-1])
        gain = after(k_gain, mine)
        lows.append(backward(*state[g][1:], mine, one, two, gain))
    pars = [hop(low, "xl", NX, 1) for low in lows]
    own_grads, par_grads = jnp.concatenate(lows, 1), jnp.concatenate(pars, 1)

    keep = xh == xl
    core_array = jnp.full((1,), core, jnp.int32)
    far = input_term(1 - core_array, weight, own_grads, par_grads)
    received = hop(far, "c", 2, 1)

    def between(t, ahead, behind):
        if t == 2:
            own_part, low = input_term(core_array, weight, own_grads, par_grads, received)
            first = jnp.where(keep, low[:, tok:], low[:, :tok])
            held["own"] = own_part
            ahead, behind, held["first"], held["second"] = lax.optimization_barrier(
                (ahead, behind, first, low[:, tok:])
            )
        return ahead, behind

    par_later = after(par_grads, far)
    grad = weight_grad(own_turned, par_turned, own_grads, par_later)
    grad = reduce_half(grad, xl, between)
    cols = [grad[:, i * hd : (i + 1) * hd] for i in range(2 * groups)]
    k_weight_grad = jnp.concatenate(cols[0::2], 1)
    v_weight_grad = jnp.concatenate(cols[1::2], 1)
    query_grad = jnp.concatenate(dqs, 1).reshape(tok, heads, hd)

    first = lax.ppermute(held["first"], ("xl", "xh"), [(0, 2), (3, 1), (1, 0), (2, 3)])
    second = lax.ppermute(held["second"], ("xl", "xh"), [(1, 2), (2, 1)])
    inputs_grad = jnp.where(keep, held["own"], second.astype(F32)) + first.astype(F32)
    return inputs_grad.astype(BF16).T, query_grad, k_weight_grad, v_weight_grad


def solution(mesh):
    fine = Mesh(mesh.devices.reshape(NY, NZ, NX, 2, 2), ("y", "z", "xl", "xh", "c"))
    seq, head = ("y", "z", "xl"), ("xh", "c")
    in_specs = (
        P(seq, None),
        P(seq, head, None),
        P(seq, head, None),
        P(seq),
        P(seq, head),
        P(seq, head),
        P(),
    )
    out_specs = (P(seq, head), P(seq, head, None), P(seq, head), P(seq, head))

    return jax.shard_map(
        per_device, mesh=fine, in_specs=in_specs, out_specs=out_specs, check_vma=False
    )
```

profile of v0, /device:TPU:1, one launch (start us, length us, event | category | flops | bytes accessed | tf_op | source)
XLA Modules:
  0.0 251.1 jit_solution(3257838276944862953)
XLA Ops:
  1.4 2.1 collective-permute-start
  4.1 2.9 %shard_map.103 = bf16[256,2688]{1,0:T(8,128)(2,1)} custom-call(s32[2]{0:T(128)} %pad_add_fusion.where, bf16[512,5376]{1,0:T(8,128)(2,1)} %x_ref.5), custom_call_target="tpu_custom_call" | custom-call | bytes 3145728 | tf_op jit(solution)/shard_map/pallas_call | solution.py:304
  7.1 4.9 %collective-permute-start.3 = (bf16[168,512]{1,0:T(8,128)(2,1)S(1)}, bf16[168,512]{1,0:T(8,128)(2,1)S(1)}, u32[]{:S(2)}, u32[]{:S(2)}) collective-permute-start(bf16[168,512]{1,0:T(8,128)(2,1)S(1)} %maximum_select_fusion.1), channel_id=1, source_target_pairs={{0,192},{64,128},{132,68},{196,4},{1,193},{65,129},{133,69},{197,5... | collective-permute-start | bytes 516104 | tf_op jit(solution)/shard_map/ppermute | solution.py:87
  12.0 1.9 collective-permute-start.2
  14.0 1.3 collective-permute-start.1
  15.3 3.3 %collective-permute-done.2 = bf16[168,512]{1,0:T(8,128)(2,1)S(1)} collective-permute-done((bf16[168,512]{1,0:T(8,128)(2,1)S(1)}, bf16[168,512]{1,0:T(8,128)(2,1)S(1)}, u32[]{:S(2)}, u32[]{:S(2)}) %collective-permute-start.2) | collective-permute-done | bytes 172064 | tf_op jit(solution)/shard_map/ppermute | solution.py:87
  18.6 1.4 collective-permute-done.1
  20.1 5.7 %collective-permute-start.5 = (bf16[2,168,512]{2,1,0:T(8,128)(2,1)S(1)}, bf16[2,168,512]{2,1,0:T(8,128)(2,1)S(1)}, u32[]{:S(2)}, u32[]{:S(2)}) collective-permute-start(bf16[2,168,512]{2,1,0:T(8,128)(2,1)S(1)} %pad_maximum_fusion.4), channel_id=1, source_target_pairs={{0,56},{8,0},{16,8},{24,16},{32,24},{40,32},{48,40},{56,48},{1,57}... | collective-permute-start | bytes 1032200 | tf_op jit(solution)/shard_map/ppermute | solution.py:16
  25.7 6.0 %shard_map.102.own_ref = bf16[2688,512]{1,0:T(8,128)(2,1)} custom-call(s32[1]{0:T(128)} %bitcast.9.where, bf16[512,5376]{1,0:T(8,128)(2,1)} %x_ref.5), custom_call_target="tpu_custom_call" | custom-call | bytes 6291456 | tf_op jit(solution)/shard_map/pallas_call | solution.py:326
  32.0 2.7 %collective-permute-start.7 = (bf16[2,168,512]{2,1,0:T(8,128)(2,1)S(1)}, bf16[2,168,512]{2,1,0:T(8,128)(2,1)S(1)}, u32[]{:S(2)}, u32[]{:S(2)}) collective-permute-start(bf16[2,168,512]{2,1,0:T(8,128)(2,1)S(1)} %collective-permute-done.5), channel_id=1, source_target_pairs={{0,56},{8,0},{16,8},{24,16},{32,24},{40,32},{48,40},{56,48},{1,57}... | collective-permute-start | bytes 1032200 | tf_op jit(solution)/shard_map/ppermute | solution.py:16
  35.9 3.1 %collective-permute-done.7 = bf16[2,168,512]{2,1,0:T(8,128)(2,1)S(1)} collective-permute-done((bf16[2,168,512]{2,1,0:T(8,128)(2,1)S(1)}, bf16[2,168,512]{2,1,0:T(8,128)(2,1)S(1)}, u32[]{:S(2)}, u32[]{:S(2)}) %collective-permute-start.7) | collective-permute-done | bytes 344096 | tf_op jit(solution)/shard_map/ppermute | solution.py:16
  39.0 3.3 %collective-permute-done.6 = bf16[2,168,512]{2,1,0:T(8,128)(2,1)S(1)} collective-permute-done((bf16[2,168,512]{2,1,0:T(8,128)(2,1)}, bf16[2,168,512]{2,1,0:T(8,128)(2,1)S(1)}, u32[]{:S(2)}, u32[]{:S(2)}) %collective-permute-start.6) | collective-permute-done | bytes 344096 | tf_op jit(solution)/shard_map/ppermute | solution.py:16
  42.3 2.7 %collective-permute-start.9 = (bf16[2,168,512]{2,1,0:T(8,128)(2,1)S(1)}, bf16[2,168,512]{2,1,0:T(8,128)(2,1)S(1)}, u32[]{:S(2)}, u32[]{:S(2)}) collective-permute-start(bf16[2,168,512]{2,1,0:T(8,128)(2,1)S(1)} %collective-permute-done.7), channel_id=1, source_target_pairs={{0,56},{8,0},{16,8},{24,16},{32,24},{40,32},{48,40},{56,48},{1,57}... | collective-permute-start | bytes 1032200 | tf_op jit(solution)/shard_map/ppermute | solution.py:16
  45.0 5.4 %collective-permute-start.13 = (bf16[256,2688]{1,0:T(8,128)(2,1)}, bf16[256,2688]{1,0:T(8,128)(2,1)S(1)}, u32[]{:S(2)}, u32[]{:S(2)}) collective-permute-start(bf16[256,2688]{1,0:T(8,128)(2,1)} %collective-permute-done.12), channel_id=1, source_target_pairs={{0,1},{1,0},{2,3},{3,2},{4,5},{5,4},{6,7},{7,6},{8,9},{9,8},{10,11... | collective-permute-start | bytes 4128776 | tf_op jit(solution)/shard_map/ppermute | solution.py:16
  50.6 2.7 %collective-permute-start.11 = (bf16[1,168,512]{2,1,0:T(8,128)(2,1)S(1)}, bf16[1,168,512]{2,1,0:T(8,128)(2,1)S(1)}, u32[]{:S(2)}, u32[]{:S(2)}) collective-permute-start(bf16[1,168,512]{2,1,0:T(8,128)(2,1)S(1)} %slice.188), channel_id=1, source_target_pairs={{0,56},{8,0},{16,8},{24,16},{32,24},{40,32},{48,40},{56,48},{1,57}... | collective-permute-start | bytes 516104 | tf_op jit(solution)/shard_map/ppermute | solution.py:16
  53.4 3.3 %collective-permute-done.10 = bf16[1,168,512]{2,1,0:T(8,128)(2,1)S(1)} collective-permute-done((bf16[1,168,512]{2,1,0:T(8,128)(2,1)S(1)}, bf16[1,168,512]{2,1,0:T(8,128)(2,1)S(1)}, u32[]{:S(2)}, u32[]{:S(2)}) %collective-permute-start.10) | collective-permute-done | bytes 172064 | tf_op jit(solution)/shard_map/ppermute | solution.py:16
  56.8 2.5 maximum_select_fusion.x_ref
  59.3 6.3 %shard_map.104 = (f32[512,256]{1,0:T(8,128)}, f32[512,256]{1,0:T(8,128)S(1)}) custom-call(s32[1]{0:T(128)} %constant.161.clone.1.where, bf16[512,2688]{1,0:T(8,128)(2,1)S(1)} %maximum_select_fusion.x_ref, bf16[2688,512]{1,0:T(8,128)(2,1)S(1)} %bitcast.103), custom_call_target="tpu_custom_call" | custom-call | flops 1409286144 | bytes 8388608 | tf_op jit(solution)/shard_map/pallas_call | solution.py:363
  66.4 2.8 %collective-permute-start.14 = (f32[512,256]{1,0:T(8,128)}, f32[512,256]{1,0:T(8,128)}, u32[]{:S(2)}, u32[]{:S(2)}) collective-permute-start(f32[512,256]{1,0:T(8,128)} %get-tuple-element.57), channel_id=1, source_target_pairs={{0,4},{4,0},{1,5},{5,1},{2,6},{6,2},{3,7},{7,3},{8,12},{12,8},{9,1... | collective-permute-start | bytes 1572872 | tf_op jit(solution)/shard_map/ppermute | solution.py:16
  70.2 2.6 %copy-done = bf16[512,5376]{1,0:T(8,128)(2,1)S(1)} copy-done((bf16[512,5376]{1,0:T(8,128)(2,1)S(1)}, bf16[512,5376]{1,0:T(8,128)(2,1)}, u32[]{:S(2)}) %copy-start) | copy-done | bytes 5505048
  72.7 5.6 %shard_map.105 = (f32[512,256]{1,0:T(8,128)S(1)}, f32[512,256]{1,0:T(8,128)S(1)}) custom-call(s32[1]{0:T(128)} %bitcast.9.where, bf16[512,5376]{1,0:T(8,128)(2,1)S(1)} %copy-done, bf16[2688,512]{1,0:T(8,128)(2,1)S(1)} %bitcast.104), custom_call_target="tpu_custom_call" | custom-call | flops 1409286144 | bytes 8388608 | tf_op jit(solution)/shard_map/pallas_call | solution.py:363
  78.3 6.0 %shard_map.106.par_ref = bf16[2688,512]{1,0:T(8,128)(2,1)} custom-call(s32[1]{0:T(128)} %constant.161.clone.1.where, bf16[512,2688]{1,0:T(8,128)(2,1)} %copy-done.1), custom_call_target="tpu_custom_call" | custom-call | bytes 6291456 | tf_op jit(solution)/shard_map/pallas_call | solution.py:326
  86.0 1.9 collective-permute-start.16
  87.9 1.3 collective-permute-start.15
  91.3 1.3 collective-permute-done.15.two_ref
  92.6 6.7 %shard_map.107 = (bf16[512,256]{1,0:T(8,128)(2,1)S(1)}, bf16[1024,256]{1,0:T(8,128)(2,1)S(1)}, f32[512,256]{1,0:T(8,128)S(1)}) custom-call(bf16[512,256]{1,0:T(8,128)(2,1)S(1)} %get-tuple-element.106.q_ref, bf16[512,256]{1,0:T(8,128)(2,1)S(1)} %get-tuple-element.104.do_ref, bf16[528,256]{1,0:T(8,128)(2,1)S(1)} %collective-permute-done.15.two_ref, ...), custom_call_target="tpu_custom_call" | custom-call | flops 1677721600 | bytes 8388608 | tf_op jit(solution)/shard_map/pallas_call | solution.py:247
  99.3 1.3 collective-permute-start.17
  100.6 1.3 collective-permute-start.18
  101.9 3.3 %collective-permute-done.19 = f32[512,256]{1,0:T(8,128)S(1)} collective-permute-done((f32[512,256]{1,0:T(8,128)S(1)}, f32[512,256]{1,0:T(8,128)S(1)}, u32[]{:S(2)}, u32[]{:S(2)}) %collective-permute-start.19) | collective-permute-done | bytes 524320 | tf_op jit(solution)/shard_map/ppermute | solution.py:16
  105.7 1.3 collective-permute-start.21
  107.0 4.8 %collective-permute-start.20 = (bf16[528,256]{1,0:T(8,128)(2,1)S(1)}, bf16[528,256]{1,0:T(8,128)(2,1)S(1)}, u32[]{:S(2)}, u32[]{:S(2)}) collective-permute-start(bf16[528,256]{1,0:T(8,128)(2,1)S(1)} %fusion.12.own_ref), channel_id=1, source_target_pairs={{0,8},{4,12},{8,16},{12,20},{16,24},{20,28},{24,32},{28,36},{32,40... | collective-permute-start | bytes 811016 | tf_op jit(solution)/shard_map/ppermute | solution.py:22
  112.2 3.0 %collective-permute-done.20.two_ref = bf16[528,256]{1,0:T(8,128)(2,1)S(1)} collective-permute-done((bf16[528,256]{1,0:T(8,128)(2,1)S(1)}, bf16[528,256]{1,0:T(8,128)(2,1)S(1)}, u32[]{:S(2)}, u32[]{:S(2)}) %collective-permute-start.20) | collective-permute-done | bytes 270368 | tf_op jit(solution)/shard_map/ppermute | solution.py:22
  115.2 6.7 %shard_map.108 = (bf16[512,256]{1,0:T(8,128)(2,1)S(1)}, bf16[1024,256]{1,0:T(8,128)(2,1)S(1)}, f32[512,256]{1,0:T(8,128)S(1)}) custom-call(bf16[512,256]{1,0:T(8,128)(2,1)S(1)} %get-tuple-element.107.q_ref, bf16[512,256]{1,0:T(8,128)(2,1)S(1)} %get-tuple-element.105.do_ref, bf16[528,256]{1,0:T(8,128)(2,1)S(1)} %collective-permute-done.20.two_ref, ...), custom_call_target="tpu_custom_call" | custom-call | flops 1677721600 | bytes 8388608 | tf_op jit(solution)/shard_map/pallas_call | solution.py:247
  121.9 1.3 collective-permute-start.22
  123.2 1.3 collective-permute-start.23
  124.8 3.1 %collective-permute-start.24 = (bf16[512,256]{1,0:T(8,128)(2,1)S(1)}, bf16[512,256]{1,0:T(8,128)(2,1)S(1)}, u32[]{:S(2)}, u32[]{:S(2)}) collective-permute-start(bf16[512,256]{1,0:T(8,128)(2,1)S(1)} %pad_maximum_fusion.5), channel_id=1, source_target_pairs={{0,4},{4,0},{1,5},{5,1},{2,6},{6,2},{3,7},{7,3},{8,12},{12,8},{9,1... | collective-permute-start | bytes 786440 | tf_op jit(solution)/shard_map/ppermute | solution.py:16
  127.8 5.0 %collective-permute-done.22 = bf16[512,256]{1,0:T(8,128)(2,1)S(1)} collective-permute-done((bf16[512,256]{1,0:T(8,128)(2,1)S(1)}, bf16[512,256]{1,0:T(8,128)(2,1)S(1)}, u32[]{:S(2)}, u32[]{:S(2)}) %collective-permute-start.22) | collective-permute-done | bytes 262176 | tf_op jit(solution)/shard_map/ppermute | solution.py:22
  135.7 7.2 %collective-permute-done.25 = bf16[512,256]{1,0:T(8,128)(2,1)S(1)} collective-permute-done((bf16[512,256]{1,0:T(8,128)(2,1)S(1)}, bf16[512,256]{1,0:T(8,128)(2,1)S(1)}, u32[]{:S(2)}, u32[]{:S(2)}) %collective-permute-start.25) | collective-permute-done | bytes 262176 | tf_op jit(solution)/shard_map/ppermute | solution.py:16
  143.0 3.4 %shard_map.109 = bf16[1344,1024]{1,0:T(8,128)(2,1)} custom-call(s32[1]{0:T(128)S(6)} %sub.43.where, bf16[2688,512]{1,0:T(8,128)(2,1)S(1)} %bitcast.105, bf16[512,512]{1,0:T(8,128)(2,1)S(1)} %pad_maximum_fusion.2.g_ref, bf16[512,512]{1,0:T(8,128)(2,1)S(1)} %constant_dynamic-update-slice_fusion.h_ref), custom_call_target="tpu_custom_call" | custom-call | flops 1409286144 | bytes 6291456 | tf_op jit(solution)/shard_map/pallas_call | solution.py:415
  146.4 7.9 %collective-permute-start.26 = (bf16[1344,1024]{1,0:T(8,128)(2,1)}, bf16[1344,1024]{1,0:T(8,128)(2,1)}, u32[]{:S(2)}, u32[]{:S(2)}) collective-permute-start(bf16[1344,1024]{1,0:T(8,128)(2,1)} %shard_map.109), channel_id=1, source_target_pairs={{0,1},{1,0},{2,3},{3,2},{4,5},{5,4},{6,7},{7,6},{8,9},{9,8},{10,11... | collective-permute-start | bytes 8257544 | tf_op jit(solution)/shard_map/ppermute | solution.py:16
  154.3 8.7 %shard_map.111 = bf16[2688,512]{1,0:T(8,128)(2,1)} custom-call(bf16[2688,512]{1,0:T(8,128)(2,1)} %shard_map.102.own_ref, bf16[2688,512]{1,0:T(8,128)(2,1)} %shard_map.106.par_ref, bf16[512,512]{1,0:T(8,128)(2,1)} %copy-done.2, bf16[512,512]{1,0:T(8,128)(2,1)} %copy-done.4), custom_call_target="tpu_custom_call" | custom-call | flops 2818572288 | bytes 12582912 | tf_op jit(solution)/shard_map/pallas_call | solution.py:284
  164.0 11.6 %collective-permute-start.28 = (bf16[1,168,512]{2,1,0:T(8,128)(2,1)S(1)}, bf16[1,168,512]{2,1,0:T(8,128)(2,1)S(1)}, u32[]{:S(2)}, u32[]{:S(2)}) collective-permute-start(bf16[1,168,512]{2,1,0:T(8,128)(2,1)S(1)} %get-tuple-element.92), channel_id=1, source_target_pairs={{0,56},{8,0},{16,8},{24,16},{32,24},{40,32},{48,40},{56,48},{1,57}... | collective-permute-start | bytes 516104 | tf_op jit(solution)/shard_map/ppermute | solution.py:16
  175.6 1.3 dynamic-slice_convert_fusion
  177.0 2.3 collective-permute-done.28
  179.4 3.1 %collective-permute-done.27 = bf16[1,168,512]{2,1,0:T(8,128)(2,1)S(1)} collective-permute-done((bf16[1,168,512]{2,1,0:T(8,128)(2,1)S(1)}, bf16[1,168,512]{2,1,0:T(8,128)(2,1)S(1)}, u32[]{:S(2)}, u32[]{:S(2)}) %collective-permute-start.27) | collective-permute-done | bytes 172064 | tf_op jit(solution)/shard_map/ppermute | solution.py:16
  182.6 4.0 %shard_map.110 = (f32[1344,512]{1,0:T(8,128)S(1)}, bf16[1344,1024]{1,0:T(8,128)(2,1)S(1)}) custom-call(s32[1]{0:T(128)} %bitcast.where, bf16[2688,512]{1,0:T(8,128)(2,1)S(1)} %bitcast.106, bf16[512,512]{1,0:T(8,128)(2,1)S(1)} %copy-done.3, bf16[512,512]{1,0:T(8,128)(2,1)S(1)} %copy-done.5, bf16[1344,1024]{1,0:T(8,128)(2,1)} %collective-permute-done.26.r_ref), custom_call_target="tpu_custom_call" | custom-call | flops 1409286144 | bytes 6291456 | tf_op jit(solution)/shard_map/pallas_call | solution.py:415
  186.6 1.5 copy-done.6
  188.1 1.7 fusion.16
  189.8 2.7 %collective-permute-start.34 = (bf16[2,168,512]{2,1,0:T(8,128)(2,1)S(1)}, bf16[2,168,512]{2,1,0:T(8,128)(2,1)S(1)}, u32[]{:S(2)}, u32[]{:S(2)}) collective-permute-start(bf16[2,168,512]{2,1,0:T(8,128)(2,1)S(1)} %pad_maximum_fusion.1), channel_id=1, source_target_pairs={{0,56},{8,0},{16,8},{24,16},{32,24},{40,32},{48,40},{56,48},{1,57}... | collective-permute-start | bytes 1032200 | tf_op jit(solution)/shard_map/ppermute | solution.py:16
  192.5 7.0 %collective-permute-done.31 = bf16[2,168,512]{2,1,0:T(8,128)(2,1)S(1)} collective-permute-done((bf16[2,168,512]{2,1,0:T(8,128)(2,1)S(1)}, bf16[2,168,512]{2,1,0:T(8,128)(2,1)S(1)}, u32[]{:S(2)}, u32[]{:S(2)}) %collective-permute-start.31) | collective-permute-done | bytes 344096 | tf_op jit(solution)/shard_map/ppermute | solution.py:16
  199.7 2.7 %collective-permute-start.35 = (bf16[2,168,512]{2,1,0:T(8,128)(2,1)S(1)}, bf16[2,168,512]{2,1,0:T(8,128)(2,1)S(1)}, u32[]{:S(2)}, u32[]{:S(2)}) collective-permute-start(bf16[2,168,512]{2,1,0:T(8,128)(2,1)S(1)} %get-tuple-element.89), channel_id=1, source_target_pairs={{0,56},{8,0},{16,8},{24,16},{32,24},{40,32},{48,40},{56,48},{1,57}... | collective-permute-start | bytes 1032200 | tf_op jit(solution)/shard_map/ppermute | solution.py:16
  202.4 6.1 %collective-permute-done.32 = bf16[2,168,512]{2,1,0:T(8,128)(2,1)S(1)} collective-permute-done((bf16[2,168,512]{2,1,0:T(8,128)(2,1)S(1)}, bf16[2,168,512]{2,1,0:T(8,128)(2,1)S(1)}, u32[]{:S(2)}, u32[]{:S(2)}) %collective-permute-start.32) | collective-permute-done | bytes 344096 | tf_op jit(solution)/shard_map/ppermute | solution.py:16
  208.8 2.7 %collective-permute-start.36 = (bf16[2,168,512]{2,1,0:T(8,128)(2,1)S(1)}, bf16[2,168,512]{2,1,0:T(8,128)(2,1)S(1)}, u32[]{:S(2)}, u32[]{:S(2)}) collective-permute-start(bf16[2,168,512]{2,1,0:T(8,128)(2,1)S(1)} %get-tuple-element.87), channel_id=1, source_target_pairs={{0,56},{8,0},{16,8},{24,16},{32,24},{40,32},{48,40},{56,48},{1,57}... | collective-permute-start | bytes 1032200 | tf_op jit(solution)/shard_map/ppermute | solution.py:16
  211.5 1.7 collective-permute-start.29
  213.2 2.4 collective-permute-start.30
  217.8 1.8 fusion.13
  222.2 2.0 collective-permute-start.37
  224.2 3.7 %collective-permute-done.39 = bf16[168,512]{1,0:T(8,128)(2,1)} collective-permute-done((bf16[168,512]{1,0:T(8,128)(2,1)}, bf16[168,512]{1,0:T(8,128)(2,1)}, u32[]{:S(2)}, u32[]{:S(2)}) %collective-permute-start.39) | collective-permute-done | bytes 172064 | tf_op jit(solution)/shard_map/ppermute | solution.py:87
  227.9 1.8 collective-permute-done.38
  229.7 2.2 fusion.10
  231.9 1.8 reshape.124
  235.6 2.0 reshape.123
  237.6 7.8 %collective-permute-done.40 = bf16[84,512]{1,0:T(8,128)(2,1)S(1)} collective-permute-done((bf16[84,512]{1,0:T(8,128)(2,1)S(1)}, bf16[84,512]{1,0:T(8,128)(2,1)S(1)}, u32[]{:S(2)}, u32[]{:S(2)}) %collective-permute-start.40) | collective-permute-done | bytes 86048 | tf_op jit(solution)/shard_map/ppermute | solution.py:16
  247.7 3.4 %fusion = bf16[512,1344]{0,1:T(8,128)(2,1)} fusion(bf16[1344,512]{1,0:T(8,128)(2,1)} %collective-permute-done.30, f32[1344,512]{1,0:T(8,128)S(1)} %copy-done.7, bf16[1344,512]{1,0:T(8,128)(2,1)} %collective-permute-done.29, pred[]{:T(512)S(6)} %eq.17), kind=kLoop, calls=%fused_computation.2 | loop fusion | flops 3440640 | bytes 6881281 | tf_op jit(solution)/shard_map/transpose | solution.py:544
  (141 shorter events, 23.1 us)
Async XLA Ops:
  1.4 5.6 %collective-permute-start = (bf16[84,512]{1,0:T(8,128)(2,1)S(1)}, bf16[84,512]{1,0:T(8,128)(2,1)S(1)}, u32[]{:S(2)}, u32[]{:S(2)}) collective-permute-start(bf16[84,512]{1,0:T(8,128)(2,1)S(1)} %pad_maximum_fusion.7), channel_id=1, source_target_pairs={{0,4},{4,0},{1,5},{5,1},{2,6},{6,2},{3,7},{7,3},{8,12},{12,8},{9,1... | collective-permute-start | bytes 258056 | tf_op jit(solution)/shard_map/ppermute | solution.py:16
  7.0 37.9 %collective-permute-start.12 = (bf16[256,2688]{1,0:T(8,128)(2,1)}, bf16[256,2688]{1,0:T(8,128)(2,1)}, u32[]{:S(2)}, u32[]{:S(2)}) collective-permute-start(bf16[256,2688]{1,0:T(8,128)(2,1)} %shard_map.103), channel_id=1, source_target_pairs={{0,4},{4,0},{1,5},{5,1},{2,6},{6,2},{3,7},{7,3},{8,12},{12,8},{9,1... | collective-permute-start | bytes 4128776 | tf_op jit(solution)/shard_map/ppermute | solution.py:16
  7.1 8.1 %collective-permute-start.3 = (bf16[168,512]{1,0:T(8,128)(2,1)S(1)}, bf16[168,512]{1,0:T(8,128)(2,1)S(1)}, u32[]{:S(2)}, u32[]{:S(2)}) collective-permute-start(bf16[168,512]{1,0:T(8,128)(2,1)S(1)} %maximum_select_fusion.1), channel_id=1, source_target_pairs={{0,192},{64,128},{132,68},{196,4},{1,193},{65,129},{133,69},{197,5... | collective-permute-start | bytes 516104 | tf_op jit(solution)/shard_map/ppermute | solution.py:87
  12.0 6.6 %collective-permute-start.2 = (bf16[168,512]{1,0:T(8,128)(2,1)S(1)}, bf16[168,512]{1,0:T(8,128)(2,1)S(1)}, u32[]{:S(2)}, u32[]{:S(2)}) collective-permute-start(bf16[168,512]{1,0:T(8,128)(2,1)S(1)} %maximum_select_fusion.1), channel_id=1, source_target_pairs={{0,64},{64,0},{132,196},{196,132},{1,65},{65,1},{133,197},{197,133... | collective-permute-start | bytes 516104 | tf_op jit(solution)/shard_map/ppermute | solution.py:87
  14.0 6.0 %collective-permute-start.1 = (bf16[168,512]{1,0:T(8,128)(2,1)S(1)}, bf16[168,512]{1,0:T(8,128)(2,1)S(1)}, u32[]{:S(2)}, u32[]{:S(2)}) collective-permute-start(bf16[168,512]{1,0:T(8,128)(2,1)S(1)} %maximum_select_fusion.1), channel_id=1, source_target_pairs={{0,128},{64,192},{132,4},{196,68},{1,129},{65,193},{133,5},{197,69... | collective-permute-start | bytes 516104 | tf_op jit(solution)/shard_map/ppermute | solution.py:87
  20.1 11.9 %collective-permute-start.5 = (bf16[2,168,512]{2,1,0:T(8,128)(2,1)S(1)}, bf16[2,168,512]{2,1,0:T(8,128)(2,1)S(1)}, u32[]{:S(2)}, u32[]{:S(2)}) collective-permute-start(bf16[2,168,512]{2,1,0:T(8,128)(2,1)S(1)} %pad_maximum_fusion.4), channel_id=1, source_target_pairs={{0,56},{8,0},{16,8},{24,16},{32,24},{40,32},{48,40},{56,48},{1,57}... | collective-permute-start | bytes 1032200 | tf_op jit(solution)/shard_map/ppermute | solution.py:16
  25.7 9.0 %collective-permute-start.4 = (bf16[2,168,512]{2,1,0:T(8,128)(2,1)S(1)}, bf16[2,168,512]{2,1,0:T(8,128)(2,1)}, u32[]{:S(2)}, u32[]{:S(2)}) collective-permute-start(bf16[2,168,512]{2,1,0:T(8,128)(2,1)S(1)} %pad_maximum_fusion.4), channel_id=1, source_target_pairs={{0,8},{8,16},{16,24},{24,32},{32,40},{40,48},{48,56},{56,0},{1,9},... | collective-permute-start | bytes 1032200 | tf_op jit(solution)/shard_map/ppermute | solution.py:16
  32.0 7.0 %collective-permute-start.7 = (bf16[2,168,512]{2,1,0:T(8,128)(2,1)S(1)}, bf16[2,168,512]{2,1,0:T(8,128)(2,1)S(1)}, u32[]{:S(2)}, u32[]{:S(2)}) collective-permute-start(bf16[2,168,512]{2,1,0:T(8,128)(2,1)S(1)} %collective-permute-done.5), channel_id=1, source_target_pairs={{0,56},{8,0},{16,8},{24,16},{32,24},{40,32},{48,40},{56,48},{1,57}... | collective-permute-start | bytes 1032200 | tf_op jit(solution)/shard_map/ppermute | solution.py:16
  34.8 7.5 %collective-permute-start.6 = (bf16[2,168,512]{2,1,0:T(8,128)(2,1)}, bf16[2,168,512]{2,1,0:T(8,128)(2,1)S(1)}, u32[]{:S(2)}, u32[]{:S(2)}) collective-permute-start(bf16[2,168,512]{2,1,0:T(8,128)(2,1)} %collective-permute-done.4), channel_id=1, source_target_pairs={{0,8},{8,16},{16,24},{24,32},{32,40},{40,48},{48,56},{56,0},{1,9},... | collective-permute-start | bytes 1032200 | tf_op jit(solution)/shard_map/ppermute | solution.py:16
  42.3 8.1 %collective-permute-start.8 = (bf16[2,168,512]{2,1,0:T(8,128)(2,1)S(1)}, bf16[2,168,512]{2,1,0:T(8,128)(2,1)S(1)}, u32[]{:S(2)}, u32[]{:S(2)}) collective-permute-start(bf16[2,168,512]{2,1,0:T(8,128)(2,1)S(1)} %collective-permute-done.6), channel_id=1, source_target_pairs={{0,8},{8,16},{16,24},{24,32},{32,40},{40,48},{48,56},{56,0},{1,9},... | collective-permute-start | bytes 1032200 | tf_op jit(solution)/shard_map/ppermute | solution.py:16
  42.3 8.2 %collective-permute-start.9 = (bf16[2,168,512]{2,1,0:T(8,128)(2,1)S(1)}, bf16[2,168,512]{2,1,0:T(8,128)(2,1)S(1)}, u32[]{:S(2)}, u32[]{:S(2)}) collective-permute-start(bf16[2,168,512]{2,1,0:T(8,128)(2,1)S(1)} %collective-permute-done.7), channel_id=1, source_target_pairs={{0,56},{8,0},{16,8},{24,16},{32,24},{40,32},{48,40},{56,48},{1,57}... | collective-permute-start | bytes 1032200 | tf_op jit(solution)/shard_map/ppermute | solution.py:16
  45.0 11.8 %collective-permute-start.13 = (bf16[256,2688]{1,0:T(8,128)(2,1)}, bf16[256,2688]{1,0:T(8,128)(2,1)S(1)}, u32[]{:S(2)}, u32[]{:S(2)}) collective-permute-start(bf16[256,2688]{1,0:T(8,128)(2,1)} %collective-permute-done.12), channel_id=1, source_target_pairs={{0,1},{1,0},{2,3},{3,2},{4,5},{5,4},{6,7},{7,6},{8,9},{9,8},{10,11... | collective-permute-start | bytes 4128776 | tf_op jit(solution)/shard_map/ppermute | solution.py:16
  50.4 6.3 %collective-permute-start.10 = (bf16[1,168,512]{2,1,0:T(8,128)(2,1)S(1)}, bf16[1,168,512]{2,1,0:T(8,128)(2,1)S(1)}, u32[]{:S(2)}, u32[]{:S(2)}) collective-permute-start(bf16[1,168,512]{2,1,0:T(8,128)(2,1)S(1)} %slice.187), channel_id=1, source_target_pairs={{0,8},{8,16},{16,24},{24,32},{32,40},{40,48},{48,56},{56,0},{1,9},... | collective-permute-start | bytes 516104 | tf_op jit(solution)/shard_map/ppermute | solution.py:16
  50.6 6.2 %collective-permute-start.11 = (bf16[1,168,512]{2,1,0:T(8,128)(2,1)S(1)}, bf16[1,168,512]{2,1,0:T(8,128)(2,1)S(1)}, u32[]{:S(2)}, u32[]{:S(2)}) collective-permute-start(bf16[1,168,512]{2,1,0:T(8,128)(2,1)S(1)} %slice.188), channel_id=1, source_target_pairs={{0,56},{8,0},{16,8},{24,16},{32,24},{40,32},{48,40},{56,48},{1,57}... | collective-permute-start | bytes 516104 | tf_op jit(solution)/shard_map/ppermute | solution.py:16
  59.3 6.3 %copy-start.1 = (bf16[512,2688]{1,0:T(8,128)(2,1)}, bf16[512,2688]{1,0:T(8,128)(2,1)S(1)}, u32[]{:S(2)}) copy-start(bf16[512,2688]{1,0:T(8,128)(2,1)S(1)} %maximum_select_fusion.x_ref) | copy-start | bytes 8257540
  59.3 9.9 %copy-start.17 = (s32[512]{0:T(512)S(1)}, s32[512]{0:T(512)}, u32[]{:S(2)}) copy-start(s32[512]{0:T(512)} %param.12) | copy-start | bytes 6148
  59.3 10.0 %copy-start.14 = (bf16[512,4,128]{2,1,0:T(4,128)(2,1)S(1)}, bf16[512,4,128]{2,1,0:T(4,128)(2,1)}, u32[]{:S(2)}) copy-start(bf16[512,4,128]{2,1,0:T(4,128)(2,1)} %param.10) | copy-start | bytes 1572868
  65.6 0.8 copy-start.10
  66.4 17.9 %collective-permute-start.14 = (f32[512,256]{1,0:T(8,128)}, f32[512,256]{1,0:T(8,128)}, u32[]{:S(2)}, u32[]{:S(2)}) collective-permute-start(f32[512,256]{1,0:T(8,128)} %get-tuple-element.57), channel_id=1, source_target_pairs={{0,4},{4,0},{1,5},{5,1},{2,6},{6,2},{3,7},{7,3},{8,12},{12,8},{9,1... | collective-permute-start | bytes 1572872 | tf_op jit(solution)/shard_map/ppermute | solution.py:16
  70.2 2.6 %copy-start = (bf16[512,5376]{1,0:T(8,128)(2,1)S(1)}, bf16[512,5376]{1,0:T(8,128)(2,1)}, u32[]{:S(2)}) copy-start(bf16[512,5376]{1,0:T(8,128)(2,1)} %x_ref.5) | copy-start | bytes 16515076
  78.3 7.5 %copy-start.16 = (f32[128]{0:T(128)S(1)}, f32[128]{0:T(128)}, u32[]{:S(2)}) copy-start(f32[128]{0:T(128)} %param.15) | copy-start | bytes 1540
  84.3 4.9 %copy-start.13 = (bf16[64,8,4,128]{3,1,2,0:T(8,128)(2,1)S(1)}, bf16[64,8,4,128]{3,1,2,0:T(8,128)(2,1)}, u32[]{:S(2)}) copy-start(bf16[64,8,4,128]{3,1,2,0:T(8,128)(2,1)} %copy.40) | copy-start | bytes 1572868
  84.3 4.9 %copy-start.15 = (bf16[512,4,128]{2,1,0:T(4,128)(2,1)S(1)}, bf16[512,4,128]{2,1,0:T(4,128)(2,1)}, u32[]{:S(2)}) copy-start(bf16[512,4,128]{2,1,0:T(4,128)(2,1)} %param.11) | copy-start | bytes 1572868
  84.4 5.0 %copy-start.11 = (f32[512,256]{1,0:T(8,128)S(1)}, f32[512,256]{1,0:T(8,128)}, u32[]{:S(2)}) copy-start(f32[512,256]{1,0:T(8,128)} %copy-done.10) | copy-start | bytes 1572868
  86.0 5.3 %collective-permute-start.16 = (bf16[528,256]{1,0:T(8,128)(2,1)S(1)}, bf16[528,256]{1,0:T(8,128)(2,1)S(1)}, u32[]{:S(2)}, u32[]{:S(2)}) collective-permute-start(bf16[528,256]{1,0:T(8,128)(2,1)S(1)} %fusion.11.own_ref), channel_id=1, source_target_pairs={{0,4},{4,8},{8,12},{12,16},{16,20},{20,24},{24,28},{28,32},{32,36}... | collective-permute-start | bytes 811016 | tf_op jit(solution)/shard_map/ppermute | solution.py:22
  87.9 4.7 %collective-permute-start.15 = (bf16[528,256]{1,0:T(8,128)(2,1)S(1)}, bf16[528,256]{1,0:T(8,128)(2,1)S(1)}, u32[]{:S(2)}, u32[]{:S(2)}) collective-permute-start(bf16[528,256]{1,0:T(8,128)(2,1)S(1)} %fusion.11.own_ref), channel_id=1, source_target_pairs={{0,8},{4,12},{8,16},{12,20},{16,24},{20,28},{24,32},{28,36},{32,40... | collective-permute-start | bytes 811016 | tf_op jit(solution)/shard_map/ppermute | solution.py:22
  89.4 15.9 %collective-permute-start.19 = (f32[512,256]{1,0:T(8,128)S(1)}, f32[512,256]{1,0:T(8,128)S(1)}, u32[]{:S(2)}, u32[]{:S(2)}) collective-permute-start(f32[512,256]{1,0:T(8,128)S(1)} %copy-done.11), channel_id=1, source_target_pairs={{0,4},{4,0},{1,5},{5,1},{2,6},{6,2},{3,7},{7,3},{8,12},{12,8},{9,1... | collective-permute-start | bytes 1572872 | tf_op jit(solution)/shard_map/ppermute | solution.py:16
  99.3 12.5 %collective-permute-start.17 = (bf16[512,256]{1,0:T(8,128)(2,1)S(1)}, bf16[512,256]{1,0:T(8,128)(2,1)S(1)}, u32[]{:S(2)}, u32[]{:S(2)}) collective-permute-start(bf16[512,256]{1,0:T(8,128)(2,1)S(1)} %get-tuple-element.102), channel_id=1, source_target_pairs={{4,0},{8,4},{12,8},{16,12},{20,16},{24,20},{28,24},{32,28},{36,32}... | collective-permute-start | bytes 786440 | tf_op jit(solution)/shard_map/ppermute | solution.py:22
  100.6 11.2 %collective-permute-start.18 = (bf16[512,256]{1,0:T(8,128)(2,1)S(1)}, bf16[512,256]{1,0:T(8,128)(2,1)S(1)}, u32[]{:S(2)}, u32[]{:S(2)}) collective-permute-start(bf16[512,256]{1,0:T(8,128)(2,1)S(1)} %get-tuple-element.103), channel_id=1, source_target_pairs={{8,0},{12,4},{16,8},{20,12},{24,16},{28,20},{32,24},{36,28},{40,32... | collective-permute-start | bytes 786440 | tf_op jit(solution)/shard_map/ppermute | solution.py:22
  105.7 6.5 %collective-permute-start.21 = (bf16[528,256]{1,0:T(8,128)(2,1)S(1)}, bf16[528,256]{1,0:T(8,128)(2,1)S(1)}, u32[]{:S(2)}, u32[]{:S(2)}) collective-permute-start(bf16[528,256]{1,0:T(8,128)(2,1)S(1)} %fusion.12.own_ref), channel_id=1, source_target_pairs={{0,4},{4,8},{8,12},{12,16},{16,20},{20,24},{24,28},{28,32},{32,36}... | collective-permute-start | bytes 811016 | tf_op jit(solution)/shard_map/ppermute | solution.py:22
  107.0 8.2 %collective-permute-start.20 = (bf16[528,256]{1,0:T(8,128)(2,1)S(1)}, bf16[528,256]{1,0:T(8,128)(2,1)S(1)}, u32[]{:S(2)}, u32[]{:S(2)}) collective-permute-start(bf16[528,256]{1,0:T(8,128)(2,1)S(1)} %fusion.12.own_ref), channel_id=1, source_target_pairs={{0,8},{4,12},{8,16},{12,20},{16,24},{20,28},{24,32},{28,36},{32,40... | collective-permute-start | bytes 811016 | tf_op jit(solution)/shard_map/ppermute | solution.py:22
  121.9 12.7 %copy-start.8 = (bf16[512,256]{1,0:T(8,128)(2,1)}, bf16[512,256]{1,0:T(8,128)(2,1)S(1)}, u32[]{:S(2)}) copy-start(bf16[512,256]{1,0:T(8,128)(2,1)S(1)} %get-tuple-element.83) | copy-start | bytes 786436
  121.9 10.9 %collective-permute-start.22 = (bf16[512,256]{1,0:T(8,128)(2,1)S(1)}, bf16[512,256]{1,0:T(8,128)(2,1)S(1)}, u32[]{:S(2)}, u32[]{:S(2)}) collective-permute-start(bf16[512,256]{1,0:T(8,128)(2,1)S(1)} %get-tuple-element.100), channel_id=1, source_target_pairs={{4,0},{8,4},{12,8},{16,12},{20,16},{24,20},{28,24},{32,28},{36,32}... | collective-permute-start | bytes 786440 | tf_op jit(solution)/shard_map/ppermute | solution.py:22
  123.2 10.7 %collective-permute-start.23 = (bf16[512,256]{1,0:T(8,128)(2,1)S(1)}, bf16[512,256]{1,0:T(8,128)(2,1)S(1)}, u32[]{:S(2)}, u32[]{:S(2)}) collective-permute-start(bf16[512,256]{1,0:T(8,128)(2,1)S(1)} %get-tuple-element.101), channel_id=1, source_target_pairs={{8,0},{12,4},{16,8},{20,12},{24,16},{28,20},{32,24},{36,28},{40,32... | collective-permute-start | bytes 786440 | tf_op jit(solution)/shard_map/ppermute | solution.py:22
  124.8 10.9 %collective-permute-start.24 = (bf16[512,256]{1,0:T(8,128)(2,1)S(1)}, bf16[512,256]{1,0:T(8,128)(2,1)S(1)}, u32[]{:S(2)}, u32[]{:S(2)}) collective-permute-start(bf16[512,256]{1,0:T(8,128)(2,1)S(1)} %pad_maximum_fusion.5), channel_id=1, source_target_pairs={{0,4},{4,0},{1,5},{5,1},{2,6},{6,2},{3,7},{7,3},{8,12},{12,8},{9,1... | collective-permute-start | bytes 786440 | tf_op jit(solution)/shard_map/ppermute | solution.py:16
  134.6 8.4 %collective-permute-start.25 = (bf16[512,256]{1,0:T(8,128)(2,1)S(1)}, bf16[512,256]{1,0:T(8,128)(2,1)S(1)}, u32[]{:S(2)}, u32[]{:S(2)}) collective-permute-start(bf16[512,256]{1,0:T(8,128)(2,1)S(1)} %pad_maximum_fusion.6), channel_id=1, source_target_pairs={{0,4},{4,0},{1,5},{5,1},{2,6},{6,2},{3,7},{7,3},{8,12},{12,8},{9,1... | collective-permute-start | bytes 786440 | tf_op jit(solution)/shard_map/ppermute | solution.py:16
  135.7 10.7 %copy-start.2 = (bf16[512,512]{1,0:T(8,128)(2,1)}, bf16[512,512]{1,0:T(8,128)(2,1)S(1)}, u32[]{:S(2)}) copy-start(bf16[512,512]{1,0:T(8,128)(2,1)S(1)} %pad_maximum_fusion.2.g_ref) | copy-start | bytes 1572868
  143.0 3.4 %copy-start.4 = (bf16[512,512]{1,0:T(8,128)(2,1)}, bf16[512,512]{1,0:T(8,128)(2,1)S(1)}, u32[]{:S(2)}) copy-start(bf16[512,512]{1,0:T(8,128)(2,1)S(1)} %constant_dynamic-update-slice_fusion.h_ref) | copy-start | bytes 1572868
  146.4 36.1 %collective-permute-start.26 = (bf16[1344,1024]{1,0:T(8,128)(2,1)}, bf16[1344,1024]{1,0:T(8,128)(2,1)}, u32[]{:S(2)}, u32[]{:S(2)}) collective-permute-start(bf16[1344,1024]{1,0:T(8,128)(2,1)} %shard_map.109), channel_id=1, source_target_pairs={{0,1},{1,0},{2,3},{3,2},{4,5},{5,4},{6,7},{7,6},{8,9},{9,8},{10,11... | collective-permute-start | bytes 8257544 | tf_op jit(solution)/shard_map/ppermute | solution.py:16
  164.0 15.3 %collective-permute-start.28 = (bf16[1,168,512]{2,1,0:T(8,128)(2,1)S(1)}, bf16[1,168,512]{2,1,0:T(8,128)(2,1)S(1)}, u32[]{:S(2)}, u32[]{:S(2)}) collective-permute-start(bf16[1,168,512]{2,1,0:T(8,128)(2,1)S(1)} %get-tuple-element.92), channel_id=1, source_target_pairs={{0,56},{8,0},{16,8},{24,16},{32,24},{40,32},{48,40},{56,48},{1,57}... | collective-permute-start | bytes 516104 | tf_op jit(solution)/shard_map/ppermute | solution.py:16
  175.6 6.9 %copy-start.3 = (bf16[512,512]{1,0:T(8,128)(2,1)S(1)}, bf16[512,512]{1,0:T(8,128)(2,1)}, u32[]{:S(2)}) copy-start(bf16[512,512]{1,0:T(8,128)(2,1)} %copy-done.2) | copy-start | bytes 1572868
  175.6 6.9 %copy-start.5 = (bf16[512,512]{1,0:T(8,128)(2,1)S(1)}, bf16[512,512]{1,0:T(8,128)(2,1)}, u32[]{:S(2)}) copy-start(bf16[512,512]{1,0:T(8,128)(2,1)} %copy-done.4) | copy-start | bytes 1572868
  175.6 6.8 %collective-permute-start.27 = (bf16[1,168,512]{2,1,0:T(8,128)(2,1)S(1)}, bf16[1,168,512]{2,1,0:T(8,128)(2,1)S(1)}, u32[]{:S(2)}, u32[]{:S(2)}) collective-permute-start(bf16[1,168,512]{2,1,0:T(8,128)(2,1)S(1)} %get-tuple-element.93), channel_id=1, source_target_pairs={{0,8},{8,16},{16,24},{24,32},{32,40},{40,48},{48,56},{56,0},{1,9},... | collective-permute-start | bytes 516104 | tf_op jit(solution)/shard_map/ppermute | solution.py:16
  186.5 1.5 copy-start.6
  188.1 11.4 %copy-start.12 = (bf16[2688,512]{1,0:T(8,128)(2,1)S(1)}, bf16[2688,512]{1,0:T(8,128)(2,1)}, u32[]{:S(2)}) copy-start(bf16[2688,512]{1,0:T(8,128)(2,1)} %shard_map.111) | copy-start | bytes 8257540
  189.8 9.7 %collective-permute-start.31 = (bf16[2,168,512]{2,1,0:T(8,128)(2,1)S(1)}, bf16[2,168,512]{2,1,0:T(8,128)(2,1)S(1)}, u32[]{:S(2)}, u32[]{:S(2)}) collective-permute-start(bf16[2,168,512]{2,1,0:T(8,128)(2,1)S(1)} %pad_maximum_fusion), channel_id=1, source_target_pairs={{0,8},{8,16},{16,24},{24,32},{32,40},{40,48},{48,56},{56,0},{1,9},... | collective-permute-start | bytes 1032200 | tf_op jit(solution)/shard_map/ppermute | solution.py:16
  189.8 9.7 %collective-permute-start.34 = (bf16[2,168,512]{2,1,0:T(8,128)(2,1)S(1)}, bf16[2,168,512]{2,1,0:T(8,128)(2,1)S(1)}, u32[]{:S(2)}, u32[]{:S(2)}) collective-permute-start(bf16[2,168,512]{2,1,0:T(8,128)(2,1)S(1)} %pad_maximum_fusion.1), channel_id=1, source_target_pairs={{0,56},{8,0},{16,8},{24,16},{32,24},{40,32},{48,40},{56,48},{1,57}... | collective-permute-start | bytes 1032200 | tf_op jit(solution)/shard_map/ppermute | solution.py:16
  199.7 8.9 %collective-permute-start.32 = (bf16[2,168,512]{2,1,0:T(8,128)(2,1)S(1)}, bf16[2,168,512]{2,1,0:T(8,128)(2,1)S(1)}, u32[]{:S(2)}, u32[]{:S(2)}) collective-permute-start(bf16[2,168,512]{2,1,0:T(8,128)(2,1)S(1)} %get-tuple-element.88), channel_id=1, source_target_pairs={{0,8},{8,16},{16,24},{24,32},{32,40},{40,48},{48,56},{56,0},{1,9},... | collective-permute-start | bytes 1032200 | tf_op jit(solution)/shard_map/ppermute | solution.py:16
  199.7 8.8 %collective-permute-start.35 = (bf16[2,168,512]{2,1,0:T(8,128)(2,1)S(1)}, bf16[2,168,512]{2,1,0:T(8,128)(2,1)S(1)}, u32[]{:S(2)}, u32[]{:S(2)}) collective-permute-start(bf16[2,168,512]{2,1,0:T(8,128)(2,1)S(1)} %get-tuple-element.89), channel_id=1, source_target_pairs={{0,56},{8,0},{16,8},{24,16},{32,24},{40,32},{48,40},{56,48},{1,57}... | collective-permute-start | bytes 1032200 | tf_op jit(solution)/shard_map/ppermute | solution.py:16
  208.7 26.0 %copy-start.9 = (bf16[512,256]{1,0:T(8,128)(2,1)S(1)}, bf16[512,256]{1,0:T(8,128)(2,1)}, u32[]{:S(2)}) copy-start(bf16[512,256]{1,0:T(8,128)(2,1)} %copy-done.8) | copy-start | bytes 786436
  208.7 8.0 %collective-permute-start.33 = (bf16[2,168,512]{2,1,0:T(8,128)(2,1)S(1)}, bf16[2,168,512]{2,1,0:T(8,128)(2,1)S(1)}, u32[]{:S(2)}, u32[]{:S(2)}) collective-permute-start(bf16[2,168,512]{2,1,0:T(8,128)(2,1)S(1)} %get-tuple-element.86), channel_id=1, source_target_pairs={{0,8},{8,16},{16,24},{24,32},{32,40},{40,48},{48,56},{56,0},{1,9},... | collective-permute-start | bytes 1032200 | tf_op jit(solution)/shard_map/ppermute | solution.py:16
  208.8 7.9 %collective-permute-start.36 = (bf16[2,168,512]{2,1,0:T(8,128)(2,1)S(1)}, bf16[2,168,512]{2,1,0:T(8,128)(2,1)S(1)}, u32[]{:S(2)}, u32[]{:S(2)}) collective-permute-start(bf16[2,168,512]{2,1,0:T(8,128)(2,1)S(1)} %get-tuple-element.87), channel_id=1, source_target_pairs={{0,56},{8,0},{16,8},{24,16},{32,24},{40,32},{48,40},{56,48},{1,57}... | collective-permute-start | bytes 1032200 | tf_op jit(solution)/shard_map/ppermute | solution.py:16
  211.5 36.2 %collective-permute-start.29 = (bf16[1344,512]{1,0:T(8,128)(2,1)}, bf16[1344,512]{1,0:T(8,128)(2,1)}, u32[]{:S(2)}, u32[]{:S(2)}) collective-permute-start(bf16[1344,512]{1,0:T(8,128)(2,1)} %get-tuple-element.80), channel_id=1, source_target_pairs={{2,4},{4,2},{3,5},{5,3},{10,12},{12,10},{11,13},{13,11},{18,20},{2... | collective-permute-start | bytes 4128776 | tf_op jit(solution)/shard_map/ppermute | solution.py:542
  213.2 34.4 %collective-permute-start.30 = (bf16[1344,512]{1,0:T(8,128)(2,1)}, bf16[1344,512]{1,0:T(8,128)(2,1)}, u32[]{:S(2)}, u32[]{:S(2)}) collective-permute-start(bf16[1344,512]{1,0:T(8,128)(2,1)} %get-tuple-element.81), channel_id=1, source_target_pairs={{0,4},{6,2},{2,0},{4,6},{1,5},{7,3},{3,1},{5,7},{8,12},{14,10},{10... | collective-permute-start | bytes 4128776 | tf_op jit(solution)/shard_map/ppermute | solution.py:541
  219.6 8.3 %collective-permute-start.39 = (bf16[168,512]{1,0:T(8,128)(2,1)}, bf16[168,512]{1,0:T(8,128)(2,1)}, u32[]{:S(2)}, u32[]{:S(2)}) collective-permute-start(bf16[168,512]{1,0:T(8,128)(2,1)} %get-tuple-element.97), channel_id=1, source_target_pairs={{128,0},{192,64},{4,132},{68,196},{129,1},{193,65},{5,133},{69,197... | collective-permute-start | bytes 516104 | tf_op jit(solution)/shard_map/ppermute | solution.py:87
  220.9 8.8 %collective-permute-start.38 = (bf16[168,512]{1,0:T(8,128)(2,1)S(1)}, bf16[168,512]{1,0:T(8,128)(2,1)}, u32[]{:S(2)}, u32[]{:S(2)}) collective-permute-start(bf16[168,512]{1,0:T(8,128)(2,1)S(1)} %get-tuple-element.96), channel_id=1, source_target_pairs={{192,0},{128,64},{68,132},{4,196},{193,1},{129,65},{69,133},{5,197... | collective-permute-start | bytes 516104 | tf_op jit(solution)/shard_map/ppermute | solution.py:87
  222.2 7.5 %collective-permute-start.37 = (bf16[168,512]{1,0:T(8,128)(2,1)S(1)}, bf16[168,512]{1,0:T(8,128)(2,1)}, u32[]{:S(2)}, u32[]{:S(2)}) collective-permute-start(bf16[168,512]{1,0:T(8,128)(2,1)S(1)} %get-tuple-element.96), channel_id=1, source_target_pairs={{64,0},{0,64},{196,132},{132,196},{65,1},{1,65},{197,133},{133,197... | collective-permute-start | bytes 516104 | tf_op jit(solution)/shard_map/ppermute | solution.py:87
  224.2 23.5 %copy-start.7 = (f32[1344,512]{1,0:T(8,128)S(1)}, f32[1344,512]{1,0:T(8,128)}, u32[]{:S(2)}) copy-start(f32[1344,512]{1,0:T(8,128)} %copy-done.6) | copy-start | bytes 8257540
  234.6 10.8 %collective-permute-start.40 = (bf16[84,512]{1,0:T(8,128)(2,1)S(1)}, bf16[84,512]{1,0:T(8,128)(2,1)S(1)}, u32[]{:S(2)}, u32[]{:S(2)}) collective-permute-start(bf16[84,512]{1,0:T(8,128)(2,1)S(1)} %fusion.14), channel_id=1, source_target_pairs={{0,4},{4,0},{1,5},{5,1},{2,6},{6,2},{3,7},{7,3},{8,12},{12,8},{9,1... | collective-permute-start | bytes 258056 | tf_op jit(solution)/shard_map/ppermute | solution.py:16
where the time goes:
time: 255 us; the launch traced here: 251 us
  starting transfers between devices  87.6 us (34%)
  waiting for transfers between devices  70.1 us (27%)
  Pallas kernels  56.2 us (22%)
  other arithmetic  21.5 us (8%)
  local copies, waits for them, and re-layouts  14.2 us (6%)
    ppermute x25, starting transfers between devices, hop(): return lax.ppermute(block, axis, [(i, (i + step) % n) for i in range(n)])  56.3 us
    ppermute x25, waiting for transfers between devices, hop(): return lax.ppermute(block, axis, [(i, (i + step) % n) for i in range(n)])  48.7 us
    ppermute x8, starting transfers between devices, seq_shift(): return lax.ppermute(block, ('y', 'z', 'xl'), route)  14.5 us
    pallas_call x2, Pallas kernels, attention(): pl.pallas_call(attention_kernel, grid=(tok // QB,), in_specs=[whole] * 6,...  13.4 us
    ppermute x6, starting transfers between devices, y_route(): lax.ppermute(block, ('y', 'xl'), [(b, a) for a, b in pairs] if back else...  12.7 us
    pallas_call x2, Pallas kernels, turned(): pl.pallas_call(turn_kernel, grid_spec=pltpu.PrefetchScalarGridSpec(num_sc...  12.1 us
    pallas_call x2, Pallas kernels, project(): pl.pallas_call(project_kernel, grid_spec=pltpu.PrefetchScalarGridSpec(num...  11.9 us
    ppermute x8, waiting for transfers between devices, seq_shift(): return lax.ppermute(block, ('y', 'z', 'xl'), route)  11.2 us
  transfers between devices with their start and end apart: 41, of which 21 were waited for; matrix products, arithmetic and copies ran while one was open for 8% of the time, Pallas kernels for 14%

commit v1 on v0

--- a/solution.py
+++ b/solution.py
@@ -127,7 +127,8 @@
     for block, route in ((other, SWAP), (other, NEAR), (mine.astype(BF16), FAR)):
         over_y = over_y + y_route(block, route, True).astype(F32)
     parts = over_y.reshape(NX, -1, width)
-    away = hop(take(parts, 1 - xl, 0).astype(BF16), "xl", NX, 1)
+    give = take(parts, 1 - xl, 0).astype(BF16)
+    away = hop(give, "xl", NX, 1)
     return take(parts, xl, 0) + away.astype(F32)
 
 
@@ -287,7 +288,7 @@
         in_specs=[left, left, right, right],
         out_specs=pl.BlockSpec((block, width), lambda i: (i, 0)),
         out_shape=jax.ShapeDtypeStruct((depth, width), BF16),
-        compiler_params=pltpu.CompilerParams(vmem_limit_bytes=60 << 20),
+        compiler_params=pltpu.CompilerParams(vmem_limit_bytes=16 << 20),
         cost_estimate=pl.CostEstimate(
             flops=4 * depth * tok * width, bytes_accessed=12 << 20, transcendentals=0
         ),
@@ -310,7 +311,7 @@
             out_specs=pl.BlockSpec((rows, cols), lambda i, w: (i, 0)),
         ),
         out_shape=jax.ShapeDtypeStruct((2 * rows, cols), inputs.dtype),
-        compiler_params=pltpu.CompilerParams(vmem_limit_bytes=60 << 20),
+        compiler_params=pltpu.CompilerParams(vmem_limit_bytes=8 << 20),
         cost_estimate=pl.CostEstimate(flops=0, bytes_accessed=3 << 20, transcendentals=0),
     )(where, inputs)
 
@@ -332,7 +333,7 @@
             out_specs=pl.BlockSpec((cols, tok), lambda i, w: (i, 0)),
         ),
         out_shape=jax.ShapeDtypeStruct((depth, tok), inputs.dtype),
-        compiler_params=pltpu.CompilerParams(vmem_limit_bytes=60 << 20),
+        compiler_params=pltpu.CompilerParams(vmem_limit_bytes=8 << 20),
         cost_estimate=pl.CostEstimate(flops=0, bytes_accessed=6 << 20, transcendentals=0),
     )(where, inputs)
 
@@ -425,6 +426,28 @@
     )(where, weight, own_grads, par_grads, *more)
 
 
+def finish_kernel(keep, own_ref, first_ref, second_ref, o_ref):
+    base = jnp.where(keep[0] == 1, own_ref[...], second_ref[...].astype(F32))
+    o_ref[...] = (base + first_ref[...].astype(F32)).astype(BF16)
+
+
+def finish(keep, own, first, second):
+    depth, tok = own.shape
+    steps = 4
+    block = pl.BlockSpec((depth // steps, tok), lambda i, w: (i, 0))
+    return pl.pallas_call(
+        finish_kernel,
+        grid_spec=pltpu.PrefetchScalarGridSpec(
+            num_scalar_prefetch=1, grid=(steps,), in_specs=[block] * 3, out_specs=block
+        ),
+        out_shape=jax.ShapeDtypeStruct((depth, tok), BF16),
+        compiler_params=pltpu.CompilerParams(vmem_limit_bytes=8 << 20),
+        cost_estimate=pl.CostEstimate(
+            flops=4 * depth * tok, bytes_accessed=10 * depth * tok, transcendentals=0
+        ),
+    )(keep, own, first, second)
+
+
 def after(value, *others):
     return lax.optimization_barrier((value, *others))[0]
 
@@ -540,8 +563,9 @@
 
     first = lax.ppermute(held["first"], ("xl", "xh"), [(0, 2), (3, 1), (1, 0), (2, 3)])
     second = lax.ppermute(held["second"], ("xl", "xh"), [(1, 2), (2, 1)])
-    inputs_grad = jnp.where(keep, held["own"], second.astype(F32)) + first.astype(F32)
-    return inputs_grad.astype(BF16).T, query_grad, k_weight_grad, v_weight_grad
+    keep_array = jnp.full((1,), keep, jnp.int32)
+    inputs_grad = finish(keep_array, held["own"], first, second)
+    return inputs_grad.T, query_grad, k_weight_grad, v_weight_grad
 
 
 def solution(mesh):

time: 255 us -> 247 us (0.969)
  local copies, waits for them, and re-layouts: 14.2 us -> 25.4 us
  Pallas kernels: 56.2 us -> 45.6 us
  other arithmetic: 21.5 us -> 16.3 us
    unnamed x39, local copies, waits for them, and re-layouts: 5.91 us -> 18.1 us
    pallas_call x2, Pallas kernels: 12.1 us -> 3.01 us  [turned(): pl.pallas_call(turn_kernel, grid_spec=pltpu.PrefetchScalarGridSpec(num_sc...]
    ppermute x25, starting transfers between devices: 56.3 us -> 47.2 us  [hop(): return lax.ppermute(block, axis, [(i, (i + step) % n) for i in range(n)])]
    ppermute x8, starting transfers between devices: 14.5 us -> 21.6 us  [seq_shift(): return lax.ppermute(block, ('y', 'z', 'xl'), route)]
    ppermute x25, waiting for transfers between devices: 48.7 us -> 44 us  [hop(): return lax.ppermute(block, axis, [(i, (i + step) % n) for i in range(n)])]
    pallas_call x1, Pallas kernels: 8.68 us -> 4.18 us  [weight_grad(): pl.pallas_call(weight_grad_kernel, grid=(8,), in_specs=[left, left, right...]
    pallas_call x0 -> x1, Pallas kernels: none -> 3.9 us  [finish(): pl.pallas_call(finish_kernel, grid_spec=pltpu.PrefetchScalarGridSpec(num_...]
    transpose x1 -> x0, other arithmetic: 3.4 us -> none  [per_device(): inputs_grad.astype(BF16)]
  transfers between devices with their start and end apart: 41 -> 41, of which waited for: 21 -> 20; matrix products, arithmetic and copies ran while one was open for 8% -> 7% of each run, Pallas kernels for 14% -> 9%
where the time goes in v1:
time: 247 us; the launch traced here: 244 us
  starting transfers between devices  85.8 us (35%)
  waiting for transfers between devices  69 us (28%)
  Pallas kernels  45.6 us (18%)
  local copies, waits for them, and re-layouts  25.4 us (10%)
  other arithmetic  16.3 us (7%)
    ppermute x25, starting transfers between devices, hop(): return lax.ppermute(block, axis, [(i, (i + step) % n) for i in range(n)])  47.2 us
    ppermute x25, waiting for transfers between devices, hop(): return lax.ppermute(block, axis, [(i, (i + step) % n) for i in range(n)])  44 us
    ppermute x8, starting transfers between devices, seq_shift(): return lax.ppermute(block, ('y', 'z', 'xl'), route)  21.6 us
    unnamed x39, local copies, waits for them, and re-layouts  18.1 us
    ppermute x6, starting transfers between devices, y_route(): lax.ppermute(block, ('y', 'xl'), [(b, a) for a, b in pairs] if back else...  13.8 us
    ppermute x8, waiting for transfers between devices, seq_shift(): return lax.ppermute(block, ('y', 'z', 'xl'), route)  13.6 us
    pallas_call x2, Pallas kernels, attention(): pl.pallas_call(attention_kernel, grid=(tok // QB,), in_specs=[whole] * 6,...  13.4 us
    pallas_call x2, Pallas kernels, project(): pl.pallas_call(project_kernel, grid_spec=pltpu.PrefetchScalarGridSpec(num...  11.9 us
  transfers between devices with their start and end apart: 41, of which 20 were waited for; matrix products, arithmetic and copies ran while one was open for 7% of the time, Pallas kernels for 9%

profile of v1, /device:TPU:1, one launch (start us, length us, event | category | flops | bytes accessed | tf_op | source)
XLA Modules:
  0.0 243.5 jit_solution(3555445845958120386)
XLA Ops:
  1.4 2.1 collective-permute-start
  3.6 2.6 %copy-done = bf16[512,5376]{1,0:T(8,128)(2,1)S(1)} copy-done((bf16[512,5376]{1,0:T(8,128)(2,1)S(1)}, bf16[512,5376]{1,0:T(8,128)(2,1)}, u32[]{:S(2)}) %copy-start) | copy-done | bytes 5505048
  6.2 1.8 shard_map.103
  8.1 5.1 %collective-permute-start.1 = (bf16[168,512]{1,0:T(8,128)(2,1)S(1)}, bf16[168,512]{1,0:T(8,128)(2,1)S(1)}, u32[]{:S(2)}, u32[]{:S(2)}) collective-permute-start(bf16[168,512]{1,0:T(8,128)(2,1)S(1)} %maximum_select_fusion.1), channel_id=1, source_target_pairs={{0,128},{64,192},{132,4},{196,68},{1,129},{65,193},{133,5},{197,69... | collective-permute-start | bytes 516104 | tf_op jit(solution)/shard_map/ppermute | solution.py:87
  13.2 2.3 collective-permute-start.2
  16.8 4.2 %collective-permute-done.2 = bf16[168,512]{1,0:T(8,128)(2,1)S(1)} collective-permute-done((bf16[168,512]{1,0:T(8,128)(2,1)S(1)}, bf16[168,512]{1,0:T(8,128)(2,1)S(1)}, u32[]{:S(2)}, u32[]{:S(2)}) %collective-permute-start.2) | collective-permute-done | bytes 172064 | tf_op jit(solution)/shard_map/ppermute | solution.py:87
  21.1 1.7 collective-permute-start.4
  22.8 4.0 %collective-permute-start.5 = (bf16[2,168,512]{2,1,0:T(8,128)(2,1)S(1)}, bf16[2,168,512]{2,1,0:T(8,128)(2,1)}, u32[]{:S(2)}, u32[]{:S(2)}) collective-permute-start(bf16[2,168,512]{2,1,0:T(8,128)(2,1)S(1)} %pad_maximum_fusion.4), channel_id=1, source_target_pairs={{0,56},{8,0},{16,8},{24,16},{32,24},{40,32},{48,40},{56,48},{1,57}... | collective-permute-start | bytes 1032200 | tf_op jit(solution)/shard_map/ppermute | solution.py:16
  26.8 2.6 %copy-done.1 = bf16[512,5376]{1,0:T(8,128)(2,1)S(1)} copy-done((bf16[512,5376]{1,0:T(8,128)(2,1)S(1)}, bf16[512,5376]{1,0:T(8,128)(2,1)}, u32[]{:S(2)}) %copy-start.1) | copy-done | bytes 5505048
  29.4 1.5 shard_map.102.own_ref
  30.9 1.5 copy-done.7
  33.6 2.7 %collective-permute-start.7 = (bf16[2,168,512]{2,1,0:T(8,128)(2,1)}, bf16[2,168,512]{2,1,0:T(8,128)(2,1)S(1)}, u32[]{:S(2)}, u32[]{:S(2)}) collective-permute-start(bf16[2,168,512]{2,1,0:T(8,128)(2,1)} %collective-permute-done.5), channel_id=1, source_target_pairs={{0,56},{8,0},{16,8},{24,16},{32,24},{40,32},{48,40},{56,48},{1,57}... | collective-permute-start | bytes 1032200 | tf_op jit(solution)/shard_map/ppermute | solution.py:16
  37.4 4.9 %collective-permute-done.6 = bf16[2,168,512]{2,1,0:T(8,128)(2,1)S(1)} collective-permute-done((bf16[2,168,512]{2,1,0:T(8,128)(2,1)S(1)}, bf16[2,168,512]{2,1,0:T(8,128)(2,1)S(1)}, u32[]{:S(2)}, u32[]{:S(2)}) %collective-permute-start.6) | collective-permute-done | bytes 344096 | tf_op jit(solution)/shard_map/ppermute | solution.py:16
  42.3 2.7 %collective-permute-start.9 = (bf16[2,168,512]{2,1,0:T(8,128)(2,1)S(1)}, bf16[2,168,512]{2,1,0:T(8,128)(2,1)S(1)}, u32[]{:S(2)}, u32[]{:S(2)}) collective-permute-start(bf16[2,168,512]{2,1,0:T(8,128)(2,1)S(1)} %collective-permute-done.7), channel_id=1, source_target_pairs={{0,56},{8,0},{16,8},{24,16},{32,24},{40,32},{48,40},{56,48},{1,57}... | collective-permute-start | bytes 1032200 | tf_op jit(solution)/shard_map/ppermute | solution.py:16
  45.0 3.6 %collective-permute-start.13 = (bf16[256,2688]{1,0:T(8,128)(2,1)}, bf16[256,2688]{1,0:T(8,128)(2,1)S(1)}, u32[]{:S(2)}, u32[]{:S(2)}) collective-permute-start(bf16[256,2688]{1,0:T(8,128)(2,1)} %collective-permute-done.12), channel_id=1, source_target_pairs={{0,1},{1,0},{2,3},{3,2},{4,5},{5,4},{6,7},{7,6},{8,9},{9,8},{10,11... | collective-permute-start | bytes 4128776 | tf_op jit(solution)/shard_map/ppermute | solution.py:16
  48.6 1.5 collective-permute-done.8
  50.2 2.7 %collective-permute-start.11 = (bf16[1,168,512]{2,1,0:T(8,128)(2,1)S(1)}, bf16[1,168,512]{2,1,0:T(8,128)(2,1)S(1)}, u32[]{:S(2)}, u32[]{:S(2)}) collective-permute-start(bf16[1,168,512]{2,1,0:T(8,128)(2,1)S(1)} %slice.188), channel_id=1, source_target_pairs={{0,56},{8,0},{16,8},{24,16},{32,24},{40,32},{48,40},{56,48},{1,57}... | collective-permute-start | bytes 516104 | tf_op jit(solution)/shard_map/ppermute | solution.py:16
  53.0 2.6 %collective-permute-done.10 = bf16[1,168,512]{2,1,0:T(8,128)(2,1)S(1)} collective-permute-done((bf16[1,168,512]{2,1,0:T(8,128)(2,1)S(1)}, bf16[1,168,512]{2,1,0:T(8,128)(2,1)S(1)}, u32[]{:S(2)}, u32[]{:S(2)}) %collective-permute-start.10) | collective-permute-done | bytes 172064 | tf_op jit(solution)/shard_map/ppermute | solution.py:16
  55.7 2.5 %maximum_select_fusion.x_ref = bf16[512,2688]{1,0:T(8,128)(2,1)S(1)} fusion(bf16[256,2688]{1,0:T(8,128)(2,1)S(1)} %collective-permute-done.13, bf16[256,2688]{1,0:T(8,128)(2,1)} %collective-permute-done.12, pred[]{:T(512)S(6)} %eq.21), kind=kLoop, calls=%fused_computation | loop fusion | flops 12386304 | bytes 5505025 | tf_op jit(solution)/shard_map/jit(_where)/select_n | solution.py:485
  58.3 6.3 %shard_map.104 = (f32[512,256]{1,0:T(8,128)S(1)}, f32[512,256]{1,0:T(8,128)}) custom-call(s32[1]{0:T(128)} %constant.161.clone.1.where, bf16[512,2688]{1,0:T(8,128)(2,1)S(1)} %maximum_select_fusion.x_ref, bf16[2688,512]{1,0:T(8,128)(2,1)S(1)} %bitcast.103), custom_call_target="tpu_custom_call" | custom-call | flops 1409286144 | bytes 8388608 | tf_op jit(solution)/shard_map/pallas_call | solution.py:364
  65.8 2.6 %copy-done.2 = bf16[512,5376]{1,0:T(8,128)(2,1)S(1)} copy-done((bf16[512,5376]{1,0:T(8,128)(2,1)S(1)}, bf16[512,5376]{1,0:T(8,128)(2,1)}, u32[]{:S(2)}) %copy-start.2) | copy-done | bytes 5505048
  68.3 5.6 %shard_map.105 = (f32[512,256]{1,0:T(8,128)S(1)}, f32[512,256]{1,0:T(8,128)S(1)}) custom-call(s32[1]{0:T(128)} %bitcast.10.where, bf16[512,5376]{1,0:T(8,128)(2,1)S(1)} %copy-done.2, bf16[2688,512]{1,0:T(8,128)(2,1)S(1)} %bitcast.104), custom_call_target="tpu_custom_call" | custom-call | flops 1409286144 | bytes 8388608 | tf_op jit(solution)/shard_map/pallas_call | solution.py:364
  73.9 1.5 shard_map.106.par_ref
  75.4 1.5 copy-done.9
  78.5 3.6 %collective-permute-start.15 = (bf16[528,256]{1,0:T(8,128)(2,1)S(1)}, bf16[528,256]{1,0:T(8,128)(2,1)S(1)}, u32[]{:S(2)}, u32[]{:S(2)}) collective-permute-start(bf16[528,256]{1,0:T(8,128)(2,1)S(1)} %fusion.10.own_ref), channel_id=1, source_target_pairs={{0,8},{4,12},{8,16},{12,20},{16,24},{20,28},{24,32},{28,36},{32,40... | collective-permute-start | bytes 811016 | tf_op jit(solution)/shard_map/ppermute | solution.py:22
  82.2 3.5 %collective-permute-start.16 = (bf16[528,256]{1,0:T(8,128)(2,1)S(1)}, bf16[528,256]{1,0:T(8,128)(2,1)S(1)}, u32[]{:S(2)}, u32[]{:S(2)}) collective-permute-start(bf16[528,256]{1,0:T(8,128)(2,1)S(1)} %fusion.10.own_ref), channel_id=1, source_target_pairs={{0,4},{4,8},{8,12},{12,16},{16,20},{20,24},{24,28},{28,32},{32,36}... | collective-permute-start | bytes 811016 | tf_op jit(solution)/shard_map/ppermute | solution.py:22
  87.2 1.7 collective-permute-done.16.one_ref
  88.8 6.7 %shard_map.107 = (bf16[512,256]{1,0:T(8,128)(2,1)S(1)}, bf16[1024,256]{1,0:T(8,128)(2,1)S(1)}, f32[512,256]{1,0:T(8,128)S(1)}) custom-call(bf16[512,256]{1,0:T(8,128)(2,1)S(1)} %get-tuple-element.106.q_ref, bf16[512,256]{1,0:T(8,128)(2,1)S(1)} %get-tuple-element.104.do_ref, bf16[528,256]{1,0:T(8,128)(2,1)S(1)} %collective-permute-done.15.two_ref, ...), custom_call_target="tpu_custom_call" | custom-call | flops 1677721600 | bytes 8388608 | tf_op jit(solution)/shard_map/pallas_call | solution.py:248
  98.8 6.1 %collective-permute-start.20 = (bf16[528,256]{1,0:T(8,128)(2,1)S(1)}, bf16[528,256]{1,0:T(8,128)(2,1)S(1)}, u32[]{:S(2)}, u32[]{:S(2)}) collective-permute-start(bf16[528,256]{1,0:T(8,128)(2,1)S(1)} %fusion.11.own_ref), channel_id=1, source_target_pairs={{0,8},{4,12},{8,16},{12,20},{16,24},{20,28},{24,32},{28,36},{32,40... | collective-permute-start | bytes 811016 | tf_op jit(solution)/shard_map/ppermute | solution.py:22
  104.9 3.3 %collective-permute-start.21 = (bf16[528,256]{1,0:T(8,128)(2,1)S(1)}, bf16[528,256]{1,0:T(8,128)(2,1)S(1)}, u32[]{:S(2)}, u32[]{:S(2)}) collective-permute-start(bf16[528,256]{1,0:T(8,128)(2,1)S(1)} %fusion.11.own_ref), channel_id=1, source_target_pairs={{0,4},{4,8},{8,12},{12,16},{16,20},{20,24},{24,28},{28,32},{32,36}... | collective-permute-start | bytes 811016 | tf_op jit(solution)/shard_map/ppermute | solution.py:22
  108.6 5.8 %collective-permute-done.21.one_ref = bf16[528,256]{1,0:T(8,128)(2,1)S(1)} collective-permute-done((bf16[528,256]{1,0:T(8,128)(2,1)S(1)}, bf16[528,256]{1,0:T(8,128)(2,1)S(1)}, u32[]{:S(2)}, u32[]{:S(2)}) %collective-permute-start.21) | collective-permute-done | bytes 270368 | tf_op jit(solution)/shard_map/ppermute | solution.py:22
  114.4 6.7 %shard_map.108 = (bf16[512,256]{1,0:T(8,128)(2,1)S(1)}, bf16[1024,256]{1,0:T(8,128)(2,1)S(1)}, f32[512,256]{1,0:T(8,128)S(1)}) custom-call(bf16[512,256]{1,0:T(8,128)(2,1)S(1)} %get-tuple-element.107.q_ref, bf16[512,256]{1,0:T(8,128)(2,1)S(1)} %get-tuple-element.105.do_ref, bf16[528,256]{1,0:T(8,128)(2,1)S(1)} %collective-permute-done.20.two_ref, ...), custom_call_target="tpu_custom_call" | custom-call | flops 1677721600 | bytes 8388608 | tf_op jit(solution)/shard_map/pallas_call | solution.py:248
  124.0 2.8 %collective-permute-start.24 = (bf16[512,256]{1,0:T(8,128)(2,1)S(1)}, bf16[512,256]{1,0:T(8,128)(2,1)S(1)}, u32[]{:S(2)}, u32[]{:S(2)}) collective-permute-start(bf16[512,256]{1,0:T(8,128)(2,1)S(1)} %pad_maximum_fusion.5), channel_id=1, source_target_pairs={{0,4},{4,0},{1,5},{5,1},{2,6},{6,2},{3,7},{7,3},{8,12},{12,8},{9,1... | collective-permute-start | bytes 786440 | tf_op jit(solution)/shard_map/ppermute | solution.py:16
  126.8 4.7 %collective-permute-done.22 = bf16[512,256]{1,0:T(8,128)(2,1)S(1)} collective-permute-done((bf16[512,256]{1,0:T(8,128)(2,1)S(1)}, bf16[512,256]{1,0:T(8,128)(2,1)S(1)}, u32[]{:S(2)}, u32[]{:S(2)}) %collective-permute-start.22) | collective-permute-done | bytes 262176 | tf_op jit(solution)/shard_map/ppermute | solution.py:22
  131.5 1.4 collective-permute-done.23
  133.6 1.8 collective-permute-done.24
  135.5 6.4 %collective-permute-done.25 = bf16[512,256]{1,0:T(8,128)(2,1)S(1)} collective-permute-done((bf16[512,256]{1,0:T(8,128)(2,1)S(1)}, bf16[512,256]{1,0:T(8,128)(2,1)S(1)}, u32[]{:S(2)}, u32[]{:S(2)}) %collective-permute-start.25) | collective-permute-done | bytes 262176 | tf_op jit(solution)/shard_map/ppermute | solution.py:16
  142.0 3.5 %shard_map.109 = bf16[1344,1024]{1,0:T(8,128)(2,1)} custom-call(s32[1]{0:T(128)S(6)} %sub.43.where, bf16[2688,512]{1,0:T(8,128)(2,1)S(1)} %bitcast.105, bf16[512,512]{1,0:T(8,128)(2,1)S(1)} %pad_maximum_fusion.2.g_ref, bf16[512,512]{1,0:T(8,128)(2,1)S(1)} %constant_dynamic-update-slice_fusion.h_ref), custom_call_target="tpu_custom_call" | custom-call | flops 1409286144 | bytes 6291456 | tf_op jit(solution)/shard_map/pallas_call | solution.py:416
  145.5 6.9 %collective-permute-start.26 = (bf16[1344,1024]{1,0:T(8,128)(2,1)}, bf16[1344,1024]{1,0:T(8,128)(2,1)}, u32[]{:S(2)}, u32[]{:S(2)}) collective-permute-start(bf16[1344,1024]{1,0:T(8,128)(2,1)} %shard_map.109), channel_id=1, source_target_pairs={{0,1},{1,0},{2,3},{3,2},{4,5},{5,4},{6,7},{7,6},{8,9},{9,8},{10,11... | collective-permute-start | bytes 8257544 | tf_op jit(solution)/shard_map/ppermute | solution.py:16
  153.4 1.8 copy-done.8
  155.2 1.8 copy-done.10
  157.0 4.2 %shard_map.111 = bf16[2688,512]{1,0:T(8,128)(2,1)S(1)} custom-call(bf16[2688,512]{1,0:T(8,128)(2,1)S(1)} %copy-done.8, bf16[2688,512]{1,0:T(8,128)(2,1)S(1)} %copy-done.10, bf16[512,512]{1,0:T(8,128)(2,1)S(1)} %pad_maximum_fusion.2.g_ref, bf16[512,512]{1,0:T(8,128)(2,1)S(1)} %copy-done.6), custom_call_target="tpu_custom_call" | custom-call | flops 2818572288 | bytes 12582912 | tf_op jit(solution)/shard_map/pallas_call | solution.py:285
  161.2 8.2 %collective-permute-start.28 = (bf16[1,168,512]{2,1,0:T(8,128)(2,1)S(1)}, bf16[1,168,512]{2,1,0:T(8,128)(2,1)S(1)}, u32[]{:S(2)}, u32[]{:S(2)}) collective-permute-start(bf16[1,168,512]{2,1,0:T(8,128)(2,1)S(1)} %get-tuple-element.92), channel_id=1, source_target_pairs={{0,56},{8,0},{16,8},{24,16},{32,24},{40,32},{48,40},{56,48},{1,57}... | collective-permute-start | bytes 516104 | tf_op jit(solution)/shard_map/ppermute | solution.py:16
  169.6 3.5 %collective-permute-done.28 = bf16[1,168,512]{2,1,0:T(8,128)(2,1)S(1)} collective-permute-done((bf16[1,168,512]{2,1,0:T(8,128)(2,1)S(1)}, bf16[1,168,512]{2,1,0:T(8,128)(2,1)S(1)}, u32[]{:S(2)}, u32[]{:S(2)}) %collective-permute-start.28) | collective-permute-done | bytes 172064 | tf_op jit(solution)/shard_map/ppermute | solution.py:16
  173.2 3.0 %collective-permute-done.27 = bf16[1,168,512]{2,1,0:T(8,128)(2,1)S(1)} collective-permute-done((bf16[1,168,512]{2,1,0:T(8,128)(2,1)S(1)}, bf16[1,168,512]{2,1,0:T(8,128)(2,1)S(1)}, u32[]{:S(2)}, u32[]{:S(2)}) %collective-permute-start.27) | collective-permute-done | bytes 172064 | tf_op jit(solution)/shard_map/ppermute | solution.py:16
  176.3 4.0 %shard_map.110 = (f32[1344,512]{1,0:T(8,128)S(1)}, bf16[1344,1024]{1,0:T(8,128)(2,1)S(1)}) custom-call(s32[1]{0:T(128)} %bitcast.1.where, bf16[2688,512]{1,0:T(8,128)(2,1)S(1)} %bitcast.106, bf16[512,512]{1,0:T(8,128)(2,1)S(1)} %pad_maximum_fusion.2.g_ref, bf16[512,512]{1,0:T(8,128)(2,1)S(1)} %copy-done.6, bf16[1344,1024]{1,0:T(8,128)(2,1)} %collective-permute-done.26.r_ref), custom_call_target="tpu_custom_call" | custom-call | flops 1409286144 | bytes 6291456 | tf_op jit(solution)/shard_map/pallas_call | solution.py:416
  180.3 1.5 copy-done.11
  181.8 1.7 fusion.15
  183.5 2.7 %collective-permute-start.34 = (bf16[2,168,512]{2,1,0:T(8,128)(2,1)S(1)}, bf16[2,168,512]{2,1,0:T(8,128)(2,1)S(1)}, u32[]{:S(2)}, u32[]{:S(2)}) collective-permute-start(bf16[2,168,512]{2,1,0:T(8,128)(2,1)S(1)} %pad_maximum_fusion.1), channel_id=1, source_target_pairs={{0,56},{8,0},{16,8},{24,16},{32,24},{40,32},{48,40},{56,48},{1,57}... | collective-permute-start | bytes 1032200 | tf_op jit(solution)/shard_map/ppermute | solution.py:16
  186.2 7.0 %collective-permute-done.31 = bf16[2,168,512]{2,1,0:T(8,128)(2,1)S(1)} collective-permute-done((bf16[2,168,512]{2,1,0:T(8,128)(2,1)S(1)}, bf16[2,168,512]{2,1,0:T(8,128)(2,1)S(1)}, u32[]{:S(2)}, u32[]{:S(2)}) %collective-permute-start.31) | collective-permute-done | bytes 344096 | tf_op jit(solution)/shard_map/ppermute | solution.py:16
  193.5 2.7 %collective-permute-start.35 = (bf16[2,168,512]{2,1,0:T(8,128)(2,1)S(1)}, bf16[2,168,512]{2,1,0:T(8,128)(2,1)S(1)}, u32[]{:S(2)}, u32[]{:S(2)}) collective-permute-start(bf16[2,168,512]{2,1,0:T(8,128)(2,1)S(1)} %get-tuple-element.89), channel_id=1, source_target_pairs={{0,56},{8,0},{16,8},{24,16},{32,24},{40,32},{48,40},{56,48},{1,57}... | collective-permute-start | bytes 1032200 | tf_op jit(solution)/shard_map/ppermute | solution.py:16
  196.2 6.1 %collective-permute-done.32 = bf16[2,168,512]{2,1,0:T(8,128)(2,1)S(1)} collective-permute-done((bf16[2,168,512]{2,1,0:T(8,128)(2,1)S(1)}, bf16[2,168,512]{2,1,0:T(8,128)(2,1)S(1)}, u32[]{:S(2)}, u32[]{:S(2)}) %collective-permute-start.32) | collective-permute-done | bytes 344096 | tf_op jit(solution)/shard_map/ppermute | solution.py:16
  202.6 2.7 %collective-permute-start.36 = (bf16[2,168,512]{2,1,0:T(8,128)(2,1)S(1)}, bf16[2,168,512]{2,1,0:T(8,128)(2,1)S(1)}, u32[]{:S(2)}, u32[]{:S(2)}) collective-permute-start(bf16[2,168,512]{2,1,0:T(8,128)(2,1)S(1)} %get-tuple-element.87), channel_id=1, source_target_pairs={{0,56},{8,0},{16,8},{24,16},{32,24},{40,32},{48,40},{56,48},{1,57}... | collective-permute-start | bytes 1032200 | tf_op jit(solution)/shard_map/ppermute | solution.py:16
  206.5 1.8 collective-permute-start.30
  208.3 2.2 collective-permute-done.33
  211.6 1.8 fusion.12
  213.4 2.6 %collective-permute-start.37 = (bf16[168,512]{1,0:T(8,128)(2,1)}, bf16[168,512]{1,0:T(8,128)(2,1)}, u32[]{:S(2)}, u32[]{:S(2)}) collective-permute-start(bf16[168,512]{1,0:T(8,128)(2,1)} %get-tuple-element.96), channel_id=1, source_target_pairs={{64,0},{0,64},{196,132},{132,196},{65,1},{1,65},{197,133},{133,197... | collective-permute-start | bytes 516104 | tf_op jit(solution)/shard_map/ppermute | solution.py:87
  218.6 1.6 collective-permute-done.37
  220.2 5.6 %collective-permute-done.38 = bf16[168,512]{1,0:T(8,128)(2,1)} collective-permute-done((bf16[168,512]{1,0:T(8,128)(2,1)}, bf16[168,512]{1,0:T(8,128)(2,1)}, u32[]{:S(2)}, u32[]{:S(2)}) %collective-permute-start.38) | collective-permute-done | bytes 172064 | tf_op jit(solution)/shard_map/ppermute | solution.py:87
  225.8 2.2 fusion.9
  228.0 1.8 reshape.124
  231.7 2.0 reshape.123
  233.7 3.7 %collective-permute-done.40 = bf16[84,512]{1,0:T(8,128)(2,1)S(1)} collective-permute-done((bf16[84,512]{1,0:T(8,128)(2,1)S(1)}, bf16[84,512]{1,0:T(8,128)(2,1)S(1)}, u32[]{:S(2)}, u32[]{:S(2)}) %collective-permute-start.40) | collective-permute-done | bytes 86048 | tf_op jit(solution)/shard_map/ppermute | solution.py:16
  239.6 3.9 %shard_map.112 = bf16[1344,512]{1,0:T(8,128)(2,1)} custom-call(s32[1]{0:T(128)} %bitcast.keep, f32[1344,512]{1,0:T(8,128)S(1)} %copy-done.12, bf16[1344,512]{1,0:T(8,128)(2,1)} %collective-permute-done.29.first_ref, bf16[1344,512]{1,0:T(8,128)(2,1)} %collective-permute-done.30.second_ref), custom_call_target="tpu_custom_call" | custom-call | flops 2752512 | bytes 6881280 | tf_op jit(solution)/shard_map/pallas_call | solution.py:438
  (141 shorter events, 27.3 us)
Async XLA Ops:
  1.4 6.6 %collective-permute-start = (bf16[84,512]{1,0:T(8,128)(2,1)S(1)}, bf16[84,512]{1,0:T(8,128)(2,1)S(1)}, u32[]{:S(2)}, u32[]{:S(2)}) collective-permute-start(bf16[84,512]{1,0:T(8,128)(2,1)S(1)} %pad_maximum_fusion.7), channel_id=1, source_target_pairs={{0,4},{4,0},{1,5},{5,1},{2,6},{6,2},{3,7},{7,3},{8,12},{12,8},{9,1... | collective-permute-start | bytes 258056 | tf_op jit(solution)/shard_map/ppermute | solution.py:16
  3.6 2.6 %copy-start = (bf16[512,5376]{1,0:T(8,128)(2,1)S(1)}, bf16[512,5376]{1,0:T(8,128)(2,1)}, u32[]{:S(2)}) copy-start(bf16[512,5376]{1,0:T(8,128)(2,1)} %x_ref.5) | copy-start | bytes 16515076
  8.0 37.0 %collective-permute-start.12 = (bf16[256,2688]{1,0:T(8,128)(2,1)}, bf16[256,2688]{1,0:T(8,128)(2,1)}, u32[]{:S(2)}, u32[]{:S(2)}) collective-permute-start(bf16[256,2688]{1,0:T(8,128)(2,1)} %shard_map.103), channel_id=1, source_target_pairs={{0,4},{4,0},{1,5},{5,1},{2,6},{6,2},{3,7},{7,3},{8,12},{12,8},{9,1... | collective-permute-start | bytes 4128776 | tf_op jit(solution)/shard_map/ppermute | solution.py:16
  8.1 8.7 %collective-permute-start.1 = (bf16[168,512]{1,0:T(8,128)(2,1)S(1)}, bf16[168,512]{1,0:T(8,128)(2,1)S(1)}, u32[]{:S(2)}, u32[]{:S(2)}) collective-permute-start(bf16[168,512]{1,0:T(8,128)(2,1)S(1)} %maximum_select_fusion.1), channel_id=1, source_target_pairs={{0,128},{64,192},{132,4},{196,68},{1,129},{65,193},{133,5},{197,69... | collective-permute-start | bytes 516104 | tf_op jit(solution)/shard_map/ppermute | solution.py:87
  13.2 7.8 %collective-permute-start.2 = (bf16[168,512]{1,0:T(8,128)(2,1)S(1)}, bf16[168,512]{1,0:T(8,128)(2,1)S(1)}, u32[]{:S(2)}, u32[]{:S(2)}) collective-permute-start(bf16[168,512]{1,0:T(8,128)(2,1)S(1)} %maximum_select_fusion.1), channel_id=1, source_target_pairs={{0,64},{64,0},{132,196},{196,132},{1,65},{65,1},{133,197},{197,133... | collective-permute-start | bytes 516104 | tf_op jit(solution)/shard_map/ppermute | solution.py:87
  15.5 5.5 %collective-permute-start.3 = (bf16[168,512]{1,0:T(8,128)(2,1)S(1)}, bf16[168,512]{1,0:T(8,128)(2,1)S(1)}, u32[]{:S(2)}, u32[]{:S(2)}) collective-permute-start(bf16[168,512]{1,0:T(8,128)(2,1)S(1)} %maximum_select_fusion.1), channel_id=1, source_target_pairs={{0,192},{64,128},{132,68},{196,4},{1,193},{65,129},{133,69},{197,5... | collective-permute-start | bytes 516104 | tf_op jit(solution)/shard_map/ppermute | solution.py:87
  21.1 12.5 %collective-permute-start.4 = (bf16[2,168,512]{2,1,0:T(8,128)(2,1)S(1)}, bf16[2,168,512]{2,1,0:T(8,128)(2,1)S(1)}, u32[]{:S(2)}, u32[]{:S(2)}) collective-permute-start(bf16[2,168,512]{2,1,0:T(8,128)(2,1)S(1)} %pad_maximum_fusion.4), channel_id=1, source_target_pairs={{0,8},{8,16},{16,24},{24,32},{32,40},{40,48},{48,56},{56,0},{1,9},... | collective-permute-start | bytes 1032200 | tf_op jit(solution)/shard_map/ppermute | solution.py:16
  22.8 10.8 %collective-permute-start.5 = (bf16[2,168,512]{2,1,0:T(8,128)(2,1)S(1)}, bf16[2,168,512]{2,1,0:T(8,128)(2,1)}, u32[]{:S(2)}, u32[]{:S(2)}) collective-permute-start(bf16[2,168,512]{2,1,0:T(8,128)(2,1)S(1)} %pad_maximum_fusion.4), channel_id=1, source_target_pairs={{0,56},{8,0},{16,8},{24,16},{32,24},{40,32},{48,40},{56,48},{1,57}... | collective-permute-start | bytes 1032200 | tf_op jit(solution)/shard_map/ppermute | solution.py:16
  26.8 2.6 %copy-start.1 = (bf16[512,5376]{1,0:T(8,128)(2,1)S(1)}, bf16[512,5376]{1,0:T(8,128)(2,1)}, u32[]{:S(2)}) copy-start(bf16[512,5376]{1,0:T(8,128)(2,1)} %x_ref.5) | copy-start | bytes 16515076
  30.9 1.5 copy-start.7
  33.6 8.7 %collective-permute-start.6 = (bf16[2,168,512]{2,1,0:T(8,128)(2,1)S(1)}, bf16[2,168,512]{2,1,0:T(8,128)(2,1)S(1)}, u32[]{:S(2)}, u32[]{:S(2)}) collective-permute-start(bf16[2,168,512]{2,1,0:T(8,128)(2,1)S(1)} %collective-permute-done.4), channel_id=1, source_target_pairs={{0,8},{8,16},{16,24},{24,32},{32,40},{40,48},{48,56},{56,0},{1,9},... | collective-permute-start | bytes 1032200 | tf_op jit(solution)/shard_map/ppermute | solution.py:16
  33.6 8.7 %collective-permute-start.7 = (bf16[2,168,512]{2,1,0:T(8,128)(2,1)}, bf16[2,168,512]{2,1,0:T(8,128)(2,1)S(1)}, u32[]{:S(2)}, u32[]{:S(2)}) collective-permute-start(bf16[2,168,512]{2,1,0:T(8,128)(2,1)} %collective-permute-done.5), channel_id=1, source_target_pairs={{0,56},{8,0},{16,8},{24,16},{32,24},{40,32},{48,40},{56,48},{1,57}... | collective-permute-start | bytes 1032200 | tf_op jit(solution)/shard_map/ppermute | solution.py:16
  42.3 7.8 %collective-permute-start.8 = (bf16[2,168,512]{2,1,0:T(8,128)(2,1)S(1)}, bf16[2,168,512]{2,1,0:T(8,128)(2,1)S(1)}, u32[]{:S(2)}, u32[]{:S(2)}) collective-permute-start(bf16[2,168,512]{2,1,0:T(8,128)(2,1)S(1)} %collective-permute-done.6), channel_id=1, source_target_pairs={{0,8},{8,16},{16,24},{24,32},{32,40},{40,48},{48,56},{56,0},{1,9},... | collective-permute-start | bytes 1032200 | tf_op jit(solution)/shard_map/ppermute | solution.py:16
  42.3 7.9 %collective-permute-start.9 = (bf16[2,168,512]{2,1,0:T(8,128)(2,1)S(1)}, bf16[2,168,512]{2,1,0:T(8,128)(2,1)S(1)}, u32[]{:S(2)}, u32[]{:S(2)}) collective-permute-start(bf16[2,168,512]{2,1,0:T(8,128)(2,1)S(1)} %collective-permute-done.7), channel_id=1, source_target_pairs={{0,56},{8,0},{16,8},{24,16},{32,24},{40,32},{48,40},{56,48},{1,57}... | collective-permute-start | bytes 1032200 | tf_op jit(solution)/shard_map/ppermute | solution.py:16
  45.0 10.8 %collective-permute-start.13 = (bf16[256,2688]{1,0:T(8,128)(2,1)}, bf16[256,2688]{1,0:T(8,128)(2,1)S(1)}, u32[]{:S(2)}, u32[]{:S(2)}) collective-permute-start(bf16[256,2688]{1,0:T(8,128)(2,1)} %collective-permute-done.12), channel_id=1, source_target_pairs={{0,1},{1,0},{2,3},{3,2},{4,5},{5,4},{6,7},{7,6},{8,9},{9,8},{10,11... | collective-permute-start | bytes 4128776 | tf_op jit(solution)/shard_map/ppermute | solution.py:16
  50.1 5.5 %collective-permute-start.10 = (bf16[1,168,512]{2,1,0:T(8,128)(2,1)S(1)}, bf16[1,168,512]{2,1,0:T(8,128)(2,1)S(1)}, u32[]{:S(2)}, u32[]{:S(2)}) collective-permute-start(bf16[1,168,512]{2,1,0:T(8,128)(2,1)S(1)} %slice.187), channel_id=1, source_target_pairs={{0,8},{8,16},{16,24},{24,32},{32,40},{40,48},{48,56},{56,0},{1,9},... | collective-permute-start | bytes 516104 | tf_op jit(solution)/shard_map/ppermute | solution.py:16
  50.2 5.4 %collective-permute-start.11 = (bf16[1,168,512]{2,1,0:T(8,128)(2,1)S(1)}, bf16[1,168,512]{2,1,0:T(8,128)(2,1)S(1)}, u32[]{:S(2)}, u32[]{:S(2)}) collective-permute-start(bf16[1,168,512]{2,1,0:T(8,128)(2,1)S(1)} %slice.188), channel_id=1, source_target_pairs={{0,56},{8,0},{16,8},{24,16},{32,24},{40,32},{48,40},{56,48},{1,57}... | collective-permute-start | bytes 516104 | tf_op jit(solution)/shard_map/ppermute | solution.py:16
  58.2 6.3 %copy-start.3 = (bf16[512,2688]{1,0:T(8,128)(2,1)}, bf16[512,2688]{1,0:T(8,128)(2,1)S(1)}, u32[]{:S(2)}) copy-start(bf16[512,2688]{1,0:T(8,128)(2,1)S(1)} %maximum_select_fusion.x_ref) | copy-start | bytes 8257540
  58.3 6.3 %copy-start.17 = (s32[512]{0:T(512)S(1)}, s32[512]{0:T(512)}, u32[]{:S(2)}) copy-start(s32[512]{0:T(512)} %param.12) | copy-start | bytes 6148
  64.6 12.4 %collective-permute-start.14 = (f32[512,256]{1,0:T(8,128)S(1)}, f32[512,256]{1,0:T(8,128)}, u32[]{:S(2)}, u32[]{:S(2)}) collective-permute-start(f32[512,256]{1,0:T(8,128)S(1)} %get-tuple-element.57), channel_id=1, source_target_pairs={{0,4},{4,0},{1,5},{5,1},{2,6},{6,2},{3,7},{7,3},{8,12},{12,8},{9,1... | collective-permute-start | bytes 1572872 | tf_op jit(solution)/shard_map/ppermute | solution.py:16
  65.7 2.6 %copy-start.2 = (bf16[512,5376]{1,0:T(8,128)(2,1)S(1)}, bf16[512,5376]{1,0:T(8,128)(2,1)}, u32[]{:S(2)}) copy-start(bf16[512,5376]{1,0:T(8,128)(2,1)} %x_ref.5) | copy-start | bytes 16515076
  68.3 5.6 %copy-start.4 = (bf16[512,2688]{1,0:T(8,128)(2,1)S(1)}, bf16[512,2688]{1,0:T(8,128)(2,1)}, u32[]{:S(2)}) copy-start(bf16[512,2688]{1,0:T(8,128)(2,1)} %copy-done.3) | copy-start | bytes 8257540
  73.9 4.5 %copy-start.16 = (f32[128]{0:T(128)S(1)}, f32[128]{0:T(128)}, u32[]{:S(2)}) copy-start(f32[128]{0:T(128)} %param.15) | copy-start | bytes 1540
  75.4 1.6 copy-start.9
  77.0 8.7 %copy-start.15 = (bf16[512,4,128]{2,1,0:T(4,128)(2,1)S(1)}, bf16[512,4,128]{2,1,0:T(4,128)(2,1)}, u32[]{:S(2)}) copy-start(bf16[512,4,128]{2,1,0:T(4,128)(2,1)} %param.10) | copy-start | bytes 1572868
  78.5 8.6 %collective-permute-start.15 = (bf16[528,256]{1,0:T(8,128)(2,1)S(1)}, bf16[528,256]{1,0:T(8,128)(2,1)S(1)}, u32[]{:S(2)}, u32[]{:S(2)}) collective-permute-start(bf16[528,256]{1,0:T(8,128)(2,1)S(1)} %fusion.10.own_ref), channel_id=1, source_target_pairs={{0,8},{4,12},{8,16},{12,20},{16,24},{20,28},{24,32},{28,36},{32,40... | collective-permute-start | bytes 811016 | tf_op jit(solution)/shard_map/ppermute | solution.py:22
  82.2 6.7 %collective-permute-start.16 = (bf16[528,256]{1,0:T(8,128)(2,1)S(1)}, bf16[528,256]{1,0:T(8,128)(2,1)S(1)}, u32[]{:S(2)}, u32[]{:S(2)}) collective-permute-start(bf16[528,256]{1,0:T(8,128)(2,1)S(1)} %fusion.10.own_ref), channel_id=1, source_target_pairs={{0,4},{4,8},{8,12},{12,16},{16,20},{20,24},{24,28},{28,32},{32,36}... | collective-permute-start | bytes 811016 | tf_op jit(solution)/shard_map/ppermute | solution.py:22
  85.8 12.6 %collective-permute-start.19 = (f32[512,256]{1,0:T(8,128)}, f32[512,256]{1,0:T(8,128)S(1)}, u32[]{:S(2)}, u32[]{:S(2)}) collective-permute-start(f32[512,256]{1,0:T(8,128)} %get-tuple-element.68), channel_id=1, source_target_pairs={{0,4},{4,0},{1,5},{5,1},{2,6},{6,2},{3,7},{7,3},{8,12},{12,8},{9,1... | collective-permute-start | bytes 1572872 | tf_op jit(solution)/shard_map/ppermute | solution.py:16
  95.6 12.6 %collective-permute-start.17 = (bf16[512,256]{1,0:T(8,128)(2,1)S(1)}, bf16[512,256]{1,0:T(8,128)(2,1)S(1)}, u32[]{:S(2)}, u32[]{:S(2)}) collective-permute-start(bf16[512,256]{1,0:T(8,128)(2,1)S(1)} %get-tuple-element.102), channel_id=1, source_target_pairs={{4,0},{8,4},{12,8},{16,12},{20,16},{24,20},{28,24},{32,28},{36,32}... | collective-permute-start | bytes 786440 | tf_op jit(solution)/shard_map/ppermute | solution.py:22
  96.9 11.3 %collective-permute-start.18 = (bf16[512,256]{1,0:T(8,128)(2,1)S(1)}, bf16[512,256]{1,0:T(8,128)(2,1)S(1)}, u32[]{:S(2)}, u32[]{:S(2)}) collective-permute-start(bf16[512,256]{1,0:T(8,128)(2,1)S(1)} %get-tuple-element.103), channel_id=1, source_target_pairs={{8,0},{12,4},{16,8},{20,12},{24,16},{28,20},{32,24},{36,28},{40,32... | collective-permute-start | bytes 786440 | tf_op jit(solution)/shard_map/ppermute | solution.py:22
  98.8 9.8 %collective-permute-start.20 = (bf16[528,256]{1,0:T(8,128)(2,1)S(1)}, bf16[528,256]{1,0:T(8,128)(2,1)S(1)}, u32[]{:S(2)}, u32[]{:S(2)}) collective-permute-start(bf16[528,256]{1,0:T(8,128)(2,1)S(1)} %fusion.11.own_ref), channel_id=1, source_target_pairs={{0,8},{4,12},{8,16},{12,20},{16,24},{20,28},{24,32},{28,36},{32,40... | collective-permute-start | bytes 811016 | tf_op jit(solution)/shard_map/ppermute | solution.py:22
  104.9 9.5 %collective-permute-start.21 = (bf16[528,256]{1,0:T(8,128)(2,1)S(1)}, bf16[528,256]{1,0:T(8,128)(2,1)S(1)}, u32[]{:S(2)}, u32[]{:S(2)}) collective-permute-start(bf16[528,256]{1,0:T(8,128)(2,1)S(1)} %fusion.11.own_ref), channel_id=1, source_target_pairs={{0,4},{4,8},{8,12},{12,16},{16,20},{20,24},{24,28},{28,32},{32,36}... | collective-permute-start | bytes 811016 | tf_op jit(solution)/shard_map/ppermute | solution.py:22
  121.1 12.5 %copy-start.13 = (bf16[512,256]{1,0:T(8,128)(2,1)}, bf16[512,256]{1,0:T(8,128)(2,1)S(1)}, u32[]{:S(2)}) copy-start(bf16[512,256]{1,0:T(8,128)(2,1)S(1)} %get-tuple-element.83) | copy-start | bytes 786436
  121.1 10.4 %collective-permute-start.22 = (bf16[512,256]{1,0:T(8,128)(2,1)S(1)}, bf16[512,256]{1,0:T(8,128)(2,1)S(1)}, u32[]{:S(2)}, u32[]{:S(2)}) collective-permute-start(bf16[512,256]{1,0:T(8,128)(2,1)S(1)} %get-tuple-element.100), channel_id=1, source_target_pairs={{4,0},{8,4},{12,8},{16,12},{20,16},{24,20},{28,24},{32,28},{36,32}... | collective-permute-start | bytes 786440 | tf_op jit(solution)/shard_map/ppermute | solution.py:22
  122.4 10.5 %collective-permute-start.23 = (bf16[512,256]{1,0:T(8,128)(2,1)S(1)}, bf16[512,256]{1,0:T(8,128)(2,1)S(1)}, u32[]{:S(2)}, u32[]{:S(2)}) collective-permute-start(bf16[512,256]{1,0:T(8,128)(2,1)S(1)} %get-tuple-element.101), channel_id=1, source_target_pairs={{8,0},{12,4},{16,8},{20,12},{24,16},{28,20},{32,24},{36,28},{40,32... | collective-permute-start | bytes 786440 | tf_op jit(solution)/shard_map/ppermute | solution.py:22
  124.0 11.5 %collective-permute-start.24 = (bf16[512,256]{1,0:T(8,128)(2,1)S(1)}, bf16[512,256]{1,0:T(8,128)(2,1)S(1)}, u32[]{:S(2)}, u32[]{:S(2)}) collective-permute-start(bf16[512,256]{1,0:T(8,128)(2,1)S(1)} %pad_maximum_fusion.5), channel_id=1, source_target_pairs={{0,4},{4,0},{1,5},{5,1},{2,6},{6,2},{3,7},{7,3},{8,12},{12,8},{9,1... | collective-permute-start | bytes 786440 | tf_op jit(solution)/shard_map/ppermute | solution.py:16
  133.5 8.4 %collective-permute-start.25 = (bf16[512,256]{1,0:T(8,128)(2,1)S(1)}, bf16[512,256]{1,0:T(8,128)(2,1)S(1)}, u32[]{:S(2)}, u32[]{:S(2)}) collective-permute-start(bf16[512,256]{1,0:T(8,128)(2,1)S(1)} %pad_maximum_fusion.6), channel_id=1, source_target_pairs={{0,4},{4,0},{1,5},{5,1},{2,6},{6,2},{3,7},{7,3},{8,12},{12,8},{9,1... | collective-permute-start | bytes 786440 | tf_op jit(solution)/shard_map/ppermute | solution.py:16
  142.0 3.5 %copy-start.5 = (bf16[512,512]{1,0:T(8,128)(2,1)}, bf16[512,512]{1,0:T(8,128)(2,1)S(1)}, u32[]{:S(2)}) copy-start(bf16[512,512]{1,0:T(8,128)(2,1)S(1)} %constant_dynamic-update-slice_fusion.h_ref) | copy-start | bytes 1572868
  145.5 30.9 %collective-permute-start.26 = (bf16[1344,1024]{1,0:T(8,128)(2,1)}, bf16[1344,1024]{1,0:T(8,128)(2,1)}, u32[]{:S(2)}, u32[]{:S(2)}) collective-permute-start(bf16[1344,1024]{1,0:T(8,128)(2,1)} %shard_map.109), channel_id=1, source_target_pairs={{0,1},{1,0},{2,3},{3,2},{4,5},{5,4},{6,7},{7,6},{8,9},{9,8},{10,11... | collective-permute-start | bytes 8257544 | tf_op jit(solution)/shard_map/ppermute | solution.py:16
  152.4 1.0 copy-start.6
  153.4 1.8 copy-start.8
  155.2 1.8 copy-start.10
  161.2 11.9 %collective-permute-start.28 = (bf16[1,168,512]{2,1,0:T(8,128)(2,1)S(1)}, bf16[1,168,512]{2,1,0:T(8,128)(2,1)S(1)}, u32[]{:S(2)}, u32[]{:S(2)}) collective-permute-start(bf16[1,168,512]{2,1,0:T(8,128)(2,1)S(1)} %get-tuple-element.92), channel_id=1, source_target_pairs={{0,56},{8,0},{16,8},{24,16},{32,24},{40,32},{48,40},{56,48},{1,57}... | collective-permute-start | bytes 516104 | tf_op jit(solution)/shard_map/ppermute | solution.py:16
  169.4 6.9 %collective-permute-start.27 = (bf16[1,168,512]{2,1,0:T(8,128)(2,1)S(1)}, bf16[1,168,512]{2,1,0:T(8,128)(2,1)S(1)}, u32[]{:S(2)}, u32[]{:S(2)}) collective-permute-start(bf16[1,168,512]{2,1,0:T(8,128)(2,1)S(1)} %get-tuple-element.93), channel_id=1, source_target_pairs={{0,8},{8,16},{16,24},{24,32},{32,40},{40,48},{48,56},{56,0},{1,9},... | collective-permute-start | bytes 516104 | tf_op jit(solution)/shard_map/ppermute | solution.py:16
  180.3 1.5 copy-start.11
  183.5 9.7 %collective-permute-start.31 = (bf16[2,168,512]{2,1,0:T(8,128)(2,1)S(1)}, bf16[2,168,512]{2,1,0:T(8,128)(2,1)S(1)}, u32[]{:S(2)}, u32[]{:S(2)}) collective-permute-start(bf16[2,168,512]{2,1,0:T(8,128)(2,1)S(1)} %pad_maximum_fusion), channel_id=1, source_target_pairs={{0,8},{8,16},{16,24},{24,32},{32,40},{40,48},{48,56},{56,0},{1,9},... | collective-permute-start | bytes 1032200 | tf_op jit(solution)/shard_map/ppermute | solution.py:16
  183.5 9.7 %collective-permute-start.34 = (bf16[2,168,512]{2,1,0:T(8,128)(2,1)S(1)}, bf16[2,168,512]{2,1,0:T(8,128)(2,1)S(1)}, u32[]{:S(2)}, u32[]{:S(2)}) collective-permute-start(bf16[2,168,512]{2,1,0:T(8,128)(2,1)S(1)} %pad_maximum_fusion.1), channel_id=1, source_target_pairs={{0,56},{8,0},{16,8},{24,16},{32,24},{40,32},{48,40},{56,48},{1,57}... | collective-permute-start | bytes 1032200 | tf_op jit(solution)/shard_map/ppermute | solution.py:16
  193.4 8.9 %collective-permute-start.32 = (bf16[2,168,512]{2,1,0:T(8,128)(2,1)S(1)}, bf16[2,168,512]{2,1,0:T(8,128)(2,1)S(1)}, u32[]{:S(2)}, u32[]{:S(2)}) collective-permute-start(bf16[2,168,512]{2,1,0:T(8,128)(2,1)S(1)} %get-tuple-element.88), channel_id=1, source_target_pairs={{0,8},{8,16},{16,24},{24,32},{32,40},{40,48},{48,56},{56,0},{1,9},... | collective-permute-start | bytes 1032200 | tf_op jit(solution)/shard_map/ppermute | solution.py:16
  193.5 8.8 %collective-permute-start.35 = (bf16[2,168,512]{2,1,0:T(8,128)(2,1)S(1)}, bf16[2,168,512]{2,1,0:T(8,128)(2,1)S(1)}, u32[]{:S(2)}, u32[]{:S(2)}) collective-permute-start(bf16[2,168,512]{2,1,0:T(8,128)(2,1)S(1)} %get-tuple-element.89), channel_id=1, source_target_pairs={{0,56},{8,0},{16,8},{24,16},{32,24},{40,32},{48,40},{56,48},{1,57}... | collective-permute-start | bytes 1032200 | tf_op jit(solution)/shard_map/ppermute | solution.py:16
  202.5 28.3 %copy-start.14 = (bf16[512,256]{1,0:T(8,128)(2,1)S(1)}, bf16[512,256]{1,0:T(8,128)(2,1)}, u32[]{:S(2)}) copy-start(bf16[512,256]{1,0:T(8,128)(2,1)} %copy-done.13) | copy-start | bytes 786436
  202.5 8.0 %collective-permute-start.33 = (bf16[2,168,512]{2,1,0:T(8,128)(2,1)S(1)}, bf16[2,168,512]{2,1,0:T(8,128)(2,1)S(1)}, u32[]{:S(2)}, u32[]{:S(2)}) collective-permute-start(bf16[2,168,512]{2,1,0:T(8,128)(2,1)S(1)} %get-tuple-element.86), channel_id=1, source_target_pairs={{0,8},{8,16},{16,24},{24,32},{32,40},{40,48},{48,56},{56,0},{1,9},... | collective-permute-start | bytes 1032200 | tf_op jit(solution)/shard_map/ppermute | solution.py:16
  202.6 8.0 %collective-permute-start.36 = (bf16[2,168,512]{2,1,0:T(8,128)(2,1)S(1)}, bf16[2,168,512]{2,1,0:T(8,128)(2,1)S(1)}, u32[]{:S(2)}, u32[]{:S(2)}) collective-permute-start(bf16[2,168,512]{2,1,0:T(8,128)(2,1)S(1)} %get-tuple-element.87), channel_id=1, source_target_pairs={{0,56},{8,0},{16,8},{24,16},{32,24},{40,32},{48,40},{56,48},{1,57}... | collective-permute-start | bytes 1032200 | tf_op jit(solution)/shard_map/ppermute | solution.py:16
  205.3 34.3 %collective-permute-start.29 = (bf16[1344,512]{1,0:T(8,128)(2,1)}, bf16[1344,512]{1,0:T(8,128)(2,1)}, u32[]{:S(2)}, u32[]{:S(2)}) collective-permute-start(bf16[1344,512]{1,0:T(8,128)(2,1)} %get-tuple-element.80), channel_id=1, source_target_pairs={{0,4},{6,2},{2,0},{4,6},{1,5},{7,3},{3,1},{5,7},{8,12},{14,10},{10... | collective-permute-start | bytes 4128776 | tf_op jit(solution)/shard_map/ppermute | solution.py:564
  206.5 33.1 %collective-permute-start.30 = (bf16[1344,512]{1,0:T(8,128)(2,1)}, bf16[1344,512]{1,0:T(8,128)(2,1)}, u32[]{:S(2)}, u32[]{:S(2)}) collective-permute-start(bf16[1344,512]{1,0:T(8,128)(2,1)} %get-tuple-element.81), channel_id=1, source_target_pairs={{2,4},{4,2},{3,5},{5,3},{10,12},{12,10},{11,13},{13,11},{18,20},{2... | collective-permute-start | bytes 4128776 | tf_op jit(solution)/shard_map/ppermute | solution.py:565
  213.4 6.8 %collective-permute-start.37 = (bf16[168,512]{1,0:T(8,128)(2,1)}, bf16[168,512]{1,0:T(8,128)(2,1)}, u32[]{:S(2)}, u32[]{:S(2)}) collective-permute-start(bf16[168,512]{1,0:T(8,128)(2,1)} %get-tuple-element.96), channel_id=1, source_target_pairs={{64,0},{0,64},{196,132},{132,196},{65,1},{1,65},{197,133},{133,197... | collective-permute-start | bytes 516104 | tf_op jit(solution)/shard_map/ppermute | solution.py:87
  216.0 9.8 %collective-permute-start.38 = (bf16[168,512]{1,0:T(8,128)(2,1)}, bf16[168,512]{1,0:T(8,128)(2,1)}, u32[]{:S(2)}, u32[]{:S(2)}) collective-permute-start(bf16[168,512]{1,0:T(8,128)(2,1)} %get-tuple-element.96), channel_id=1, source_target_pairs={{192,0},{128,64},{68,132},{4,196},{193,1},{129,65},{69,133},{5,197... | collective-permute-start | bytes 516104 | tf_op jit(solution)/shard_map/ppermute | solution.py:87
  217.3 8.5 %collective-permute-start.39 = (bf16[168,512]{1,0:T(8,128)(2,1)S(1)}, bf16[168,512]{1,0:T(8,128)(2,1)}, u32[]{:S(2)}, u32[]{:S(2)}) collective-permute-start(bf16[168,512]{1,0:T(8,128)(2,1)S(1)} %get-tuple-element.97), channel_id=1, source_target_pairs={{128,0},{192,64},{4,132},{68,196},{129,1},{193,65},{5,133},{69,197... | collective-permute-start | bytes 516104 | tf_op jit(solution)/shard_map/ppermute | solution.py:87
  218.6 21.0 %copy-start.12 = (f32[1344,512]{1,0:T(8,128)S(1)}, f32[1344,512]{1,0:T(8,128)}, u32[]{:S(2)}) copy-start(f32[1344,512]{1,0:T(8,128)} %copy-done.11) | copy-start | bytes 8257540
  230.7 6.6 %collective-permute-start.40 = (bf16[84,512]{1,0:T(8,128)(2,1)S(1)}, bf16[84,512]{1,0:T(8,128)(2,1)S(1)}, u32[]{:S(2)}, u32[]{:S(2)}) collective-permute-start(bf16[84,512]{1,0:T(8,128)(2,1)S(1)} %fusion.13), channel_id=1, source_target_pairs={{0,4},{4,0},{1,5},{5,1},{2,6},{6,2},{3,7},{7,3},{8,12},{12,8},{9,1... | collective-permute-start | bytes 258056 | tf_op jit(solution)/shard_map/ppermute | solution.py:16

commit v2 on v1

--- a/solution.py
+++ b/solution.py
@@ -544,6 +544,9 @@
     received = hop(far, "c", 2, 1)
 
     def between(t, ahead, behind):
+        if t == 4:
+            queries_out = jnp.concatenate(dqs, 1).reshape(tok, heads, hd)
+            ahead, behind, held["queries"] = lax.optimization_barrier((ahead, behind, queries_out))
         if t == 2:
             own_part, low = input_term(core_array, weight, own_grads, par_grads, received)
             first = jnp.where(keep, low[:, tok:], low[:, :tok])
@@ -559,7 +562,7 @@
     cols = [grad[:, i * hd : (i + 1) * hd] for i in range(2 * groups)]
     k_weight_grad = jnp.concatenate(cols[0::2], 1)
     v_weight_grad = jnp.concatenate(cols[1::2], 1)
-    query_grad = jnp.concatenate(dqs, 1).reshape(tok, heads, hd)
+    query_grad = held["queries"]
 
     first = lax.ppermute(held["first"], ("xl", "xh"), [(0, 2), (3, 1), (1, 0), (2, 3)])
     second = lax.ppermute(held["second"], ("xl", "xh"), [(1, 2), (2, 1)])

time: 247 us -> 248 us (level)
  waiting for transfers between devices: 69 us -> 73.7 us
    ppermute x25, waiting for transfers between devices: 44 us -> 48.8 us  [hop(): return lax.ppermute(block, axis, [(i, (i + step) % n) for i in range(n)])]
    unnamed x39 -> x45, local copies, waits for them, and re-layouts: 18.1 us -> 18.9 us
  transfers between devices with their start and end apart: 41 -> 41, of which waited for: 20 -> 20; matrix products, arithmetic and copies ran while one was open for 7% -> 5% of each run, Pallas kernels for 9% -> 9%
where the time goes in v2:
time: 248 us; the launch traced here: 244 us
  starting transfers between devices  85.8 us (35%)
  waiting for transfers between devices  73.7 us (30%)
  Pallas kernels  44.9 us (18%)
  local copies, waits for them, and re-layouts  23.5 us (9%)
  other arithmetic  14.4 us (6%)
    ppermute x25, waiting for transfers between devices, hop(): return lax.ppermute(block, axis, [(i, (i + step) % n) for i in range(n)])  48.8 us
    ppermute x25, starting transfers between devices, hop(): return lax.ppermute(block, axis, [(i, (i + step) % n) for i in range(n)])  47.3 us
    ppermute x8, starting transfers between devices, seq_shift(): return lax.ppermute(block, ('y', 'z', 'xl'), route)  21.8 us
    unnamed x45, local copies, waits for them, and re-layouts  18.9 us
    ppermute x6, starting transfers between devices, y_route(): lax.ppermute(block, ('y', 'xl'), [(b, a) for a, b in pairs] if back else...  13.8 us
    ppermute x8, waiting for transfers between devices, seq_shift(): return lax.ppermute(block, ('y', 'z', 'xl'), route)  13.6 us
    pallas_call x2, Pallas kernels, attention(): pl.pallas_call(attention_kernel, grid=(tok // QB,), in_specs=[whole] * 6,...  13.4 us
    ppermute x6, waiting for transfers between devices, y_route(): lax.ppermute(block, ('y', 'xl'), [(b, a) for a, b in pairs] if back else...  11.4 us
  transfers between devices with their start and end apart: 41, of which 20 were waited for; matrix products, arithmetic and copies ran while one was open for 5% of the time, Pallas kernels for 9%

profile of v2, /device:TPU:1, one launch (start us, length us, event | category | flops | bytes accessed | tf_op | source)
XLA Modules:
  0.0 243.8 jit_solution(398769345749283674)
XLA Ops:
  1.4 2.1 collective-permute-start
  3.6 2.6 %copy-done = bf16[512,5376]{1,0:T(8,128)(2,1)S(1)} copy-done((bf16[512,5376]{1,0:T(8,128)(2,1)S(1)}, bf16[512,5376]{1,0:T(8,128)(2,1)}, u32[]{:S(2)}) %copy-start) | copy-done | bytes 5505048
  6.2 1.8 shard_map.103
  8.1 5.1 %collective-permute-start.1 = (bf16[168,512]{1,0:T(8,128)(2,1)S(1)}, bf16[168,512]{1,0:T(8,128)(2,1)S(1)}, u32[]{:S(2)}, u32[]{:S(2)}) collective-permute-start(bf16[168,512]{1,0:T(8,128)(2,1)S(1)} %maximum_select_fusion.1), channel_id=1, source_target_pairs={{0,128},{64,192},{132,4},{196,68},{1,129},{65,193},{133,5},{197,69... | collective-permute-start | bytes 516104 | tf_op jit(solution)/shard_map/ppermute | solution.py:87
  13.2 2.3 collective-permute-start.2
  15.5 1.3 collective-permute-start.3
  16.8 4.2 %collective-permute-done.2 = bf16[168,512]{1,0:T(8,128)(2,1)S(1)} collective-permute-done((bf16[168,512]{1,0:T(8,128)(2,1)S(1)}, bf16[168,512]{1,0:T(8,128)(2,1)S(1)}, u32[]{:S(2)}, u32[]{:S(2)}) %collective-permute-start.2) | collective-permute-done | bytes 172064 | tf_op jit(solution)/shard_map/ppermute | solution.py:87
  21.1 1.7 collective-permute-start.4
  22.8 4.0 %collective-permute-start.5 = (bf16[2,168,512]{2,1,0:T(8,128)(2,1)S(1)}, bf16[2,168,512]{2,1,0:T(8,128)(2,1)}, u32[]{:S(2)}, u32[]{:S(2)}) collective-permute-start(bf16[2,168,512]{2,1,0:T(8,128)(2,1)S(1)} %pad_maximum_fusion.4), channel_id=1, source_target_pairs={{0,56},{8,0},{16,8},{24,16},{32,24},{40,32},{48,40},{56,48},{1,57}... | collective-permute-start | bytes 1032200 | tf_op jit(solution)/shard_map/ppermute | solution.py:16
  26.8 2.6 %copy-done.1 = bf16[512,5376]{1,0:T(8,128)(2,1)S(1)} copy-done((bf16[512,5376]{1,0:T(8,128)(2,1)S(1)}, bf16[512,5376]{1,0:T(8,128)(2,1)}, u32[]{:S(2)}) %copy-start.1) | copy-done | bytes 5505048
  29.4 1.5 shard_map.102.own_ref
  30.9 1.5 copy-done.8
  33.6 2.7 %collective-permute-start.7 = (bf16[2,168,512]{2,1,0:T(8,128)(2,1)}, bf16[2,168,512]{2,1,0:T(8,128)(2,1)S(1)}, u32[]{:S(2)}, u32[]{:S(2)}) collective-permute-start(bf16[2,168,512]{2,1,0:T(8,128)(2,1)} %collective-permute-done.5), channel_id=1, source_target_pairs={{0,56},{8,0},{16,8},{24,16},{32,24},{40,32},{48,40},{56,48},{1,57}... | collective-permute-start | bytes 1032200 | tf_op jit(solution)/shard_map/ppermute | solution.py:16
  37.4 4.9 %collective-permute-done.6 = bf16[2,168,512]{2,1,0:T(8,128)(2,1)S(1)} collective-permute-done((bf16[2,168,512]{2,1,0:T(8,128)(2,1)S(1)}, bf16[2,168,512]{2,1,0:T(8,128)(2,1)S(1)}, u32[]{:S(2)}, u32[]{:S(2)}) %collective-permute-start.6) | collective-permute-done | bytes 344096 | tf_op jit(solution)/shard_map/ppermute | solution.py:16
  42.3 2.7 %collective-permute-start.9 = (bf16[2,168,512]{2,1,0:T(8,128)(2,1)S(1)}, bf16[2,168,512]{2,1,0:T(8,128)(2,1)S(1)}, u32[]{:S(2)}, u32[]{:S(2)}) collective-permute-start(bf16[2,168,512]{2,1,0:T(8,128)(2,1)S(1)} %collective-permute-done.7), channel_id=1, source_target_pairs={{0,56},{8,0},{16,8},{24,16},{32,24},{40,32},{48,40},{56,48},{1,57}... | collective-permute-start | bytes 1032200 | tf_op jit(solution)/shard_map/ppermute | solution.py:16
  45.0 3.6 %collective-permute-start.13 = (bf16[256,2688]{1,0:T(8,128)(2,1)}, bf16[256,2688]{1,0:T(8,128)(2,1)S(1)}, u32[]{:S(2)}, u32[]{:S(2)}) collective-permute-start(bf16[256,2688]{1,0:T(8,128)(2,1)} %collective-permute-done.12), channel_id=1, source_target_pairs={{0,1},{1,0},{2,3},{3,2},{4,5},{5,4},{6,7},{7,6},{8,9},{9,8},{10,11... | collective-permute-start | bytes 4128776 | tf_op jit(solution)/shard_map/ppermute | solution.py:16
  48.6 1.5 collective-permute-done.8
  50.2 2.7 %collective-permute-start.11 = (bf16[1,168,512]{2,1,0:T(8,128)(2,1)S(1)}, bf16[1,168,512]{2,1,0:T(8,128)(2,1)S(1)}, u32[]{:S(2)}, u32[]{:S(2)}) collective-permute-start(bf16[1,168,512]{2,1,0:T(8,128)(2,1)S(1)} %slice.188), channel_id=1, source_target_pairs={{0,56},{8,0},{16,8},{24,16},{32,24},{40,32},{48,40},{56,48},{1,57}... | collective-permute-start | bytes 516104 | tf_op jit(solution)/shard_map/ppermute | solution.py:16
  53.0 2.6 %collective-permute-done.10 = bf16[1,168,512]{2,1,0:T(8,128)(2,1)S(1)} collective-permute-done((bf16[1,168,512]{2,1,0:T(8,128)(2,1)S(1)}, bf16[1,168,512]{2,1,0:T(8,128)(2,1)S(1)}, u32[]{:S(2)}, u32[]{:S(2)}) %collective-permute-start.10) | collective-permute-done | bytes 172064 | tf_op jit(solution)/shard_map/ppermute | solution.py:16
  55.7 2.4 maximum_select_fusion.x_ref
  58.2 5.6 %shard_map.104 = (f32[512,256]{1,0:T(8,128)S(1)}, f32[512,256]{1,0:T(8,128)S(1)}) custom-call(s32[1]{0:T(128)} %constant.161.clone.1.where, bf16[512,2688]{1,0:T(8,128)(2,1)S(1)} %maximum_select_fusion.x_ref, bf16[2688,512]{1,0:T(8,128)(2,1)S(1)} %bitcast.103), custom_call_target="tpu_custom_call" | custom-call | flops 1409286144 | bytes 8388608 | tf_op jit(solution)/shard_map/pallas_call | solution.py:364
  65.8 2.6 %copy-done.2 = bf16[512,5376]{1,0:T(8,128)(2,1)S(1)} copy-done((bf16[512,5376]{1,0:T(8,128)(2,1)S(1)}, bf16[512,5376]{1,0:T(8,128)(2,1)}, u32[]{:S(2)}) %copy-start.2) | copy-done | bytes 5505048
  68.3 5.6 %shard_map.105 = (f32[512,256]{1,0:T(8,128)S(1)}, f32[512,256]{1,0:T(8,128)S(1)}) custom-call(s32[1]{0:T(128)} %bitcast.10.where, bf16[512,5376]{1,0:T(8,128)(2,1)S(1)} %copy-done.2, bf16[2688,512]{1,0:T(8,128)(2,1)S(1)} %bitcast.104), custom_call_target="tpu_custom_call" | custom-call | flops 1409286144 | bytes 8388608 | tf_op jit(solution)/shard_map/pallas_call | solution.py:364
  73.9 1.5 shard_map.106.par_ref
  75.4 1.5 copy-done.10
  78.6 3.6 %collective-permute-start.15 = (bf16[528,256]{1,0:T(8,128)(2,1)S(1)}, bf16[528,256]{1,0:T(8,128)(2,1)S(1)}, u32[]{:S(2)}, u32[]{:S(2)}) collective-permute-start(bf16[528,256]{1,0:T(8,128)(2,1)S(1)} %fusion.8.own_ref), channel_id=1, source_target_pairs={{0,8},{4,12},{8,16},{12,20},{16,24},{20,28},{24,32},{28,36},{32,40... | collective-permute-start | bytes 811016 | tf_op jit(solution)/shard_map/ppermute | solution.py:22
  82.2 3.5 %collective-permute-start.16 = (bf16[528,256]{1,0:T(8,128)(2,1)S(1)}, bf16[528,256]{1,0:T(8,128)(2,1)S(1)}, u32[]{:S(2)}, u32[]{:S(2)}) collective-permute-start(bf16[528,256]{1,0:T(8,128)(2,1)S(1)} %fusion.8.own_ref), channel_id=1, source_target_pairs={{0,4},{4,8},{8,12},{12,16},{16,20},{20,24},{24,28},{28,32},{32,36}... | collective-permute-start | bytes 811016 | tf_op jit(solution)/shard_map/ppermute | solution.py:22
  85.8 1.3 collective-permute-start.19
  87.2 1.6 collective-permute-done.16.one_ref
  88.8 6.8 %shard_map.107 = (bf16[512,256]{1,0:T(8,128)(2,1)S(1)}, bf16[1024,256]{1,0:T(8,128)(2,1)S(1)}, f32[512,256]{1,0:T(8,128)S(1)}) custom-call(bf16[512,256]{1,0:T(8,128)(2,1)S(1)} %get-tuple-element.112.q_ref, bf16[512,256]{1,0:T(8,128)(2,1)S(1)} %get-tuple-element.110.do_ref, bf16[528,256]{1,0:T(8,128)(2,1)S(1)} %collective-permute-done.15.two_ref, ...), custom_call_target="tpu_custom_call" | custom-call | flops 1677721600 | bytes 8388608 | tf_op jit(solution)/shard_map/pallas_call | solution.py:248
  98.7 6.3 %collective-permute-start.20 = (bf16[528,256]{1,0:T(8,128)(2,1)S(1)}, bf16[528,256]{1,0:T(8,128)(2,1)S(1)}, u32[]{:S(2)}, u32[]{:S(2)}) collective-permute-start(bf16[528,256]{1,0:T(8,128)(2,1)S(1)} %fusion.9.own_ref), channel_id=1, source_target_pairs={{0,8},{4,12},{8,16},{12,20},{16,24},{20,28},{24,32},{28,36},{32,40... | collective-permute-start | bytes 811016 | tf_op jit(solution)/shard_map/ppermute | solution.py:22
  105.0 3.3 %collective-permute-start.21 = (bf16[528,256]{1,0:T(8,128)(2,1)S(1)}, bf16[528,256]{1,0:T(8,128)(2,1)S(1)}, u32[]{:S(2)}, u32[]{:S(2)}) collective-permute-start(bf16[528,256]{1,0:T(8,128)(2,1)S(1)} %fusion.9.own_ref), channel_id=1, source_target_pairs={{0,4},{4,8},{8,12},{12,16},{16,20},{20,24},{24,28},{28,32},{32,36}... | collective-permute-start | bytes 811016 | tf_op jit(solution)/shard_map/ppermute | solution.py:22
  108.7 5.8 %collective-permute-done.21.one_ref = bf16[528,256]{1,0:T(8,128)(2,1)S(1)} collective-permute-done((bf16[528,256]{1,0:T(8,128)(2,1)S(1)}, bf16[528,256]{1,0:T(8,128)(2,1)S(1)}, u32[]{:S(2)}, u32[]{:S(2)}) %collective-permute-start.21) | collective-permute-done | bytes 270368 | tf_op jit(solution)/shard_map/ppermute | solution.py:22
  114.5 6.6 %shard_map.108 = (bf16[512,256]{1,0:T(8,128)(2,1)S(1)}, bf16[1024,256]{1,0:T(8,128)(2,1)S(1)}, f32[512,256]{1,0:T(8,128)S(1)}) custom-call(bf16[512,256]{1,0:T(8,128)(2,1)S(1)} %get-tuple-element.113.q_ref, bf16[512,256]{1,0:T(8,128)(2,1)S(1)} %get-tuple-element.111.do_ref, bf16[528,256]{1,0:T(8,128)(2,1)S(1)} %collective-permute-done.20.two_ref, ...), custom_call_target="tpu_custom_call" | custom-call | flops 1677721600 | bytes 8388608 | tf_op jit(solution)/shard_map/pallas_call | solution.py:248
  124.0 2.8 %collective-permute-start.24 = (bf16[512,256]{1,0:T(8,128)(2,1)S(1)}, bf16[512,256]{1,0:T(8,128)(2,1)S(1)}, u32[]{:S(2)}, u32[]{:S(2)}) collective-permute-start(bf16[512,256]{1,0:T(8,128)(2,1)S(1)} %pad_maximum_fusion.5), channel_id=1, source_target_pairs={{0,4},{4,0},{1,5},{5,1},{2,6},{6,2},{3,7},{7,3},{8,12},{12,8},{9,1... | collective-permute-start | bytes 786440 | tf_op jit(solution)/shard_map/ppermute | solution.py:16
  126.8 4.8 %collective-permute-done.22 = bf16[512,256]{1,0:T(8,128)(2,1)S(1)} collective-permute-done((bf16[512,256]{1,0:T(8,128)(2,1)S(1)}, bf16[512,256]{1,0:T(8,128)(2,1)S(1)}, u32[]{:S(2)}, u32[]{:S(2)}) %collective-permute-start.22) | collective-permute-done | bytes 262176 | tf_op jit(solution)/shard_map/ppermute | solution.py:22
  131.6 1.4 collective-permute-done.23
  133.7 1.9 collective-permute-done.24
  135.6 6.3 %collective-permute-done.25 = bf16[512,256]{1,0:T(8,128)(2,1)S(1)} collective-permute-done((bf16[512,256]{1,0:T(8,128)(2,1)S(1)}, bf16[512,256]{1,0:T(8,128)(2,1)S(1)}, u32[]{:S(2)}, u32[]{:S(2)}) %collective-permute-start.25) | collective-permute-done | bytes 262176 | tf_op jit(solution)/shard_map/ppermute | solution.py:16
  142.0 3.5 %shard_map.109 = bf16[1344,1024]{1,0:T(8,128)(2,1)} custom-call(s32[1]{0:T(128)S(6)} %sub.43.where, bf16[2688,512]{1,0:T(8,128)(2,1)S(1)} %bitcast.105, bf16[512,512]{1,0:T(8,128)(2,1)S(1)} %pad_maximum_fusion.2.g_ref, bf16[512,512]{1,0:T(8,128)(2,1)S(1)} %constant_dynamic-update-slice_fusion.h_ref), custom_call_target="tpu_custom_call" | custom-call | flops 1409286144 | bytes 6291456 | tf_op jit(solution)/shard_map/pallas_call | solution.py:416
  145.5 6.9 %collective-permute-start.26 = (bf16[1344,1024]{1,0:T(8,128)(2,1)}, bf16[1344,1024]{1,0:T(8,128)(2,1)}, u32[]{:S(2)}, u32[]{:S(2)}) collective-permute-start(bf16[1344,1024]{1,0:T(8,128)(2,1)} %shard_map.109), channel_id=1, source_target_pairs={{0,1},{1,0},{2,3},{3,2},{4,5},{5,4},{6,7},{7,6},{8,9},{9,8},{10,11... | collective-permute-start | bytes 8257544 | tf_op jit(solution)/shard_map/ppermute | solution.py:16
  153.4 1.8 copy-done.9
  155.2 1.8 copy-done.11
  157.0 4.2 %shard_map.111 = bf16[2688,512]{1,0:T(8,128)(2,1)S(1)} custom-call(bf16[2688,512]{1,0:T(8,128)(2,1)S(1)} %copy-done.9, bf16[2688,512]{1,0:T(8,128)(2,1)S(1)} %copy-done.11, bf16[512,512]{1,0:T(8,128)(2,1)S(1)} %pad_maximum_fusion.2.g_ref, bf16[512,512]{1,0:T(8,128)(2,1)S(1)} %copy-done.6), custom_call_target="tpu_custom_call" | custom-call | flops 2818572288 | bytes 12582912 | tf_op jit(solution)/shard_map/pallas_call | solution.py:285
  161.2 8.2 %collective-permute-start.28 = (bf16[1,168,512]{2,1,0:T(8,128)(2,1)S(1)}, bf16[1,168,512]{2,1,0:T(8,128)(2,1)S(1)}, u32[]{:S(2)}, u32[]{:S(2)}) collective-permute-start(bf16[1,168,512]{2,1,0:T(8,128)(2,1)S(1)} %get-tuple-element.98), channel_id=1, source_target_pairs={{0,56},{8,0},{16,8},{24,16},{32,24},{40,32},{48,40},{56,48},{1,57}... | collective-permute-start | bytes 516104 | tf_op jit(solution)/shard_map/ppermute | solution.py:16
  169.7 3.5 %collective-permute-done.28 = bf16[1,168,512]{2,1,0:T(8,128)(2,1)S(1)} collective-permute-done((bf16[1,168,512]{2,1,0:T(8,128)(2,1)S(1)}, bf16[1,168,512]{2,1,0:T(8,128)(2,1)S(1)}, u32[]{:S(2)}, u32[]{:S(2)}) %collective-permute-start.28) | collective-permute-done | bytes 172064 | tf_op jit(solution)/shard_map/ppermute | solution.py:16
  173.3 3.0 %collective-permute-done.27 = bf16[1,168,512]{2,1,0:T(8,128)(2,1)S(1)} collective-permute-done((bf16[1,168,512]{2,1,0:T(8,128)(2,1)S(1)}, bf16[1,168,512]{2,1,0:T(8,128)(2,1)S(1)}, u32[]{:S(2)}, u32[]{:S(2)}) %collective-permute-start.27) | collective-permute-done | bytes 172064 | tf_op jit(solution)/shard_map/ppermute | solution.py:16
  176.4 4.0 %shard_map.110 = (f32[1344,512]{1,0:T(8,128)S(1)}, bf16[1344,1024]{1,0:T(8,128)(2,1)S(1)}) custom-call(s32[1]{0:T(128)} %bitcast.1.where, bf16[2688,512]{1,0:T(8,128)(2,1)S(1)} %bitcast.106, bf16[512,512]{1,0:T(8,128)(2,1)S(1)} %pad_maximum_fusion.2.g_ref, bf16[512,512]{1,0:T(8,128)(2,1)S(1)} %copy-done.6, bf16[1344,1024]{1,0:T(8,128)(2,1)} %collective-permute-done.26.r_ref), custom_call_target="tpu_custom_call" | custom-call | flops 1409286144 | bytes 6291456 | tf_op jit(solution)/shard_map/pallas_call | solution.py:416
  180.4 1.5 copy-done.12
  181.9 1.7 fusion.13
  183.6 2.7 %collective-permute-start.33 = (bf16[2,168,512]{2,1,0:T(8,128)(2,1)S(1)}, bf16[2,168,512]{2,1,0:T(8,128)(2,1)S(1)}, u32[]{:S(2)}, u32[]{:S(2)}) collective-permute-start(bf16[2,168,512]{2,1,0:T(8,128)(2,1)S(1)} %pad_maximum_fusion.1), channel_id=1, source_target_pairs={{0,56},{8,0},{16,8},{24,16},{32,24},{40,32},{48,40},{56,48},{1,57}... | collective-permute-start | bytes 1032200 | tf_op jit(solution)/shard_map/ppermute | solution.py:16
  186.3 7.0 %collective-permute-done.31 = bf16[2,168,512]{2,1,0:T(8,128)(2,1)S(1)} collective-permute-done((bf16[2,168,512]{2,1,0:T(8,128)(2,1)S(1)}, bf16[2,168,512]{2,1,0:T(8,128)(2,1)S(1)}, u32[]{:S(2)}, u32[]{:S(2)}) %collective-permute-start.31) | collective-permute-done | bytes 344096 | tf_op jit(solution)/shard_map/ppermute | solution.py:16
  193.6 2.7 %collective-permute-start.34 = (bf16[2,168,512]{2,1,0:T(8,128)(2,1)S(1)}, bf16[2,168,512]{2,1,0:T(8,128)(2,1)S(1)}, u32[]{:S(2)}, u32[]{:S(2)}) collective-permute-start(bf16[2,168,512]{2,1,0:T(8,128)(2,1)S(1)} %get-tuple-element.94), channel_id=1, source_target_pairs={{0,56},{8,0},{16,8},{24,16},{32,24},{40,32},{48,40},{56,48},{1,57}... | collective-permute-start | bytes 1032200 | tf_op jit(solution)/shard_map/ppermute | solution.py:16
  197.2 5.2 %collective-permute-done.32 = bf16[2,168,512]{2,1,0:T(8,128)(2,1)S(1)} collective-permute-done((bf16[2,168,512]{2,1,0:T(8,128)(2,1)S(1)}, bf16[2,168,512]{2,1,0:T(8,128)(2,1)S(1)}, u32[]{:S(2)}, u32[]{:S(2)}) %collective-permute-start.32) | collective-permute-done | bytes 344096 | tf_op jit(solution)/shard_map/ppermute | solution.py:16
  203.8 2.7 %collective-permute-start.36 = (bf16[2,168,512]{2,1,0:T(8,128)(2,1)S(1)}, bf16[2,168,512]{2,1,0:T(8,128)(2,1)S(1)}, u32[]{:S(2)}, u32[]{:S(2)}) collective-permute-start(bf16[2,168,512]{2,1,0:T(8,128)(2,1)S(1)} %get-tuple-element.91), channel_id=1, source_target_pairs={{0,56},{8,0},{16,8},{24,16},{32,24},{40,32},{48,40},{56,48},{1,57}... | collective-permute-start | bytes 1032200 | tf_op jit(solution)/shard_map/ppermute | solution.py:16
  207.7 1.7 collective-permute-start.30
  209.4 2.3 collective-permute-done.35
  213.7 2.5 %collective-permute-start.37 = (bf16[168,512]{1,0:T(8,128)(2,1)}, bf16[168,512]{1,0:T(8,128)(2,1)}, u32[]{:S(2)}, u32[]{:S(2)}) collective-permute-start(bf16[168,512]{1,0:T(8,128)(2,1)} %get-tuple-element.102), channel_id=1, source_target_pairs={{64,0},{0,64},{196,132},{132,196},{65,1},{1,65},{197,133},{133,197... | collective-permute-start | bytes 516104 | tf_op jit(solution)/shard_map/ppermute | solution.py:87
  218.8 1.6 collective-permute-done.37
  220.4 3.8 %collective-permute-done.38 = bf16[168,512]{1,0:T(8,128)(2,1)} collective-permute-done((bf16[168,512]{1,0:T(8,128)(2,1)}, bf16[168,512]{1,0:T(8,128)(2,1)}, u32[]{:S(2)}, u32[]{:S(2)}) %collective-permute-start.38) | collective-permute-done | bytes 172064 | tf_op jit(solution)/shard_map/ppermute | solution.py:87
  224.2 1.9 collective-permute-done.39
  226.1 1.9 fusion.7
  229.2 9.4 %collective-permute-done.40 = bf16[84,512]{1,0:T(8,128)(2,1)S(1)} collective-permute-done((bf16[84,512]{1,0:T(8,128)(2,1)S(1)}, bf16[84,512]{1,0:T(8,128)(2,1)S(1)}, u32[]{:S(2)}, u32[]{:S(2)}) %collective-permute-start.40) | collective-permute-done | bytes 86048 | tf_op jit(solution)/shard_map/ppermute | solution.py:16
  239.9 3.9 %shard_map.112 = bf16[1344,512]{1,0:T(8,128)(2,1)} custom-call(s32[1]{0:T(128)} %bitcast.keep, f32[1344,512]{1,0:T(8,128)S(1)} %copy-done.13, bf16[1344,512]{1,0:T(8,128)(2,1)} %collective-permute-done.29.first_ref, bf16[1344,512]{1,0:T(8,128)(2,1)} %collective-permute-done.30.second_ref), custom_call_target="tpu_custom_call" | custom-call | flops 2752512 | bytes 6881280 | tf_op jit(solution)/shard_map/pallas_call | solution.py:438
  (147 shorter events, 26.4 us)
Async XLA Ops:
  1.4 6.6 %collective-permute-start = (bf16[84,512]{1,0:T(8,128)(2,1)S(1)}, bf16[84,512]{1,0:T(8,128)(2,1)S(1)}, u32[]{:S(2)}, u32[]{:S(2)}) collective-permute-start(bf16[84,512]{1,0:T(8,128)(2,1)S(1)} %pad_maximum_fusion.7), channel_id=1, source_target_pairs={{0,4},{4,0},{1,5},{5,1},{2,6},{6,2},{3,7},{7,3},{8,12},{12,8},{9,1... | collective-permute-start | bytes 258056 | tf_op jit(solution)/shard_map/ppermute | solution.py:16
  3.6 2.6 %copy-start = (bf16[512,5376]{1,0:T(8,128)(2,1)S(1)}, bf16[512,5376]{1,0:T(8,128)(2,1)}, u32[]{:S(2)}) copy-start(bf16[512,5376]{1,0:T(8,128)(2,1)} %x_ref.5) | copy-start | bytes 16515076
  8.0 37.0 %collective-permute-start.12 = (bf16[256,2688]{1,0:T(8,128)(2,1)}, bf16[256,2688]{1,0:T(8,128)(2,1)}, u32[]{:S(2)}, u32[]{:S(2)}) collective-permute-start(bf16[256,2688]{1,0:T(8,128)(2,1)} %shard_map.103), channel_id=1, source_target_pairs={{0,4},{4,0},{1,5},{5,1},{2,6},{6,2},{3,7},{7,3},{8,12},{12,8},{9,1... | collective-permute-start | bytes 4128776 | tf_op jit(solution)/shard_map/ppermute | solution.py:16
  8.1 8.7 %collective-permute-start.1 = (bf16[168,512]{1,0:T(8,128)(2,1)S(1)}, bf16[168,512]{1,0:T(8,128)(2,1)S(1)}, u32[]{:S(2)}, u32[]{:S(2)}) collective-permute-start(bf16[168,512]{1,0:T(8,128)(2,1)S(1)} %maximum_select_fusion.1), channel_id=1, source_target_pairs={{0,128},{64,192},{132,4},{196,68},{1,129},{65,193},{133,5},{197,69... | collective-permute-start | bytes 516104 | tf_op jit(solution)/shard_map/ppermute | solution.py:87
  13.2 7.8 %collective-permute-start.2 = (bf16[168,512]{1,0:T(8,128)(2,1)S(1)}, bf16[168,512]{1,0:T(8,128)(2,1)S(1)}, u32[]{:S(2)}, u32[]{:S(2)}) collective-permute-start(bf16[168,512]{1,0:T(8,128)(2,1)S(1)} %maximum_select_fusion.1), channel_id=1, source_target_pairs={{0,64},{64,0},{132,196},{196,132},{1,65},{65,1},{133,197},{197,133... | collective-permute-start | bytes 516104 | tf_op jit(solution)/shard_map/ppermute | solution.py:87
  15.5 5.5 %collective-permute-start.3 = (bf16[168,512]{1,0:T(8,128)(2,1)S(1)}, bf16[168,512]{1,0:T(8,128)(2,1)S(1)}, u32[]{:S(2)}, u32[]{:S(2)}) collective-permute-start(bf16[168,512]{1,0:T(8,128)(2,1)S(1)} %maximum_select_fusion.1), channel_id=1, source_target_pairs={{0,192},{64,128},{132,68},{196,4},{1,193},{65,129},{133,69},{197,5... | collective-permute-start | bytes 516104 | tf_op jit(solution)/shard_map/ppermute | solution.py:87
  21.1 12.5 %collective-permute-start.4 = (bf16[2,168,512]{2,1,0:T(8,128)(2,1)S(1)}, bf16[2,168,512]{2,1,0:T(8,128)(2,1)S(1)}, u32[]{:S(2)}, u32[]{:S(2)}) collective-permute-start(bf16[2,168,512]{2,1,0:T(8,128)(2,1)S(1)} %pad_maximum_fusion.4), channel_id=1, source_target_pairs={{0,8},{8,16},{16,24},{24,32},{32,40},{40,48},{48,56},{56,0},{1,9},... | collective-permute-start | bytes 1032200 | tf_op jit(solution)/shard_map/ppermute | solution.py:16
  22.8 10.8 %collective-permute-start.5 = (bf16[2,168,512]{2,1,0:T(8,128)(2,1)S(1)}, bf16[2,168,512]{2,1,0:T(8,128)(2,1)}, u32[]{:S(2)}, u32[]{:S(2)}) collective-permute-start(bf16[2,168,512]{2,1,0:T(8,128)(2,1)S(1)} %pad_maximum_fusion.4), channel_id=1, source_target_pairs={{0,56},{8,0},{16,8},{24,16},{32,24},{40,32},{48,40},{56,48},{1,57}... | collective-permute-start | bytes 1032200 | tf_op jit(solution)/shard_map/ppermute | solution.py:16
  26.8 2.6 %copy-start.1 = (bf16[512,5376]{1,0:T(8,128)(2,1)S(1)}, bf16[512,5376]{1,0:T(8,128)(2,1)}, u32[]{:S(2)}) copy-start(bf16[512,5376]{1,0:T(8,128)(2,1)} %x_ref.5) | copy-start | bytes 16515076
  30.9 1.5 copy-start.8
  33.6 8.7 %collective-permute-start.6 = (bf16[2,168,512]{2,1,0:T(8,128)(2,1)S(1)}, bf16[2,168,512]{2,1,0:T(8,128)(2,1)S(1)}, u32[]{:S(2)}, u32[]{:S(2)}) collective-permute-start(bf16[2,168,512]{2,1,0:T(8,128)(2,1)S(1)} %collective-permute-done.4), channel_id=1, source_target_pairs={{0,8},{8,16},{16,24},{24,32},{32,40},{40,48},{48,56},{56,0},{1,9},... | collective-permute-start | bytes 1032200 | tf_op jit(solution)/shard_map/ppermute | solution.py:16
  33.6 8.7 %collective-permute-start.7 = (bf16[2,168,512]{2,1,0:T(8,128)(2,1)}, bf16[2,168,512]{2,1,0:T(8,128)(2,1)S(1)}, u32[]{:S(2)}, u32[]{:S(2)}) collective-permute-start(bf16[2,168,512]{2,1,0:T(8,128)(2,1)} %collective-permute-done.5), channel_id=1, source_target_pairs={{0,56},{8,0},{16,8},{24,16},{32,24},{40,32},{48,40},{56,48},{1,57}... | collective-permute-start | bytes 1032200 | tf_op jit(solution)/shard_map/ppermute | solution.py:16
  42.3 7.8 %collective-permute-start.8 = (bf16[2,168,512]{2,1,0:T(8,128)(2,1)S(1)}, bf16[2,168,512]{2,1,0:T(8,128)(2,1)S(1)}, u32[]{:S(2)}, u32[]{:S(2)}) collective-permute-start(bf16[2,168,512]{2,1,0:T(8,128)(2,1)S(1)} %collective-permute-done.6), channel_id=1, source_target_pairs={{0,8},{8,16},{16,24},{24,32},{32,40},{40,48},{48,56},{56,0},{1,9},... | collective-permute-start | bytes 1032200 | tf_op jit(solution)/shard_map/ppermute | solution.py:16
  42.3 7.9 %collective-permute-start.9 = (bf16[2,168,512]{2,1,0:T(8,128)(2,1)S(1)}, bf16[2,168,512]{2,1,0:T(8,128)(2,1)S(1)}, u32[]{:S(2)}, u32[]{:S(2)}) collective-permute-start(bf16[2,168,512]{2,1,0:T(8,128)(2,1)S(1)} %collective-permute-done.7), channel_id=1, source_target_pairs={{0,56},{8,0},{16,8},{24,16},{32,24},{40,32},{48,40},{56,48},{1,57}... | collective-permute-start | bytes 1032200 | tf_op jit(solution)/shard_map/ppermute | solution.py:16
  45.0 10.8 %collective-permute-start.13 = (bf16[256,2688]{1,0:T(8,128)(2,1)}, bf16[256,2688]{1,0:T(8,128)(2,1)S(1)}, u32[]{:S(2)}, u32[]{:S(2)}) collective-permute-start(bf16[256,2688]{1,0:T(8,128)(2,1)} %collective-permute-done.12), channel_id=1, source_target_pairs={{0,1},{1,0},{2,3},{3,2},{4,5},{5,4},{6,7},{7,6},{8,9},{9,8},{10,11... | collective-permute-start | bytes 4128776 | tf_op jit(solution)/shard_map/ppermute | solution.py:16
  50.1 5.5 %collective-permute-start.10 = (bf16[1,168,512]{2,1,0:T(8,128)(2,1)S(1)}, bf16[1,168,512]{2,1,0:T(8,128)(2,1)S(1)}, u32[]{:S(2)}, u32[]{:S(2)}) collective-permute-start(bf16[1,168,512]{2,1,0:T(8,128)(2,1)S(1)} %slice.187), channel_id=1, source_target_pairs={{0,8},{8,16},{16,24},{24,32},{32,40},{40,48},{48,56},{56,0},{1,9},... | collective-permute-start | bytes 516104 | tf_op jit(solution)/shard_map/ppermute | solution.py:16
  50.2 5.4 %collective-permute-start.11 = (bf16[1,168,512]{2,1,0:T(8,128)(2,1)S(1)}, bf16[1,168,512]{2,1,0:T(8,128)(2,1)S(1)}, u32[]{:S(2)}, u32[]{:S(2)}) collective-permute-start(bf16[1,168,512]{2,1,0:T(8,128)(2,1)S(1)} %slice.188), channel_id=1, source_target_pairs={{0,56},{8,0},{16,8},{24,16},{32,24},{40,32},{48,40},{56,48},{1,57}... | collective-permute-start | bytes 516104 | tf_op jit(solution)/shard_map/ppermute | solution.py:16
  58.2 5.6 %copy-start.3 = (bf16[512,2688]{1,0:T(8,128)(2,1)}, bf16[512,2688]{1,0:T(8,128)(2,1)S(1)}, u32[]{:S(2)}) copy-start(bf16[512,2688]{1,0:T(8,128)(2,1)S(1)} %maximum_select_fusion.x_ref) | copy-start | bytes 8257540
  58.2 6.4 %copy-start.20 = (s32[512]{0:T(512)S(1)}, s32[512]{0:T(512)}, u32[]{:S(2)}) copy-start(s32[512]{0:T(512)} %param.12) | copy-start | bytes 6148
  63.8 0.8 copy-start.16
  64.6 12.4 %collective-permute-start.14 = (f32[512,256]{1,0:T(8,128)S(1)}, f32[512,256]{1,0:T(8,128)}, u32[]{:S(2)}, u32[]{:S(2)}) collective-permute-start(f32[512,256]{1,0:T(8,128)S(1)} %get-tuple-element.60), channel_id=1, source_target_pairs={{0,4},{4,0},{1,5},{5,1},{2,6},{6,2},{3,7},{7,3},{8,12},{12,8},{9,1... | collective-permute-start | bytes 1572872 | tf_op jit(solution)/shard_map/ppermute | solution.py:16
  65.7 2.6 %copy-start.2 = (bf16[512,5376]{1,0:T(8,128)(2,1)S(1)}, bf16[512,5376]{1,0:T(8,128)(2,1)}, u32[]{:S(2)}) copy-start(bf16[512,5376]{1,0:T(8,128)(2,1)} %x_ref.5) | copy-start | bytes 16515076
  68.3 5.6 %copy-start.4 = (bf16[512,2688]{1,0:T(8,128)(2,1)S(1)}, bf16[512,2688]{1,0:T(8,128)(2,1)}, u32[]{:S(2)}) copy-start(bf16[512,2688]{1,0:T(8,128)(2,1)} %copy-done.3) | copy-start | bytes 8257540
  73.9 4.5 %copy-start.19 = (f32[128]{0:T(128)S(1)}, f32[128]{0:T(128)}, u32[]{:S(2)}) copy-start(f32[128]{0:T(128)} %param.15) | copy-start | bytes 1540
  75.4 1.5 copy-start.10
  77.0 8.7 %copy-start.18 = (bf16[512,4,128]{2,1,0:T(4,128)(2,1)S(1)}, bf16[512,4,128]{2,1,0:T(4,128)(2,1)}, u32[]{:S(2)}) copy-start(bf16[512,4,128]{2,1,0:T(4,128)(2,1)} %param.10) | copy-start | bytes 1572868
  77.0 8.8 %copy-start.17 = (f32[512,256]{1,0:T(8,128)S(1)}, f32[512,256]{1,0:T(8,128)}, u32[]{:S(2)}) copy-start(f32[512,256]{1,0:T(8,128)} %copy-done.16) | copy-start | bytes 1572868
  78.6 8.6 %collective-permute-start.15 = (bf16[528,256]{1,0:T(8,128)(2,1)S(1)}, bf16[528,256]{1,0:T(8,128)(2,1)S(1)}, u32[]{:S(2)}, u32[]{:S(2)}) collective-permute-start(bf16[528,256]{1,0:T(8,128)(2,1)S(1)} %fusion.8.own_ref), channel_id=1, source_target_pairs={{0,8},{4,12},{8,16},{12,20},{16,24},{20,28},{24,32},{28,36},{32,40... | collective-permute-start | bytes 811016 | tf_op jit(solution)/shard_map/ppermute | solution.py:22
  82.2 6.7 %collective-permute-start.16 = (bf16[528,256]{1,0:T(8,128)(2,1)S(1)}, bf16[528,256]{1,0:T(8,128)(2,1)S(1)}, u32[]{:S(2)}, u32[]{:S(2)}) collective-permute-start(bf16[528,256]{1,0:T(8,128)(2,1)S(1)} %fusion.8.own_ref), channel_id=1, source_target_pairs={{0,4},{4,8},{8,12},{12,16},{16,20},{20,24},{24,28},{28,32},{32,36}... | collective-permute-start | bytes 811016 | tf_op jit(solution)/shard_map/ppermute | solution.py:22
  85.8 12.5 %collective-permute-start.19 = (f32[512,256]{1,0:T(8,128)S(1)}, f32[512,256]{1,0:T(8,128)S(1)}, u32[]{:S(2)}, u32[]{:S(2)}) collective-permute-start(f32[512,256]{1,0:T(8,128)S(1)} %copy-done.17), channel_id=1, source_target_pairs={{0,4},{4,0},{1,5},{5,1},{2,6},{6,2},{3,7},{7,3},{8,12},{12,8},{9,1... | collective-permute-start | bytes 1572872 | tf_op jit(solution)/shard_map/ppermute | solution.py:16
  95.7 12.6 %collective-permute-start.17 = (bf16[512,256]{1,0:T(8,128)(2,1)S(1)}, bf16[512,256]{1,0:T(8,128)(2,1)S(1)}, u32[]{:S(2)}, u32[]{:S(2)}) collective-permute-start(bf16[512,256]{1,0:T(8,128)(2,1)S(1)} %get-tuple-element.108), channel_id=1, source_target_pairs={{4,0},{8,4},{12,8},{16,12},{20,16},{24,20},{28,24},{32,28},{36,32}... | collective-permute-start | bytes 786440 | tf_op jit(solution)/shard_map/ppermute | solution.py:22
  97.0 11.3 %collective-permute-start.18 = (bf16[512,256]{1,0:T(8,128)(2,1)S(1)}, bf16[512,256]{1,0:T(8,128)(2,1)S(1)}, u32[]{:S(2)}, u32[]{:S(2)}) collective-permute-start(bf16[512,256]{1,0:T(8,128)(2,1)S(1)} %get-tuple-element.109), channel_id=1, source_target_pairs={{8,0},{12,4},{16,8},{20,12},{24,16},{28,20},{32,24},{36,28},{40,32... | collective-permute-start | bytes 786440 | tf_op jit(solution)/shard_map/ppermute | solution.py:22
  98.7 9.9 %collective-permute-start.20 = (bf16[528,256]{1,0:T(8,128)(2,1)S(1)}, bf16[528,256]{1,0:T(8,128)(2,1)S(1)}, u32[]{:S(2)}, u32[]{:S(2)}) collective-permute-start(bf16[528,256]{1,0:T(8,128)(2,1)S(1)} %fusion.9.own_ref), channel_id=1, source_target_pairs={{0,8},{4,12},{8,16},{12,20},{16,24},{20,28},{24,32},{28,36},{32,40... | collective-permute-start | bytes 811016 | tf_op jit(solution)/shard_map/ppermute | solution.py:22
  105.0 9.5 %collective-permute-start.21 = (bf16[528,256]{1,0:T(8,128)(2,1)S(1)}, bf16[528,256]{1,0:T(8,128)(2,1)S(1)}, u32[]{:S(2)}, u32[]{:S(2)}) collective-permute-start(bf16[528,256]{1,0:T(8,128)(2,1)S(1)} %fusion.9.own_ref), channel_id=1, source_target_pairs={{0,4},{4,8},{8,12},{12,16},{16,20},{20,24},{24,28},{28,32},{32,36}... | collective-permute-start | bytes 811016 | tf_op jit(solution)/shard_map/ppermute | solution.py:22
  121.1 12.5 %copy-start.14 = (bf16[512,256]{1,0:T(8,128)(2,1)}, bf16[512,256]{1,0:T(8,128)(2,1)S(1)}, u32[]{:S(2)}) copy-start(bf16[512,256]{1,0:T(8,128)(2,1)S(1)} %get-tuple-element.88) | copy-start | bytes 786436
  121.1 10.4 %collective-permute-start.22 = (bf16[512,256]{1,0:T(8,128)(2,1)S(1)}, bf16[512,256]{1,0:T(8,128)(2,1)S(1)}, u32[]{:S(2)}, u32[]{:S(2)}) collective-permute-start(bf16[512,256]{1,0:T(8,128)(2,1)S(1)} %get-tuple-element.106), channel_id=1, source_target_pairs={{4,0},{8,4},{12,8},{16,12},{20,16},{24,20},{28,24},{32,28},{36,32}... | collective-permute-start | bytes 786440 | tf_op jit(solution)/shard_map/ppermute | solution.py:22
  122.4 10.5 %collective-permute-start.23 = (bf16[512,256]{1,0:T(8,128)(2,1)S(1)}, bf16[512,256]{1,0:T(8,128)(2,1)S(1)}, u32[]{:S(2)}, u32[]{:S(2)}) collective-permute-start(bf16[512,256]{1,0:T(8,128)(2,1)S(1)} %get-tuple-element.107), channel_id=1, source_target_pairs={{8,0},{12,4},{16,8},{20,12},{24,16},{28,20},{32,24},{36,28},{40,32... | collective-permute-start | bytes 786440 | tf_op jit(solution)/shard_map/ppermute | solution.py:22
  124.0 11.6 %collective-permute-start.24 = (bf16[512,256]{1,0:T(8,128)(2,1)S(1)}, bf16[512,256]{1,0:T(8,128)(2,1)S(1)}, u32[]{:S(2)}, u32[]{:S(2)}) collective-permute-start(bf16[512,256]{1,0:T(8,128)(2,1)S(1)} %pad_maximum_fusion.5), channel_id=1, source_target_pairs={{0,4},{4,0},{1,5},{5,1},{2,6},{6,2},{3,7},{7,3},{8,12},{12,8},{9,1... | collective-permute-start | bytes 786440 | tf_op jit(solution)/shard_map/ppermute | solution.py:16
  133.6 8.4 %collective-permute-start.25 = (bf16[512,256]{1,0:T(8,128)(2,1)S(1)}, bf16[512,256]{1,0:T(8,128)(2,1)S(1)}, u32[]{:S(2)}, u32[]{:S(2)}) collective-permute-start(bf16[512,256]{1,0:T(8,128)(2,1)S(1)} %pad_maximum_fusion.6), channel_id=1, source_target_pairs={{0,4},{4,0},{1,5},{5,1},{2,6},{6,2},{3,7},{7,3},{8,12},{12,8},{9,1... | collective-permute-start | bytes 786440 | tf_op jit(solution)/shard_map/ppermute | solution.py:16
  142.0 3.5 %copy-start.5 = (bf16[512,512]{1,0:T(8,128)(2,1)}, bf16[512,512]{1,0:T(8,128)(2,1)S(1)}, u32[]{:S(2)}) copy-start(bf16[512,512]{1,0:T(8,128)(2,1)S(1)} %constant_dynamic-update-slice_fusion.h_ref) | copy-start | bytes 1572868
  145.5 30.9 %collective-permute-start.26 = (bf16[1344,1024]{1,0:T(8,128)(2,1)}, bf16[1344,1024]{1,0:T(8,128)(2,1)}, u32[]{:S(2)}, u32[]{:S(2)}) collective-permute-start(bf16[1344,1024]{1,0:T(8,128)(2,1)} %shard_map.109), channel_id=1, source_target_pairs={{0,1},{1,0},{2,3},{3,2},{4,5},{5,4},{6,7},{7,6},{8,9},{9,8},{10,11... | collective-permute-start | bytes 8257544 | tf_op jit(solution)/shard_map/ppermute | solution.py:16
  152.4 1.0 copy-start.6
  153.4 1.8 copy-start.9
  155.2 1.8 copy-start.11
  161.2 32.1 %copy-start.7 = (bf16[2688,512]{1,0:T(8,128)(2,1)}, bf16[2688,512]{1,0:T(8,128)(2,1)S(1)}, u32[]{:S(2)}) copy-start(bf16[2688,512]{1,0:T(8,128)(2,1)S(1)} %shard_map.111) | copy-start | bytes 8257540
  161.2 12.0 %collective-permute-start.28 = (bf16[1,168,512]{2,1,0:T(8,128)(2,1)S(1)}, bf16[1,168,512]{2,1,0:T(8,128)(2,1)S(1)}, u32[]{:S(2)}, u32[]{:S(2)}) collective-permute-start(bf16[1,168,512]{2,1,0:T(8,128)(2,1)S(1)} %get-tuple-element.98), channel_id=1, source_target_pairs={{0,56},{8,0},{16,8},{24,16},{32,24},{40,32},{48,40},{56,48},{1,57}... | collective-permute-start | bytes 516104 | tf_op jit(solution)/shard_map/ppermute | solution.py:16
  169.5 6.9 %collective-permute-start.27 = (bf16[1,168,512]{2,1,0:T(8,128)(2,1)S(1)}, bf16[1,168,512]{2,1,0:T(8,128)(2,1)S(1)}, u32[]{:S(2)}, u32[]{:S(2)}) collective-permute-start(bf16[1,168,512]{2,1,0:T(8,128)(2,1)S(1)} %get-tuple-element.99), channel_id=1, source_target_pairs={{0,8},{8,16},{16,24},{24,32},{32,40},{40,48},{48,56},{56,0},{1,9},... | collective-permute-start | bytes 516104 | tf_op jit(solution)/shard_map/ppermute | solution.py:16
  180.4 1.5 copy-start.12
  181.9 14.4 %copy-start.15 = (bf16[512,256]{1,0:T(8,128)(2,1)S(1)}, bf16[512,256]{1,0:T(8,128)(2,1)}, u32[]{:S(2)}) copy-start(bf16[512,256]{1,0:T(8,128)(2,1)} %copy-done.14) | copy-start | bytes 786436
  183.6 9.7 %collective-permute-start.31 = (bf16[2,168,512]{2,1,0:T(8,128)(2,1)S(1)}, bf16[2,168,512]{2,1,0:T(8,128)(2,1)S(1)}, u32[]{:S(2)}, u32[]{:S(2)}) collective-permute-start(bf16[2,168,512]{2,1,0:T(8,128)(2,1)S(1)} %pad_maximum_fusion), channel_id=1, source_target_pairs={{0,8},{8,16},{16,24},{24,32},{32,40},{40,48},{48,56},{56,0},{1,9},... | collective-permute-start | bytes 1032200 | tf_op jit(solution)/shard_map/ppermute | solution.py:16
  183.6 9.7 %collective-permute-start.33 = (bf16[2,168,512]{2,1,0:T(8,128)(2,1)S(1)}, bf16[2,168,512]{2,1,0:T(8,128)(2,1)S(1)}, u32[]{:S(2)}, u32[]{:S(2)}) collective-permute-start(bf16[2,168,512]{2,1,0:T(8,128)(2,1)S(1)} %pad_maximum_fusion.1), channel_id=1, source_target_pairs={{0,56},{8,0},{16,8},{24,16},{32,24},{40,32},{48,40},{56,48},{1,57}... | collective-permute-start | bytes 1032200 | tf_op jit(solution)/shard_map/ppermute | solution.py:16
  193.5 8.9 %collective-permute-start.32 = (bf16[2,168,512]{2,1,0:T(8,128)(2,1)S(1)}, bf16[2,168,512]{2,1,0:T(8,128)(2,1)S(1)}, u32[]{:S(2)}, u32[]{:S(2)}) collective-permute-start(bf16[2,168,512]{2,1,0:T(8,128)(2,1)S(1)} %get-tuple-element.95), channel_id=1, source_target_pairs={{0,8},{8,16},{16,24},{24,32},{32,40},{40,48},{48,56},{56,0},{1,9},... | collective-permute-start | bytes 1032200 | tf_op jit(solution)/shard_map/ppermute | solution.py:16
  193.6 8.8 %collective-permute-start.34 = (bf16[2,168,512]{2,1,0:T(8,128)(2,1)S(1)}, bf16[2,168,512]{2,1,0:T(8,128)(2,1)S(1)}, u32[]{:S(2)}, u32[]{:S(2)}) collective-permute-start(bf16[2,168,512]{2,1,0:T(8,128)(2,1)S(1)} %get-tuple-element.94), channel_id=1, source_target_pairs={{0,56},{8,0},{16,8},{24,16},{32,24},{40,32},{48,40},{56,48},{1,57}... | collective-permute-start | bytes 1032200 | tf_op jit(solution)/shard_map/ppermute | solution.py:16
  203.7 36.2 %copy-start.13 = (f32[1344,512]{1,0:T(8,128)S(1)}, f32[1344,512]{1,0:T(8,128)}, u32[]{:S(2)}) copy-start(f32[1344,512]{1,0:T(8,128)} %copy-done.12) | copy-start | bytes 8257540
  203.7 8.1 %collective-permute-start.35 = (bf16[2,168,512]{2,1,0:T(8,128)(2,1)S(1)}, bf16[2,168,512]{2,1,0:T(8,128)(2,1)S(1)}, u32[]{:S(2)}, u32[]{:S(2)}) collective-permute-start(bf16[2,168,512]{2,1,0:T(8,128)(2,1)S(1)} %get-tuple-element.90), channel_id=1, source_target_pairs={{0,8},{8,16},{16,24},{24,32},{32,40},{40,48},{48,56},{56,0},{1,9},... | collective-permute-start | bytes 1032200 | tf_op jit(solution)/shard_map/ppermute | solution.py:16
  203.8 8.0 %collective-permute-start.36 = (bf16[2,168,512]{2,1,0:T(8,128)(2,1)S(1)}, bf16[2,168,512]{2,1,0:T(8,128)(2,1)S(1)}, u32[]{:S(2)}, u32[]{:S(2)}) collective-permute-start(bf16[2,168,512]{2,1,0:T(8,128)(2,1)S(1)} %get-tuple-element.91), channel_id=1, source_target_pairs={{0,56},{8,0},{16,8},{24,16},{32,24},{40,32},{48,40},{56,48},{1,57}... | collective-permute-start | bytes 1032200 | tf_op jit(solution)/shard_map/ppermute | solution.py:16
  206.5 33.5 %collective-permute-start.29 = (bf16[1344,512]{1,0:T(8,128)(2,1)}, bf16[1344,512]{1,0:T(8,128)(2,1)}, u32[]{:S(2)}, u32[]{:S(2)}) collective-permute-start(bf16[1344,512]{1,0:T(8,128)(2,1)} %get-tuple-element.83), channel_id=1, source_target_pairs={{0,4},{6,2},{2,0},{4,6},{1,5},{7,3},{3,1},{5,7},{8,12},{14,10},{10... | collective-permute-start | bytes 4128776 | tf_op jit(solution)/shard_map/ppermute | solution.py:567
  207.7 32.2 %collective-permute-start.30 = (bf16[1344,512]{1,0:T(8,128)(2,1)}, bf16[1344,512]{1,0:T(8,128)(2,1)}, u32[]{:S(2)}, u32[]{:S(2)}) collective-permute-start(bf16[1344,512]{1,0:T(8,128)(2,1)} %get-tuple-element.84), channel_id=1, source_target_pairs={{2,4},{4,2},{3,5},{5,3},{10,12},{12,10},{11,13},{13,11},{18,20},{2... | collective-permute-start | bytes 4128776 | tf_op jit(solution)/shard_map/ppermute | solution.py:568
  213.7 6.8 %collective-permute-start.37 = (bf16[168,512]{1,0:T(8,128)(2,1)}, bf16[168,512]{1,0:T(8,128)(2,1)}, u32[]{:S(2)}, u32[]{:S(2)}) collective-permute-start(bf16[168,512]{1,0:T(8,128)(2,1)} %get-tuple-element.102), channel_id=1, source_target_pairs={{64,0},{0,64},{196,132},{132,196},{65,1},{1,65},{197,133},{133,197... | collective-permute-start | bytes 516104 | tf_op jit(solution)/shard_map/ppermute | solution.py:87
  216.2 8.0 %collective-permute-start.38 = (bf16[168,512]{1,0:T(8,128)(2,1)}, bf16[168,512]{1,0:T(8,128)(2,1)}, u32[]{:S(2)}, u32[]{:S(2)}) collective-permute-start(bf16[168,512]{1,0:T(8,128)(2,1)} %get-tuple-element.102), channel_id=1, source_target_pairs={{192,0},{128,64},{68,132},{4,196},{193,1},{129,65},{69,133},{5,197... | collective-permute-start | bytes 516104 | tf_op jit(solution)/shard_map/ppermute | solution.py:87
  217.5 8.5 %collective-permute-start.39 = (bf16[168,512]{1,0:T(8,128)(2,1)}, bf16[168,512]{1,0:T(8,128)(2,1)}, u32[]{:S(2)}, u32[]{:S(2)}) collective-permute-start(bf16[168,512]{1,0:T(8,128)(2,1)} %get-tuple-element.103), channel_id=1, source_target_pairs={{128,0},{192,64},{4,132},{68,196},{129,1},{193,65},{5,133},{69,197... | collective-permute-start | bytes 516104 | tf_op jit(solution)/shard_map/ppermute | solution.py:87
  229.1 9.5 %collective-permute-start.40 = (bf16[84,512]{1,0:T(8,128)(2,1)S(1)}, bf16[84,512]{1,0:T(8,128)(2,1)S(1)}, u32[]{:S(2)}, u32[]{:S(2)}) collective-permute-start(bf16[84,512]{1,0:T(8,128)(2,1)S(1)} %fusion.11), channel_id=1, source_target_pairs={{0,4},{4,0},{1,5},{5,1},{2,6},{6,2},{3,7},{7,3},{8,12},{12,8},{9,1... | collective-permute-start | bytes 258056 | tf_op jit(solution)/shard_map/ppermute | solution.py:16
